TPU v7x, 128 devices: a whole 4x4x4 slice. The times are simulated.
128 devices in a mesh: head: 2 (over y_hi), seq: 64 (over z, x, y_lo, core).
Axes of the slice: x: 4, y: 4 (y_hi: 2, y_lo: 2; y = y_hi * 2 + y_lo), z: 4, core: 2. Of those that a mesh axis runs over, the one named last changes fastest.
Arguments:
- queries: bfloat16 [65536, 2048], P('seq', 'head'), may hold values from -24 to 24
- key_rows: bfloat16 [65536, 2048], P('seq', 'head'), may hold values from -24 to 24
- value_rows: bfloat16 [65536, 2048], P('seq', 'head'), may hold values from -6 to 6
- token_rates: float32 [4, 65536], P('head', 'seq'), may hold values from 0.01 to 1
- gate_fast: float32 [4, 512, 512], P('head'), may hold values from -0.25 to 0.25
- lift_fast: float32 [4, 512, 512], P('head'), may hold values from -0.25 to 0.25
- down_fast: float32 [4, 512, 512], P('head'), may hold values from -0.25 to 0.25
- memory_gain: float32 [4, 512], P('head'), may hold values from 0.1 to 1
- out_weight: bfloat16 [2048, 2048], P('head'), may hold values from -0.125 to 0.125
Outputs:
- layer_out: bfloat16 [65536, 2048], P('seq', 'head')
All inputs are finite; a program needn't handle non-finite values.
Results may differ from a plain program's by a relative error of at most 0.014.
Values may be sent and summed in bfloat16 or wider, within the bound.
No kernel may reach another device: no remote copies, remote signals or barrier semaphores. Data moves between devices by JAX's collectives and lax.ppermute only.
A program may use at most 128 MiB of HBM per device.

v0:
```python
import jax
import jax.numpy as jnp
from jax import lax
from jax.experimental import pallas as pl
from jax.experimental.pallas import tpu as pltpu
from jax.sharding import PartitionSpec as P


HEAD = 512
WINDOW = 1024
NS_STEPS = 2
COEF_A = 3.4445
COEF_B = -4.775
COEF_C = 2.0315
EPSILON = 1e-06

CHUNK = 256
BF = jnp.bfloat16
F32 = jnp.float32
MIB = 1 << 20

PLANE = 4
PLANES = 16

ROW_BY_ROW = (((1,), (1,)), ((), ()))
COL_BY_COL = (((0,), (0,)), ((), ()))


def dot(a, b):
    return jnp.dot(a, b, preferred_element_type=F32)


def dot_on(a, b, dims):
    return lax.dot_general(a, b, dims, preferred_element_type=F32)


def any_spec():
    return pl.BlockSpec(memory_space=pl.ANY)


def sigmoid(x):
    return 1.0 / (1.0 + jnp.exp(-x))


def grads_body(where, k_ref, v_ref, rate_ref, gate_ref, lift_ref, down_ref, out_ref, acc, w16):
    step = pl.program_id(0)

    @pl.when(step == 0)
    def _():
        w16[0] = gate_ref[0].astype(BF)
        w16[1] = lift_ref[0].astype(BF)
        w16[2] = down_ref[0].astype(BF)
        acc[...] = jnp.zeros_like(acc)

    keys = k_ref[...]
    rates = jnp.where(where[0] == 0, rate_ref[0:1, :], rate_ref[1:2, :])
    rate_col = jnp.broadcast_to(rates, (128, rates.shape[1])).T[:, :1]
    target = (-rate_col * v_ref[...].astype(F32)).astype(BF)
    gate_pre = dot(keys, w16[0])
    lift_pre = dot(keys, w16[1])
    back_hidden = dot_on(target, w16[2], ROW_BY_ROW)
    sig = sigmoid(gate_pre)
    activated = gate_pre * sig
    hidden = (activated * lift_pre).astype(BF)
    back_gate = (back_hidden * lift_pre * sig * (1.0 + gate_pre * (1.0 - sig))).astype(BF)
    back_lift = (back_hidden * activated).astype(BF)
    acc[0] += dot_on(keys, back_gate, COL_BY_COL)
    acc[1] += dot_on(keys, back_lift, COL_BY_COL)
    acc[2] += dot_on(hidden, target, COL_BY_COL)

    @pl.when(step == pl.num_programs(0) - 1)
    def _():
        for i in range(3):
            out_ref[i * HEAD : (i + 1) * HEAD, :] = acc[i].astype(out_ref.dtype)


def head_grads(which, keys, values, rates, gate, lift, down, dtype):
    tokens = keys.shape[0]
    rows = 256
    weight = pl.BlockSpec((1, HEAD, HEAD), lambda i, w: (w[0], 0, 0))
    token = pl.BlockSpec((rows, HEAD), lambda i, w: (i, w[0]))
    return pl.pallas_call(
        grads_body,
        out_shape=jax.ShapeDtypeStruct((3 * HEAD, HEAD), dtype),
        grid_spec=pltpu.PrefetchScalarGridSpec(
            num_scalar_prefetch=1,
            grid=(tokens // rows,),
            in_specs=[
                token,
                token,
                pl.BlockSpec((2, rows), lambda i, w: (0, i)),
                weight,
                weight,
                weight,
            ],
            out_specs=pl.BlockSpec((3 * HEAD, HEAD), lambda i, w: (0, 0)),
            scratch_shapes=[pltpu.VMEM((3, HEAD, HEAD), F32), pltpu.VMEM((3, HEAD, HEAD), BF)],
        ),
        compiler_params=pltpu.CompilerParams(
            dimension_semantics=("arbitrary",), vmem_limit_bytes=32 * MIB
        ),
        name="head_grads",
    )(which, keys, values, rates, gate, lift, down)


def renew_body(where, g_ref, gate_ref, lift_ref, down_ref, out_ref, olds, sems):
    copies = [
        pltpu.make_async_copy(ref.at[where[0]], olds.at[i], sems.at[i])
        for i, ref in enumerate((gate_ref, lift_ref, down_ref))
    ]
    for copy in copies:
        copy.start()
    eye = (
        lax.broadcasted_iota(jnp.int32, (HEAD, HEAD), 0)
        == lax.broadcasted_iota(jnp.int32, (HEAD, HEAD), 1)
    ).astype(F32)
    iterates, grams = [], []
    for i in range(3):
        g = g_ref[i * HEAD : (i + 1) * HEAD, :]
        wide = g.astype(F32)
        gram = dot_on(g, g, COL_BY_COL)
        squares = jnp.sum(wide * wide, axis=0, keepdims=True)
        inverse = lax.rsqrt(jnp.sum(squares, axis=1, keepdims=True) + EPSILON)
        iterates.append((wide * inverse).astype(BF))
        grams.append(gram * (inverse * inverse))
    for sweep in range(NS_STEPS):
        polys = []
        for i in range(3):
            half = grams[i].astype(BF)
            square = dot(half, half)
            polys.append((COEF_A * eye + COEF_B * grams[i] + COEF_C * square).astype(BF))
        for i in range(3):
            iterates[i] = dot(iterates[i], polys[i]).astype(BF)
        if sweep + 1 < NS_STEPS:
            for i in range(3):
                grams[i] = dot_on(iterates[i], iterates[i], COL_BY_COL)
    for i in range(3):
        copies[i].wait()
        old = olds[i]
        change = old - iterates[i].astype(F32)
        old_square = jnp.sum(old * old, axis=0, keepdims=True)
        new_square = jnp.sum(change * change, axis=0, keepdims=True)
        out_ref[i * HEAD : (i + 1) * HEAD, :] = (
            change * jnp.sqrt(old_square / (new_square + EPSILON))
        ).astype(BF)


def renewed_weights(which, grads, gate, lift, down):
    whole = pl.BlockSpec((3 * HEAD, HEAD), lambda i, w: (0, 0))
    return pl.pallas_call(
        renew_body,
        out_shape=jax.ShapeDtypeStruct((3 * HEAD, HEAD), BF),
        grid_spec=pltpu.PrefetchScalarGridSpec(
            num_scalar_prefetch=1,
            grid=(1,),
            in_specs=[whole, any_spec(), any_spec(), any_spec()],
            out_specs=whole,
            scratch_shapes=[pltpu.VMEM((3, HEAD, HEAD), F32), pltpu.SemaphoreType.DMA((3,))],
        ),
        compiler_params=pltpu.CompilerParams(vmem_limit_bytes=48 * MIB),
        name="renewed_weights",
    )(which, grads, gate, lift, down)


def attention_chunk(at, has_edge, queries, keys, values, edge_keys, edge_values, after):
    blocks = WINDOW // CHUNK
    total = blocks + 1
    from_edge = blocks - at
    scale = HEAD ** (-0.5)

    def body(flag, q_ref, *refs):
        k_refs, v_refs, out_ref = refs[:total], refs[total : 2 * total], refs[-1]
        q = q_ref[...]
        row = lax.broadcasted_iota(jnp.int32, (CHUNK, CHUNK), 0)
        col = lax.broadcasted_iota(jnp.int32, (CHUNK, CHUNK), 1)
        scores = [dot_on(q, k_refs[j][...], ROW_BY_ROW) for j in range(total)]
        scores[0] = jnp.where(col > row, scores[0], -jnp.inf)
        scores[-1] = jnp.where(col <= row, scores[-1], -jnp.inf)
        edge_on = flag[0] > 0

        def rowmax(parts):
            best = parts[0]
            for part in parts[1:]:
                best = jnp.maximum(best, part)
            return jnp.max(best, axis=1, keepdims=True)

        own_max = rowmax(scores[from_edge:])
        both_max = jnp.maximum(own_max, rowmax(scores[:from_edge]))
        largest = jnp.where(edge_on, both_max, own_max)
        edge_largest = jnp.where(edge_on, both_max, jnp.inf)
        weights = [
            jnp.exp((scores[j] - (edge_largest if j < from_edge else largest)) * scale)
            for j in range(total)
        ]
        together = weights[0]
        for part in weights[1:]:
            together = together + part
        summed = jnp.sum(together, axis=1, keepdims=True)
        mixed = dot(weights[0].astype(BF), v_refs[0][...])
        for j in range(1, total):
            mixed = mixed + dot(weights[j].astype(BF), v_refs[j][...])
        out_ref[...] = mixed / summed

    def spec(row):
        return pl.BlockSpec((CHUNK, HEAD), lambda h, flag: (row, h))

    rows = [spec(at + j) for j in range(from_edge)] + [spec(j) for j in range(at + 1)]
    key_args = [edge_keys] * from_edge + [keys] * (at + 1)
    value_args = [edge_values] * from_edge + [values] * (at + 1)
    width = queries.shape[1]
    return pl.pallas_call(
        body,
        out_shape=jax.ShapeDtypeStruct((CHUNK, width), F32),
        grid_spec=pltpu.PrefetchScalarGridSpec(
            num_scalar_prefetch=1,
            grid=(width // HEAD,),
            in_specs=[spec(at)] + rows + rows + [any_spec()] * len(after),
            out_specs=pl.BlockSpec((CHUNK, HEAD), lambda h, flag: (0, h)),
        ),
        compiler_params=pltpu.CompilerParams(vmem_limit_bytes=32 * MIB),
    )(has_edge, queries, *key_args, *value_args, *after)


def tail_body(where, q0, q1, a0, a1, w0, w1, gain, s0, s1, o0, o1, send_ref, own_ref):
    combined = []
    for q_ref, a_ref, w_ref, head in ((q0, a0, w0, where[0]), (q1, a1, w1, 1 - where[0])):
        q = q_ref[...]
        gate = dot(q, w_ref[0:HEAD, :])
        lift = dot(q, w_ref[HEAD : 2 * HEAD, :])
        hidden = (gate * sigmoid(gate) * lift).astype(BF)
        out = dot(hidden, w_ref[2 * HEAD :, :])
        mean_square = jnp.mean(out * out, axis=1, keepdims=True)
        scale = jnp.where(head == 0, gain[0:1, :], gain[1:2, :])
        combined.append((a_ref[...] + out * lax.rsqrt(mean_square + EPSILON) * scale).astype(BF))
    send_ref[...] = (dot(combined[0], s0[...]) + dot(combined[1], s1[...])).astype(BF)
    own_ref[...] = dot(combined[0], o0[...]) + dot(combined[1], o1[...])


def tail_chunk(at, where, queries, attended, mine, theirs, gain, out_weight):
    columns = out_weight.shape[1] // 2
    whole = pl.BlockSpec((3 * HEAD, HEAD), lambda i, w: (0, 0))

    def token(row, mirror):
        return pl.BlockSpec((CHUNK, HEAD), lambda i, w: (row, 1 - w[0] if mirror else w[0]))

    def out_rows(mirror, send):
        return pl.BlockSpec(
            (HEAD, columns),
            lambda i, w: (1 - w[0] if mirror else w[0], 1 - w[1] if send else w[1]),
        )

    block = pl.BlockSpec((CHUNK, columns), lambda i, w: (0, 0))
    return pl.pallas_call(
        tail_body,
        out_shape=(
            jax.ShapeDtypeStruct((CHUNK, columns), BF),
            jax.ShapeDtypeStruct((CHUNK, columns), F32),
        ),
        grid_spec=pltpu.PrefetchScalarGridSpec(
            num_scalar_prefetch=1,
            grid=(1,),
            in_specs=[
                token(at, False),
                token(at, True),
                token(0, False),
                token(0, True),
                whole,
                whole,
                pl.BlockSpec((2, HEAD), lambda i, w: (0, 0)),
                out_rows(False, True),
                out_rows(True, True),
                out_rows(False, False),
                out_rows(True, False),
            ],
            out_specs=[block, block],
        ),
        compiler_params=pltpu.CompilerParams(vmem_limit_bytes=40 * MIB),
    )(
        where,
        queries,
        queries,
        attended,
        attended,
        mine,
        theirs,
        gain,
        out_weight,
        out_weight,
        out_weight,
        out_weight,
    )


def partner(value, flip):
    count = lax.axis_size("seq")
    return lax.ppermute(value, "seq", [(i, i ^ flip) for i in range(count)])


def over_planes(value):
    groups = [[p * PLANE + r for p in range(PLANES)] for r in range(PLANE)]
    return lax.all_to_all(value, "seq", 0, 0, tiled=True, axis_index_groups=groups)


def shards(
    queries,
    key_rows,
    value_rows,
    token_rates,
    gate_fast,
    lift_fast,
    down_fast,
    memory_gain,
    out_weight,
):
    queries, key_rows, value_rows, gate_fast, lift_fast, down_fast, out_weight = (
        pltpu.with_memory_space_constraint(x, pltpu.HBM)
        for x in (queries, key_rows, value_rows, gate_fast, lift_fast, down_fast, out_weight)
    )
    tokens_here = queries.shape[0]
    chunks = tokens_here // CHUNK
    seq = lax.axis_index("seq")
    core = (seq % 2).astype(jnp.int32)
    head = lax.axis_index("head").astype(jnp.int32)
    where = jnp.stack([core, head])
    mirrored = jnp.stack([1 - core, head])
    has_edge = jnp.where(seq > 0, 1, 0).astype(jnp.int32).reshape(1)

    fast = (gate_fast, lift_fast, down_fast)
    tokens = (key_rows, value_rows, token_rates)
    grads_send = head_grads(mirrored, *tokens, *fast, BF)
    grads_got = partner(grads_send, 1)
    grads_mine = head_grads(where, *tokens, *fast, F32)

    count = lax.axis_size("seq")
    along = [(i, i + 1) for i in range(count - 1)]
    edge_keys = lax.ppermute(key_rows, "seq", along)
    edge_values = lax.ppermute(value_rows, "seq", along)

    chip_sum = (grads_mine + grads_got.astype(F32)).astype(BF)
    slices = over_planes(chip_sum.reshape(PLANES, -1, HEAD))
    part = slices.astype(F32).sum(axis=0).astype(BF)
    other = partner(part, 2)
    part = (part.astype(F32) + other.astype(F32)).astype(BF)
    spread = jnp.broadcast_to(part[None], (PLANES, *part.shape))
    grads = over_planes(spread).reshape(3 * HEAD, HEAD)

    weights_mine = renewed_weights(where, grads, *fast)
    weights_theirs = partner(weights_mine, 1)

    head_pair = [(0, 1), (1, 0)]
    owns, arrivals = [], []
    after = ()
    for at in range(chunks):
        attended = attention_chunk(
            at, has_edge, queries, key_rows, value_rows, edge_keys, edge_values, after
        )
        send, own = tail_chunk(
            at, where, queries, attended, weights_mine, weights_theirs, memory_gain, out_weight
        )
        owns.append(own)
        arrivals.append(lax.ppermute(send, "head", head_pair))
        after = (send,)
    out = jnp.zeros((tokens_here, owns[0].shape[1]), BF)
    for at in range(chunks):
        rows = (owns[at] + arrivals[at].astype(F32)).astype(BF)
        out = lax.dynamic_update_slice(out, rows, (at * CHUNK, 0))
    return out


def solution(mesh):
    return jax.shard_map(
        shards,
        mesh=mesh,
        in_specs=(
            P("seq", "head"),
            P("seq", "head"),
            P("seq", "head"),
            P("head", "seq"),
            P("head", None, None),
            P("head", None, None),
            P("head", None, None),
            P("head", None),
            P("head", None),
        ),
        out_specs=P("seq", "head"),
        check_vma=False,
    )
```

profile of v0, /device:TPU:32, one launch (start us, length us, event | category | flops | bytes accessed | tf_op | source)
XLA Modules:
  0.0 185.8 jit_solution(12006015020828069310)
XLA Ops:
  0.0 0.1 pad_add_fusion.1.where
  0.1 0.0 copy-start.1
  0.1 0.7 copy-done.1
  0.8 0.0 copy-start.2
  0.8 8.4 %head_grads.3 = bf16[1536,512]{1,0:T(8,128)(2,1)S(1)} custom-call(s32[2]{0:T(128)S(1)} %pad_add_fusion.1.where, bf16[1024,1024]{1,0:T(8,128)(2,1)} %refs_4_.7, bf16[1024,1024]{1,0:T(8,128)(2,1)} %refs_9_.7, f32[2,1024]{1,0:T(2,128)S(1)} %copy-done.1, f32[2,512,512]{2,1,0:T(8,128)} %gate_ref.5, f32[2,512,512]{2,1,0:T(8,128)} %lift_ref.5, f32[2,512,512]{2,1,0:T(8,128)} %down_ref.5), custom_call_target="tpu_custom_call" | custom-call | tf_op jit(solution)/shard_map/head_grads/pallas_call | solution.py:82
  9.2 0.1 collective-permute-start.2
  9.2 0.1 pad_add_fusion.where
  9.3 0.0 copy-done.2
  9.3 8.4 %head_grads.2 = f32[1536,512]{1,0:T(8,128)S(1)} custom-call(s32[2]{0:T(128)S(1)} %pad_add_fusion.where, bf16[1024,1024]{1,0:T(8,128)(2,1)} %refs_4_.7, bf16[1024,1024]{1,0:T(8,128)(2,1)} %refs_9_.7, f32[2,1024]{1,0:T(2,128)S(1)} %copy-done.2, f32[2,512,512]{2,1,0:T(8,128)} %gate_ref.5, f32[2,512,512]{2,1,0:T(8,128)} %lift_ref.5, f32[2,512,512]{2,1,0:T(8,128)} %down_ref.5), custom_call_target="tpu_custom_call" | custom-call | tf_op jit(solution)/shard_map/head_grads/pallas_call | solution.py:82
  17.8 0.0 collective-permute-done.2
  17.8 0.6 add_convert_fusion
  18.3 28.6 %all_to_all.10 = bf16[16,96,512]{2,1,0:T(8,128)(2,1)S(1)} all-to-all(bf16[16,96,512]{2,1,0:T(8,128)(2,1)S(1)} %bitcast.7), channel_id=1, replica_groups={{0,4,8,12,16,20,24,28,32,36,40,44,48,52,56,60},{1,5,9,13,17,21,25,29,33..., dimensions={0} | all-to-all | bytes 3145728 | tf_op jit(solution)/shard_map/all_to_all | solution.py:301
  46.9 0.2 reduce_sum.12
  47.2 1.7 collective-permute-start.3
  48.8 3.0 %collective-permute-done.3 = bf16[96,512]{1,0:T(8,128)(2,1)S(1)} collective-permute-done((bf16[96,512]{1,0:T(8,128)(2,1)S(1)}, bf16[96,512]{1,0:T(8,128)(2,1)S(1)}, u32[]{:S(2)}, u32[]{:S(2)}) %collective-permute-start.3) | collective-permute-done | bytes 98336 | tf_op jit(solution)/shard_map/ppermute | solution.py:296
  51.9 1.3 broadcast_in_dim.2
  53.2 6.2 %all-to-all-start.1 = ((bf16[16,96,512]{2,1,0:T(8,128)(2,1)}), bf16[16,96,512]{2,1,0:T(8,128)(2,1)S(1)}, u32[]{:S(2)}, u32[]{:S(2)}) async-start(bf16[16,96,512]{2,1,0:T(8,128)(2,1)} %broadcast_in_dim.2), calls=%async_computation.1 | async-start | bytes 3145728 | tf_op jit(solution)/shard_map/all_to_all | solution.py:301
  59.4 1.9 %collective-permute-start = (bf16[1024,1024]{1,0:T(8,128)(2,1)}, bf16[1024,1024]{1,0:T(8,128)(2,1)}, u32[]{:S(2)}, u32[]{:S(2)}) collective-permute-start(bf16[1024,1024]{1,0:T(8,128)(2,1)} %refs_4_.7), channel_id=1, source_target_pairs={{0,1},{1,2},{2,3},{3,4},{4,5},{5,6},{6,7},{7,8},{8,9},{9,10},{10,1... | collective-permute-start | bytes 6291464 | tf_op jit(solution)/shard_map/ppermute | solution.py:336
  61.3 3.8 %collective-permute-start.1 = (bf16[1024,1024]{1,0:T(8,128)(2,1)}, bf16[1024,1024]{1,0:T(8,128)(2,1)}, u32[]{:S(2)}, u32[]{:S(2)}) collective-permute-start(bf16[1024,1024]{1,0:T(8,128)(2,1)} %refs_9_.7), channel_id=1, source_target_pairs={{0,1},{1,2},{2,3},{3,4},{4,5},{5,6},{6,7},{7,8},{8,9},{9,10},{10,1... | collective-permute-start | bytes 6291464 | tf_op jit(solution)/shard_map/ppermute | solution.py:337
  65.1 14.0 %all-to-all-done.1 = bf16[16,96,512]{2,1,0:T(8,128)(2,1)S(1)} async-done(((bf16[16,96,512]{2,1,0:T(8,128)(2,1)}), bf16[16,96,512]{2,1,0:T(8,128)(2,1)S(1)}, u32[]{:S(2)}, u32[]{:S(2)}) %all-to-all-start.1) | async-done | bytes 1572896 | tf_op jit(solution)/shard_map/all_to_all | solution.py:301
  79.1 7.1 %renewed_weights.1.w0 = bf16[1536,512]{1,0:T(8,128)(2,1)S(1)} custom-call(s32[2]{0:T(128)S(1)} %pad_add_fusion.where, bf16[1536,512]{1,0:T(8,128)(2,1)S(1)} %bitcast.6, f32[2,512,512]{2,1,0:T(8,128)} %gate_ref.5, f32[2,512,512]{2,1,0:T(8,128)} %lift_ref.5, f32[2,512,512]{2,1,0:T(8,128)} %down_ref.5), custom_call_target="tpu_custom_call" | custom-call | tf_op jit(solution)/shard_map/renewed_weights/pallas_call | solution.py:150
  86.2 0.1 collective-permute-start.4
  86.3 14.8 %collective-permute-done.refs_0_.refs_1_.refs_2_.refs_3_ = bf16[1024,1024]{1,0:T(8,128)(2,1)} collective-permute-done((bf16[1024,1024]{1,0:T(8,128)(2,1)}, bf16[1024,1024]{1,0:T(8,128)(2,1)}, u32[]{:S(2)}, u32[]{:S(2)}) %collective-permute-start) | collective-permute-done | bytes 2097184 | tf_op jit(solution)/shard_map/ppermute | solution.py:336
  101.2 22.5 %collective-permute-done.1.refs_5_.refs_6_.refs_7_.refs_8_ = bf16[1024,1024]{1,0:T(8,128)(2,1)} collective-permute-done((bf16[1024,1024]{1,0:T(8,128)(2,1)}, bf16[1024,1024]{1,0:T(8,128)(2,1)}, u32[]{:S(2)}, u32[]{:S(2)}) %collective-permute-start.1) | collective-permute-done | bytes 2097184 | tf_op jit(solution)/shard_map/ppermute | solution.py:337
  123.7 0.0 copy-start
  123.7 5.5 %shard_map.91.a0.a1 = f32[256,1024]{1,0:T(8,128)S(1)} custom-call(s32[1]{0:T(128)} %bitcast.2.flag, bf16[1024,1024]{1,0:T(8,128)(2,1)} %q1.7, bf16[1024,1024]{1,0:T(8,128)(2,1)} %collective-permute-done.refs_0_.refs_1_.refs_2_.refs_3_, bf16[1024,1024]{1,0:T(8,128)(2,1)} %collective-permute-done.refs_0_.refs_1_.refs_2_.refs_3_, ...), custom_call_target="tpu_custom_call" | custom-call | tf_op jit(solution)/shard_map/pallas_call | solution.py:211
  129.2 0.0 collective-permute-done.4.w1
  129.2 0.0 copy-done
  129.2 5.3 %shard_map.92 = (bf16[256,1024]{1,0:T(8,128)(2,1)S(1)}, f32[256,1024]{1,0:T(8,128)S(1)}) custom-call(s32[2]{0:T(128)S(1)} %pad_add_fusion.where, bf16[1024,1024]{1,0:T(8,128)(2,1)} %q1.7, bf16[1024,1024]{1,0:T(8,128)(2,1)} %q1.7, f32[256,1024]{1,0:T(8,128)S(1)} %shard_map.91.a0.a1, f32[256,1024]{1,0:T(8,128)S(1)} %shard_map.91.a0.a1, ...), custom_call_target="tpu_custom_call" | custom-call | tf_op jit(solution)/shard_map/pallas_call | solution.py:253
  134.6 3.2 %collective-permute-start.5 = (bf16[256,1024]{1,0:T(8,128)(2,1)S(1)}, bf16[256,1024]{1,0:T(8,128)(2,1)S(1)}, u32[]{:S(2)}, u32[]{:S(2)}) collective-permute-start(bf16[256,1024]{1,0:T(8,128)(2,1)S(1)} %get-tuple-element.14.refs_10_), channel_id=1, source_target_pairs={{0,64},{64,0},{1,65},{65,1},{2,66},{66,2},{3,67},{67,3},{4,68},{68... | collective-permute-start | bytes 1572872 | tf_op jit(solution)/shard_map/ppermute | solution.py:361
  137.8 5.5 %shard_map.93.a0.a1 = f32[256,1024]{1,0:T(8,128)S(1)} custom-call(s32[1]{0:T(128)} %bitcast.2.flag, bf16[1024,1024]{1,0:T(8,128)(2,1)} %q1.7, bf16[1024,1024]{1,0:T(8,128)(2,1)} %collective-permute-done.refs_0_.refs_1_.refs_2_.refs_3_, bf16[1024,1024]{1,0:T(8,128)(2,1)} %collective-permute-done.refs_0_.refs_1_.refs_2_.refs_3_, ...), custom_call_target="tpu_custom_call" | custom-call | tf_op jit(solution)/shard_map/pallas_call | solution.py:211
  143.3 5.3 %shard_map.94 = (bf16[256,1024]{1,0:T(8,128)(2,1)S(1)}, f32[256,1024]{1,0:T(8,128)S(1)}) custom-call(s32[2]{0:T(128)S(1)} %pad_add_fusion.where, bf16[1024,1024]{1,0:T(8,128)(2,1)} %q1.7, bf16[1024,1024]{1,0:T(8,128)(2,1)} %q1.7, f32[256,1024]{1,0:T(8,128)S(1)} %shard_map.93.a0.a1, f32[256,1024]{1,0:T(8,128)S(1)} %shard_map.93.a0.a1, ...), custom_call_target="tpu_custom_call" | custom-call | tf_op jit(solution)/shard_map/pallas_call | solution.py:253
  148.6 0.7 collective-permute-start.6
  149.4 5.5 %shard_map.95.a0.a1 = f32[256,1024]{1,0:T(8,128)S(1)} custom-call(s32[1]{0:T(128)} %bitcast.2.flag, bf16[1024,1024]{1,0:T(8,128)(2,1)} %q1.7, bf16[1024,1024]{1,0:T(8,128)(2,1)} %collective-permute-done.refs_0_.refs_1_.refs_2_.refs_3_, bf16[1024,1024]{1,0:T(8,128)(2,1)} %collective-permute-done.refs_0_.refs_1_.refs_2_.refs_3_, bf16[1024,1024]{1,0:T(8,128)(2,1)} %refs_4_.7, ...), custom_call_target="tpu_custom_call" | custom-call | tf_op jit(solution)/shard_map/pallas_call | solution.py:211
  154.9 5.3 %shard_map.96 = (bf16[256,1024]{1,0:T(8,128)(2,1)S(1)}, f32[256,1024]{1,0:T(8,128)S(1)}) custom-call(s32[2]{0:T(128)S(1)} %pad_add_fusion.where, bf16[1024,1024]{1,0:T(8,128)(2,1)} %q1.7, bf16[1024,1024]{1,0:T(8,128)(2,1)} %q1.7, f32[256,1024]{1,0:T(8,128)S(1)} %shard_map.95.a0.a1, f32[256,1024]{1,0:T(8,128)S(1)} %shard_map.95.a0.a1, ...), custom_call_target="tpu_custom_call" | custom-call | tf_op jit(solution)/shard_map/pallas_call | solution.py:253
  160.2 3.0 %collective-permute-start.7 = (bf16[256,1024]{1,0:T(8,128)(2,1)S(1)}, bf16[256,1024]{1,0:T(8,128)(2,1)S(1)}, u32[]{:S(2)}, u32[]{:S(2)}) collective-permute-start(bf16[256,1024]{1,0:T(8,128)(2,1)S(1)} %get-tuple-element.18.refs_10_), channel_id=1, source_target_pairs={{0,64},{64,0},{1,65},{65,1},{2,66},{66,2},{3,67},{67,3},{4,68},{68... | collective-permute-start | bytes 1572872 | tf_op jit(solution)/shard_map/ppermute | solution.py:361
  163.2 5.5 %shard_map.97.a0.a1 = f32[256,1024]{1,0:T(8,128)S(1)} custom-call(s32[1]{0:T(128)} %bitcast.2.flag, bf16[1024,1024]{1,0:T(8,128)(2,1)} %q1.7, bf16[1024,1024]{1,0:T(8,128)(2,1)} %collective-permute-done.refs_0_.refs_1_.refs_2_.refs_3_, bf16[1024,1024]{1,0:T(8,128)(2,1)} %refs_4_.7, bf16[1024,1024]{1,0:T(8,128)(2,1)} %refs_4_.7, bf16[1024,1024]{1,0:T(8,128)(2,1)} %refs_4_.7, ...), custom_call_target="tpu_custom_call" | custom-call | tf_op jit(solution)/shard_map/pallas_call | solution.py:211
  168.8 5.4 %shard_map.98 = (bf16[256,1024]{1,0:T(8,128)(2,1)S(1)}, f32[256,1024]{1,0:T(8,128)S(1)}) custom-call(s32[2]{0:T(128)S(1)} %pad_add_fusion.where, bf16[1024,1024]{1,0:T(8,128)(2,1)} %q1.7, bf16[1024,1024]{1,0:T(8,128)(2,1)} %q1.7, f32[256,1024]{1,0:T(8,128)S(1)} %shard_map.97.a0.a1, f32[256,1024]{1,0:T(8,128)S(1)} %shard_map.97.a0.a1, ...), custom_call_target="tpu_custom_call" | custom-call | tf_op jit(solution)/shard_map/pallas_call | solution.py:253
  174.1 0.7 collective-permute-start.8
  174.8 0.0 collective-permute-done.5
  174.8 0.2 add_convert_fusion.4
  175.0 0.2 dynamic_update_slice.12
  175.2 0.0 collective-permute-done.6
  175.2 0.2 fusion
  175.4 0.0 collective-permute-done.7
  175.4 0.2 fusion.1
  175.6 0.0 copy-start.3
  175.6 9.3 %collective-permute-done.8 = bf16[256,1024]{1,0:T(8,128)(2,1)S(1)} collective-permute-done((bf16[256,1024]{1,0:T(8,128)(2,1)S(1)}, bf16[256,1024]{1,0:T(8,128)(2,1)S(1)}, u32[]{:S(2)}, u32[]{:S(2)}) %collective-permute-start.8) | collective-permute-done | bytes 524320 | tf_op jit(solution)/shard_map/ppermute | solution.py:361
  184.9 0.0 copy-done.3
  184.9 1.0 fusion.2
  (1 shorter events, 0.0 us)
Async XLA Ops:
  0.1 0.7 copy-start.1
  0.8 8.6 %copy-start.2 = (f32[2,1024]{1,0:T(2,128)S(1)}, f32[2,1024]{1,0:T(2,128)}, u32[]{:S(2)}) copy-start(f32[2,1024]{1,0:T(2,128)} %rate_ref.3) | copy-start | bytes 24580
  9.2 8.6 %collective-permute-start.2 = (bf16[1536,512]{1,0:T(8,128)(2,1)S(1)}, bf16[1536,512]{1,0:T(8,128)(2,1)S(1)}, u32[]{:S(2)}, u32[]{:S(2)}) collective-permute-start(bf16[1536,512]{1,0:T(8,128)(2,1)S(1)} %head_grads.3), channel_id=1, source_target_pairs={{0,1},{1,0},{2,3},{3,2},{4,5},{5,4},{6,7},{7,6},{8,9},{9,8},{10,11... | collective-permute-start | bytes 4718600 | tf_op jit(solution)/shard_map/ppermute | solution.py:296
  47.2 4.7 %collective-permute-start.3 = (bf16[96,512]{1,0:T(8,128)(2,1)S(1)}, bf16[96,512]{1,0:T(8,128)(2,1)S(1)}, u32[]{:S(2)}, u32[]{:S(2)}) collective-permute-start(bf16[96,512]{1,0:T(8,128)(2,1)S(1)} %reduce_sum.12), channel_id=1, source_target_pairs={{0,2},{1,3},{2,0},{3,1},{4,6},{5,7},{6,4},{7,5},{8,10},{9,11},{10,... | collective-permute-start | bytes 294920 | tf_op jit(solution)/shard_map/ppermute | solution.py:296
  53.2 25.9 %all-to-all-start.1 = ((bf16[16,96,512]{2,1,0:T(8,128)(2,1)}), bf16[16,96,512]{2,1,0:T(8,128)(2,1)S(1)}, u32[]{:S(2)}, u32[]{:S(2)}) async-start(bf16[16,96,512]{2,1,0:T(8,128)(2,1)} %broadcast_in_dim.2), calls=%async_computation.1 | async-start | bytes 3145728 | tf_op jit(solution)/shard_map/all_to_all | solution.py:301
  59.4 41.8 %collective-permute-start = (bf16[1024,1024]{1,0:T(8,128)(2,1)}, bf16[1024,1024]{1,0:T(8,128)(2,1)}, u32[]{:S(2)}, u32[]{:S(2)}) collective-permute-start(bf16[1024,1024]{1,0:T(8,128)(2,1)} %refs_4_.7), channel_id=1, source_target_pairs={{0,1},{1,2},{2,3},{3,4},{4,5},{5,6},{6,7},{7,8},{8,9},{9,10},{10,1... | collective-permute-start | bytes 6291464 | tf_op jit(solution)/shard_map/ppermute | solution.py:336
  61.3 62.3 %collective-permute-start.1 = (bf16[1024,1024]{1,0:T(8,128)(2,1)}, bf16[1024,1024]{1,0:T(8,128)(2,1)}, u32[]{:S(2)}, u32[]{:S(2)}) collective-permute-start(bf16[1024,1024]{1,0:T(8,128)(2,1)} %refs_9_.7), channel_id=1, source_target_pairs={{0,1},{1,2},{2,3},{3,4},{4,5},{5,6},{6,7},{7,8},{8,9},{9,10},{10,1... | collective-permute-start | bytes 6291464 | tf_op jit(solution)/shard_map/ppermute | solution.py:337
  86.2 43.0 %collective-permute-start.4 = (bf16[1536,512]{1,0:T(8,128)(2,1)S(1)}, bf16[1536,512]{1,0:T(8,128)(2,1)S(1)}, u32[]{:S(2)}, u32[]{:S(2)}) collective-permute-start(bf16[1536,512]{1,0:T(8,128)(2,1)S(1)} %renewed_weights.1.w0), channel_id=1, source_target_pairs={{0,1},{1,0},{2,3},{3,2},{4,5},{5,4},{6,7},{7,6},{8,9},{9,8},{10,11... | collective-permute-start | bytes 4718600 | tf_op jit(solution)/shard_map/ppermute | solution.py:296
  123.7 5.6 %copy-start = (f32[2,512]{1,0:T(2,128)S(1)}, f32[2,512]{1,0:T(2,128)}, u32[]{:S(2)}) copy-start(f32[2,512]{1,0:T(2,128)} %gain.7) | copy-start | bytes 12292
  134.6 40.3 %collective-permute-start.5 = (bf16[256,1024]{1,0:T(8,128)(2,1)S(1)}, bf16[256,1024]{1,0:T(8,128)(2,1)S(1)}, u32[]{:S(2)}, u32[]{:S(2)}) collective-permute-start(bf16[256,1024]{1,0:T(8,128)(2,1)S(1)} %get-tuple-element.14.refs_10_), channel_id=1, source_target_pairs={{0,64},{64,0},{1,65},{65,1},{2,66},{66,2},{3,67},{67,3},{4,68},{68... | collective-permute-start | bytes 1572872 | tf_op jit(solution)/shard_map/ppermute | solution.py:361
  148.6 26.6 %collective-permute-start.6 = (bf16[256,1024]{1,0:T(8,128)(2,1)S(1)}, bf16[256,1024]{1,0:T(8,128)(2,1)S(1)}, u32[]{:S(2)}, u32[]{:S(2)}) collective-permute-start(bf16[256,1024]{1,0:T(8,128)(2,1)S(1)} %get-tuple-element.16.refs_10_), channel_id=1, source_target_pairs={{0,64},{64,0},{1,65},{65,1},{2,66},{66,2},{3,67},{67,3},{4,68},{68... | collective-permute-start | bytes 1572872 | tf_op jit(solution)/shard_map/ppermute | solution.py:361
  160.2 15.2 %collective-permute-start.7 = (bf16[256,1024]{1,0:T(8,128)(2,1)S(1)}, bf16[256,1024]{1,0:T(8,128)(2,1)S(1)}, u32[]{:S(2)}, u32[]{:S(2)}) collective-permute-start(bf16[256,1024]{1,0:T(8,128)(2,1)S(1)} %get-tuple-element.18.refs_10_), channel_id=1, source_target_pairs={{0,64},{64,0},{1,65},{65,1},{2,66},{66,2},{3,67},{67,3},{4,68},{68... | collective-permute-start | bytes 1572872 | tf_op jit(solution)/shard_map/ppermute | solution.py:361
  174.1 10.8 %collective-permute-start.8 = (bf16[256,1024]{1,0:T(8,128)(2,1)S(1)}, bf16[256,1024]{1,0:T(8,128)(2,1)S(1)}, u32[]{:S(2)}, u32[]{:S(2)}) collective-permute-start(bf16[256,1024]{1,0:T(8,128)(2,1)S(1)} %get-tuple-element.20), channel_id=1, source_target_pairs={{0,64},{64,0},{1,65},{65,1},{2,66},{66,2},{3,67},{67,3},{4,68},{68... | collective-permute-start | bytes 1572872 | tf_op jit(solution)/shard_map/ppermute | solution.py:361
  175.6 9.3 %copy-start.3 = (bf16[1024,1024]{1,0:T(8,128)(2,1)}, bf16[1024,1024]{1,0:T(8,128)(2,1)S(1)}, u32[]{:S(2)}) copy-start(bf16[1024,1024]{1,0:T(8,128)(2,1)S(1)} %fusion.1) | copy-start | bytes 6291460
where the time goes:
time: 186 us
  Pallas kernels  67.4 us (36%)
  waiting for transfers between devices  63.7 us (34%)
  blocking collectives  28.6 us (15%)
  starting transfers between devices  21.3 us (11%)
  other arithmetic  2.39 us (1%)
  local copies, waits for them, and re-layouts  2.25 us (1%)
    all_to_all x1, blocking collectives, over_planes(): lax.all_to_all(value, 'seq', 0, 0, tiled=True, axis_index_groups=groups)  28.6 us
    ppermute x1, waiting for transfers between devices, shards(): edge_values = lax.ppermute(value_rows, 'seq', along)  22.5 us
    pallas_call x4, Pallas kernels, attention_chunk(): pl.pallas_call(body, out_shape=jax.ShapeDtypeStruct((CHUNK, width), F32),...  22.1 us
    pallas_call x4, Pallas kernels, tail_chunk(): pl.pallas_call(tail_body, out_shape=(jax.ShapeDtypeStruct((CHUNK, columns...  21.4 us
    pallas_call x2, Pallas kernels, head_grads(): pl.pallas_call(grads_body, out_shape=jax.ShapeDtypeStruct((3 * HEAD, HEAD...  16.8 us
    ppermute x1, waiting for transfers between devices, shards(): edge_keys = lax.ppermute(key_rows, 'seq', along)  14.8 us
    all_to_all x1, waiting for transfers between devices, over_planes(): lax.all_to_all(value, 'seq', 0, 0, tiled=True, axis_index_groups=groups)  14 us
    ppermute x4, waiting for transfers between devices, shards(): arrivals.append(lax.ppermute(send, 'head', head_pair))  9.28 us
  transfers between devices with their start and end apart: 10, of which 5 were waited for; matrix products, arithmetic and copies ran while one was open for 0% of the time, Pallas kernels for 29%

commit v1 on v0

--- a/solution.py
+++ b/solution.py
@@ -39,44 +39,49 @@
 
 
 def sigmoid(x):
-    return 1.0 / (1.0 + jnp.exp(-x))
-
-
-def grads_body(where, k_ref, v_ref, rate_ref, gate_ref, lift_ref, down_ref, out_ref, acc, w16):
+    return 0.5 * jnp.tanh(0.5 * x) + 0.5
+
+
+def grads_body(where, k_ref, v_ref, rate_ref, gate_ref, lift_ref, down_ref, out_ref, acc, w16, back):
     step = pl.program_id(0)
 
     @pl.when(step == 0)
     def _():
-        w16[0] = gate_ref[0].astype(BF)
-        w16[1] = lift_ref[0].astype(BF)
-        w16[2] = down_ref[0].astype(BF)
-        acc[...] = jnp.zeros_like(acc)
+        w16[:, :HEAD] = gate_ref[0].astype(BF)
+        w16[:, HEAD : 2 * HEAD] = lift_ref[0].astype(BF)
+        w16[:, 2 * HEAD :] = down_ref[0].astype(BF)
 
     keys = k_ref[...]
     rates = jnp.where(where[0] == 0, rate_ref[0:1, :], rate_ref[1:2, :])
     rate_col = jnp.broadcast_to(rates, (128, rates.shape[1])).T[:, :1]
     target = (-rate_col * v_ref[...].astype(F32)).astype(BF)
-    gate_pre = dot(keys, w16[0])
-    lift_pre = dot(keys, w16[1])
-    back_hidden = dot_on(target, w16[2], ROW_BY_ROW)
+    gate_pre = dot(keys, w16[:, :HEAD])
+    lift_pre = dot(keys, w16[:, HEAD : 2 * HEAD])
+    back_hidden = dot_on(target, w16[:, 2 * HEAD :], ROW_BY_ROW)
     sig = sigmoid(gate_pre)
     activated = gate_pre * sig
     hidden = (activated * lift_pre).astype(BF)
-    back_gate = (back_hidden * lift_pre * sig * (1.0 + gate_pre * (1.0 - sig))).astype(BF)
-    back_lift = (back_hidden * activated).astype(BF)
-    acc[0] += dot_on(keys, back_gate, COL_BY_COL)
-    acc[1] += dot_on(keys, back_lift, COL_BY_COL)
-    acc[2] += dot_on(hidden, target, COL_BY_COL)
+    back[:, :HEAD] = (back_hidden * lift_pre * (sig + activated * (1.0 - sig))).astype(BF)
+    back[:, HEAD:] = (back_hidden * activated).astype(BF)
+    into = dot_on(keys, back[...], COL_BY_COL)
+    down = dot_on(hidden, target, COL_BY_COL)
+
+    @pl.when(step == 0)
+    def _():
+        acc[:, : 2 * HEAD] = into
+        acc[:, 2 * HEAD :] = down
 
     @pl.when(step == pl.num_programs(0) - 1)
     def _():
-        for i in range(3):
-            out_ref[i * HEAD : (i + 1) * HEAD, :] = acc[i].astype(out_ref.dtype)
+        total_into = acc[:, : 2 * HEAD] + into
+        total_down = acc[:, 2 * HEAD :] + down
+        out_ref[:HEAD, :] = total_into[:, :HEAD].astype(out_ref.dtype)
+        out_ref[HEAD : 2 * HEAD, :] = total_into[:, HEAD:].astype(out_ref.dtype)
+        out_ref[2 * HEAD :, :] = total_down.astype(out_ref.dtype)
 
 
 def head_grads(which, keys, values, rates, gate, lift, down, dtype):
-    tokens = keys.shape[0]
-    rows = 256
+    rows = keys.shape[0] // 2
     weight = pl.BlockSpec((1, HEAD, HEAD), lambda i, w: (w[0], 0, 0))
     token = pl.BlockSpec((rows, HEAD), lambda i, w: (i, w[0]))
     return pl.pallas_call(
@@ -84,7 +89,7 @@
         out_shape=jax.ShapeDtypeStruct((3 * HEAD, HEAD), dtype),
         grid_spec=pltpu.PrefetchScalarGridSpec(
             num_scalar_prefetch=1,
-            grid=(tokens // rows,),
+            grid=(2,),
             in_specs=[
                 token,
                 token,
@@ -94,10 +99,14 @@
                 weight,
             ],
             out_specs=pl.BlockSpec((3 * HEAD, HEAD), lambda i, w: (0, 0)),
-            scratch_shapes=[pltpu.VMEM((3, HEAD, HEAD), F32), pltpu.VMEM((3, HEAD, HEAD), BF)],
+            scratch_shapes=[
+                pltpu.VMEM((HEAD, 3 * HEAD), F32),
+                pltpu.VMEM((HEAD, 3 * HEAD), BF),
+                pltpu.VMEM((rows, 2 * HEAD), BF),
+            ],
         ),
         compiler_params=pltpu.CompilerParams(
-            dimension_semantics=("arbitrary",), vmem_limit_bytes=32 * MIB
+            dimension_semantics=("arbitrary",), vmem_limit_bytes=40 * MIB
         ),
         name="head_grads",
     )(which, keys, values, rates, gate, lift, down)

time: 186 us -> 185 us (level)
  no operation moved by 1% of the time
where the time goes in v1:
time: 185 us; the launch traced here: 184 us
  Pallas kernels  65.7 us (36%)
  waiting for transfers between devices  63.7 us (34%)
  blocking collectives  28.6 us (15%)
  starting transfers between devices  21.3 us (12%)
  other arithmetic  2.39 us (1%)
  local copies, waits for them, and re-layouts  2.25 us (1%)
    all_to_all x1, blocking collectives, over_planes(): lax.all_to_all(value, 'seq', 0, 0, tiled=True, axis_index_groups=groups)  28.6 us
    ppermute x1, waiting for transfers between devices, shards(): edge_values = lax.ppermute(value_rows, 'seq', along)  22.5 us
    pallas_call x4, Pallas kernels, attention_chunk(): pl.pallas_call(body, out_shape=jax.ShapeDtypeStruct((CHUNK, width), F32),...  22.1 us
    pallas_call x4, Pallas kernels, tail_chunk(): pl.pallas_call(tail_body, out_shape=(jax.ShapeDtypeStruct((CHUNK, columns...  21.3 us
    pallas_call x2, Pallas kernels, head_grads(): pl.pallas_call(grads_body, out_shape=jax.ShapeDtypeStruct((3 * HEAD, HEAD...  15.2 us
    ppermute x1, waiting for transfers between devices, shards(): edge_keys = lax.ppermute(key_rows, 'seq', along)  14.8 us
    all_to_all x1, waiting for transfers between devices, over_planes(): lax.all_to_all(value, 'seq', 0, 0, tiled=True, axis_index_groups=groups)  14 us
    ppermute x4, waiting for transfers between devices, shards(): arrivals.append(lax.ppermute(send, 'head', head_pair))  9.28 us
  transfers between devices with their start and end apart: 10, of which 5 were waited for; matrix products, arithmetic and copies ran while one was open for 0% of the time, Pallas kernels for 29%

profile of v1, /device:TPU:32, one launch (start us, length us, event | category | flops | bytes accessed | tf_op | source)
XLA Modules:
  0.0 184.2 jit_solution(4137007290940451039)
XLA Ops:
  0.0 0.1 pad_add_fusion.1.where
  0.1 0.0 copy-start.1
  0.1 0.7 copy-done.1
  0.8 0.0 copy-start.2
  0.8 7.6 %head_grads.3 = bf16[1536,512]{1,0:T(8,128)(2,1)S(1)} custom-call(s32[2]{0:T(128)S(1)} %pad_add_fusion.1.where, bf16[1024,1024]{1,0:T(8,128)(2,1)} %refs_4_.7, bf16[1024,1024]{1,0:T(8,128)(2,1)} %refs_9_.7, f32[2,1024]{1,0:T(2,128)S(1)} %copy-done.1, f32[2,512,512]{2,1,0:T(8,128)} %gate_ref.5, f32[2,512,512]{2,1,0:T(8,128)} %lift_ref.5, f32[2,512,512]{2,1,0:T(8,128)} %down_ref.5), custom_call_target="tpu_custom_call" | custom-call | tf_op jit(solution)/shard_map/head_grads/pallas_call | solution.py:87
  8.4 0.1 collective-permute-start.2
  8.5 0.1 pad_add_fusion.where
  8.5 0.0 copy-done.2
  8.5 7.6 %head_grads.2 = f32[1536,512]{1,0:T(8,128)S(1)} custom-call(s32[2]{0:T(128)S(1)} %pad_add_fusion.where, bf16[1024,1024]{1,0:T(8,128)(2,1)} %refs_4_.7, bf16[1024,1024]{1,0:T(8,128)(2,1)} %refs_9_.7, f32[2,1024]{1,0:T(2,128)S(1)} %copy-done.2, f32[2,512,512]{2,1,0:T(8,128)} %gate_ref.5, f32[2,512,512]{2,1,0:T(8,128)} %lift_ref.5, f32[2,512,512]{2,1,0:T(8,128)} %down_ref.5), custom_call_target="tpu_custom_call" | custom-call | tf_op jit(solution)/shard_map/head_grads/pallas_call | solution.py:87
  16.2 0.0 collective-permute-done.2
  16.2 0.6 add_convert_fusion
  16.7 28.6 %all_to_all.10 = bf16[16,96,512]{2,1,0:T(8,128)(2,1)S(1)} all-to-all(bf16[16,96,512]{2,1,0:T(8,128)(2,1)S(1)} %bitcast.7), channel_id=1, replica_groups={{0,4,8,12,16,20,24,28,32,36,40,44,48,52,56,60},{1,5,9,13,17,21,25,29,33..., dimensions={0} | all-to-all | bytes 3145728 | tf_op jit(solution)/shard_map/all_to_all | solution.py:310
  45.4 0.2 reduce_sum.12
  45.6 1.7 collective-permute-start.3
  47.2 3.0 %collective-permute-done.3 = bf16[96,512]{1,0:T(8,128)(2,1)S(1)} collective-permute-done((bf16[96,512]{1,0:T(8,128)(2,1)S(1)}, bf16[96,512]{1,0:T(8,128)(2,1)S(1)}, u32[]{:S(2)}, u32[]{:S(2)}) %collective-permute-start.3) | collective-permute-done | bytes 98336 | tf_op jit(solution)/shard_map/ppermute | solution.py:305
  50.3 1.3 broadcast_in_dim.2
  51.6 6.2 %all-to-all-start.1 = ((bf16[16,96,512]{2,1,0:T(8,128)(2,1)}), bf16[16,96,512]{2,1,0:T(8,128)(2,1)S(1)}, u32[]{:S(2)}, u32[]{:S(2)}) async-start(bf16[16,96,512]{2,1,0:T(8,128)(2,1)} %broadcast_in_dim.2), calls=%async_computation.1 | async-start | bytes 3145728 | tf_op jit(solution)/shard_map/all_to_all | solution.py:310
  57.8 1.9 %collective-permute-start = (bf16[1024,1024]{1,0:T(8,128)(2,1)}, bf16[1024,1024]{1,0:T(8,128)(2,1)}, u32[]{:S(2)}, u32[]{:S(2)}) collective-permute-start(bf16[1024,1024]{1,0:T(8,128)(2,1)} %refs_4_.7), channel_id=1, source_target_pairs={{0,1},{1,2},{2,3},{3,4},{4,5},{5,6},{6,7},{7,8},{8,9},{9,10},{10,1... | collective-permute-start | bytes 6291464 | tf_op jit(solution)/shard_map/ppermute | solution.py:345
  59.7 3.8 %collective-permute-start.1 = (bf16[1024,1024]{1,0:T(8,128)(2,1)}, bf16[1024,1024]{1,0:T(8,128)(2,1)}, u32[]{:S(2)}, u32[]{:S(2)}) collective-permute-start(bf16[1024,1024]{1,0:T(8,128)(2,1)} %refs_9_.7), channel_id=1, source_target_pairs={{0,1},{1,2},{2,3},{3,4},{4,5},{5,6},{6,7},{7,8},{8,9},{9,10},{10,1... | collective-permute-start | bytes 6291464 | tf_op jit(solution)/shard_map/ppermute | solution.py:346
  63.5 14.0 %all-to-all-done.1 = bf16[16,96,512]{2,1,0:T(8,128)(2,1)S(1)} async-done(((bf16[16,96,512]{2,1,0:T(8,128)(2,1)}), bf16[16,96,512]{2,1,0:T(8,128)(2,1)S(1)}, u32[]{:S(2)}, u32[]{:S(2)}) %all-to-all-start.1) | async-done | bytes 1572896 | tf_op jit(solution)/shard_map/all_to_all | solution.py:310
  77.5 7.1 %renewed_weights.1.w0 = bf16[1536,512]{1,0:T(8,128)(2,1)S(1)} custom-call(s32[2]{0:T(128)S(1)} %pad_add_fusion.where, bf16[1536,512]{1,0:T(8,128)(2,1)S(1)} %bitcast.6, f32[2,512,512]{2,1,0:T(8,128)} %gate_ref.5, f32[2,512,512]{2,1,0:T(8,128)} %lift_ref.5, f32[2,512,512]{2,1,0:T(8,128)} %down_ref.5), custom_call_target="tpu_custom_call" | custom-call | tf_op jit(solution)/shard_map/renewed_weights/pallas_call | solution.py:159
  84.7 0.1 collective-permute-start.4
  84.8 14.8 %collective-permute-done.refs_0_.refs_1_.refs_2_.refs_3_ = bf16[1024,1024]{1,0:T(8,128)(2,1)} collective-permute-done((bf16[1024,1024]{1,0:T(8,128)(2,1)}, bf16[1024,1024]{1,0:T(8,128)(2,1)}, u32[]{:S(2)}, u32[]{:S(2)}) %collective-permute-start) | collective-permute-done | bytes 2097184 | tf_op jit(solution)/shard_map/ppermute | solution.py:345
  99.6 22.5 %collective-permute-done.1.refs_5_.refs_6_.refs_7_.refs_8_ = bf16[1024,1024]{1,0:T(8,128)(2,1)} collective-permute-done((bf16[1024,1024]{1,0:T(8,128)(2,1)}, bf16[1024,1024]{1,0:T(8,128)(2,1)}, u32[]{:S(2)}, u32[]{:S(2)}) %collective-permute-start.1) | collective-permute-done | bytes 2097184 | tf_op jit(solution)/shard_map/ppermute | solution.py:346
  122.1 0.0 copy-start
  122.1 5.5 %shard_map.91.a0.a1 = f32[256,1024]{1,0:T(8,128)S(1)} custom-call(s32[1]{0:T(128)} %bitcast.2.flag, bf16[1024,1024]{1,0:T(8,128)(2,1)} %q1.7, bf16[1024,1024]{1,0:T(8,128)(2,1)} %collective-permute-done.refs_0_.refs_1_.refs_2_.refs_3_, bf16[1024,1024]{1,0:T(8,128)(2,1)} %collective-permute-done.refs_0_.refs_1_.refs_2_.refs_3_, ...), custom_call_target="tpu_custom_call" | custom-call | tf_op jit(solution)/shard_map/pallas_call | solution.py:220
  127.6 0.0 collective-permute-done.4.w1
  127.6 0.0 copy-done
  127.6 5.3 %shard_map.92 = (bf16[256,1024]{1,0:T(8,128)(2,1)S(1)}, f32[256,1024]{1,0:T(8,128)S(1)}) custom-call(s32[2]{0:T(128)S(1)} %pad_add_fusion.where, bf16[1024,1024]{1,0:T(8,128)(2,1)} %q1.7, bf16[1024,1024]{1,0:T(8,128)(2,1)} %q1.7, f32[256,1024]{1,0:T(8,128)S(1)} %shard_map.91.a0.a1, f32[256,1024]{1,0:T(8,128)S(1)} %shard_map.91.a0.a1, ...), custom_call_target="tpu_custom_call" | custom-call | tf_op jit(solution)/shard_map/pallas_call | solution.py:262
  133.0 3.2 %collective-permute-start.5 = (bf16[256,1024]{1,0:T(8,128)(2,1)S(1)}, bf16[256,1024]{1,0:T(8,128)(2,1)S(1)}, u32[]{:S(2)}, u32[]{:S(2)}) collective-permute-start(bf16[256,1024]{1,0:T(8,128)(2,1)S(1)} %get-tuple-element.14.refs_10_), channel_id=1, source_target_pairs={{0,64},{64,0},{1,65},{65,1},{2,66},{66,2},{3,67},{67,3},{4,68},{68... | collective-permute-start | bytes 1572872 | tf_op jit(solution)/shard_map/ppermute | solution.py:370
  136.2 5.5 %shard_map.93.a0.a1 = f32[256,1024]{1,0:T(8,128)S(1)} custom-call(s32[1]{0:T(128)} %bitcast.2.flag, bf16[1024,1024]{1,0:T(8,128)(2,1)} %q1.7, bf16[1024,1024]{1,0:T(8,128)(2,1)} %collective-permute-done.refs_0_.refs_1_.refs_2_.refs_3_, bf16[1024,1024]{1,0:T(8,128)(2,1)} %collective-permute-done.refs_0_.refs_1_.refs_2_.refs_3_, ...), custom_call_target="tpu_custom_call" | custom-call | tf_op jit(solution)/shard_map/pallas_call | solution.py:220
  141.7 5.3 %shard_map.94 = (bf16[256,1024]{1,0:T(8,128)(2,1)S(1)}, f32[256,1024]{1,0:T(8,128)S(1)}) custom-call(s32[2]{0:T(128)S(1)} %pad_add_fusion.where, bf16[1024,1024]{1,0:T(8,128)(2,1)} %q1.7, bf16[1024,1024]{1,0:T(8,128)(2,1)} %q1.7, f32[256,1024]{1,0:T(8,128)S(1)} %shard_map.93.a0.a1, f32[256,1024]{1,0:T(8,128)S(1)} %shard_map.93.a0.a1, ...), custom_call_target="tpu_custom_call" | custom-call | tf_op jit(solution)/shard_map/pallas_call | solution.py:262
  147.0 0.7 collective-permute-start.6
  147.7 5.5 %shard_map.95.a0.a1 = f32[256,1024]{1,0:T(8,128)S(1)} custom-call(s32[1]{0:T(128)} %bitcast.2.flag, bf16[1024,1024]{1,0:T(8,128)(2,1)} %q1.7, bf16[1024,1024]{1,0:T(8,128)(2,1)} %collective-permute-done.refs_0_.refs_1_.refs_2_.refs_3_, bf16[1024,1024]{1,0:T(8,128)(2,1)} %collective-permute-done.refs_0_.refs_1_.refs_2_.refs_3_, bf16[1024,1024]{1,0:T(8,128)(2,1)} %refs_4_.7, ...), custom_call_target="tpu_custom_call" | custom-call | tf_op jit(solution)/shard_map/pallas_call | solution.py:220
  153.3 5.3 %shard_map.96 = (bf16[256,1024]{1,0:T(8,128)(2,1)S(1)}, f32[256,1024]{1,0:T(8,128)S(1)}) custom-call(s32[2]{0:T(128)S(1)} %pad_add_fusion.where, bf16[1024,1024]{1,0:T(8,128)(2,1)} %q1.7, bf16[1024,1024]{1,0:T(8,128)(2,1)} %q1.7, f32[256,1024]{1,0:T(8,128)S(1)} %shard_map.95.a0.a1, f32[256,1024]{1,0:T(8,128)S(1)} %shard_map.95.a0.a1, ...), custom_call_target="tpu_custom_call" | custom-call | tf_op jit(solution)/shard_map/pallas_call | solution.py:262
  158.6 3.0 %collective-permute-start.7 = (bf16[256,1024]{1,0:T(8,128)(2,1)S(1)}, bf16[256,1024]{1,0:T(8,128)(2,1)S(1)}, u32[]{:S(2)}, u32[]{:S(2)}) collective-permute-start(bf16[256,1024]{1,0:T(8,128)(2,1)S(1)} %get-tuple-element.18.refs_10_), channel_id=1, source_target_pairs={{0,64},{64,0},{1,65},{65,1},{2,66},{66,2},{3,67},{67,3},{4,68},{68... | collective-permute-start | bytes 1572872 | tf_op jit(solution)/shard_map/ppermute | solution.py:370
  161.6 5.5 %shard_map.97.a0.a1 = f32[256,1024]{1,0:T(8,128)S(1)} custom-call(s32[1]{0:T(128)} %bitcast.2.flag, bf16[1024,1024]{1,0:T(8,128)(2,1)} %q1.7, bf16[1024,1024]{1,0:T(8,128)(2,1)} %collective-permute-done.refs_0_.refs_1_.refs_2_.refs_3_, bf16[1024,1024]{1,0:T(8,128)(2,1)} %refs_4_.7, bf16[1024,1024]{1,0:T(8,128)(2,1)} %refs_4_.7, bf16[1024,1024]{1,0:T(8,128)(2,1)} %refs_4_.7, ...), custom_call_target="tpu_custom_call" | custom-call | tf_op jit(solution)/shard_map/pallas_call | solution.py:220
  167.1 5.3 %shard_map.98 = (bf16[256,1024]{1,0:T(8,128)(2,1)S(1)}, f32[256,1024]{1,0:T(8,128)S(1)}) custom-call(s32[2]{0:T(128)S(1)} %pad_add_fusion.where, bf16[1024,1024]{1,0:T(8,128)(2,1)} %q1.7, bf16[1024,1024]{1,0:T(8,128)(2,1)} %q1.7, f32[256,1024]{1,0:T(8,128)S(1)} %shard_map.97.a0.a1, f32[256,1024]{1,0:T(8,128)S(1)} %shard_map.97.a0.a1, ...), custom_call_target="tpu_custom_call" | custom-call | tf_op jit(solution)/shard_map/pallas_call | solution.py:262
  172.5 0.7 collective-permute-start.8
  173.2 0.0 collective-permute-done.5
  173.2 0.2 add_convert_fusion.4
  173.4 0.2 dynamic_update_slice.12
  173.6 0.0 collective-permute-done.6
  173.6 0.2 fusion
  173.8 0.0 collective-permute-done.7
  173.8 0.2 fusion.1
  174.0 0.0 copy-start.3
  174.0 9.3 %collective-permute-done.8 = bf16[256,1024]{1,0:T(8,128)(2,1)S(1)} collective-permute-done((bf16[256,1024]{1,0:T(8,128)(2,1)S(1)}, bf16[256,1024]{1,0:T(8,128)(2,1)S(1)}, u32[]{:S(2)}, u32[]{:S(2)}) %collective-permute-start.8) | collective-permute-done | bytes 524320 | tf_op jit(solution)/shard_map/ppermute | solution.py:370
  183.3 0.0 copy-done.3
  183.3 1.0 fusion.2
  (1 shorter events, 0.0 us)
Async XLA Ops:
  0.1 0.7 copy-start.1
  0.8 7.8 %copy-start.2 = (f32[2,1024]{1,0:T(2,128)S(1)}, f32[2,1024]{1,0:T(2,128)}, u32[]{:S(2)}) copy-start(f32[2,1024]{1,0:T(2,128)} %rate_ref.3) | copy-start | bytes 24580
  8.4 7.8 %collective-permute-start.2 = (bf16[1536,512]{1,0:T(8,128)(2,1)S(1)}, bf16[1536,512]{1,0:T(8,128)(2,1)S(1)}, u32[]{:S(2)}, u32[]{:S(2)}) collective-permute-start(bf16[1536,512]{1,0:T(8,128)(2,1)S(1)} %head_grads.3), channel_id=1, source_target_pairs={{0,1},{1,0},{2,3},{3,2},{4,5},{5,4},{6,7},{7,6},{8,9},{9,8},{10,11... | collective-permute-start | bytes 4718600 | tf_op jit(solution)/shard_map/ppermute | solution.py:305
  45.6 4.7 %collective-permute-start.3 = (bf16[96,512]{1,0:T(8,128)(2,1)S(1)}, bf16[96,512]{1,0:T(8,128)(2,1)S(1)}, u32[]{:S(2)}, u32[]{:S(2)}) collective-permute-start(bf16[96,512]{1,0:T(8,128)(2,1)S(1)} %reduce_sum.12), channel_id=1, source_target_pairs={{0,2},{1,3},{2,0},{3,1},{4,6},{5,7},{6,4},{7,5},{8,10},{9,11},{10,... | collective-permute-start | bytes 294920 | tf_op jit(solution)/shard_map/ppermute | solution.py:305
  51.6 25.9 %all-to-all-start.1 = ((bf16[16,96,512]{2,1,0:T(8,128)(2,1)}), bf16[16,96,512]{2,1,0:T(8,128)(2,1)S(1)}, u32[]{:S(2)}, u32[]{:S(2)}) async-start(bf16[16,96,512]{2,1,0:T(8,128)(2,1)} %broadcast_in_dim.2), calls=%async_computation.1 | async-start | bytes 3145728 | tf_op jit(solution)/shard_map/all_to_all | solution.py:310
  57.8 41.8 %collective-permute-start = (bf16[1024,1024]{1,0:T(8,128)(2,1)}, bf16[1024,1024]{1,0:T(8,128)(2,1)}, u32[]{:S(2)}, u32[]{:S(2)}) collective-permute-start(bf16[1024,1024]{1,0:T(8,128)(2,1)} %refs_4_.7), channel_id=1, source_target_pairs={{0,1},{1,2},{2,3},{3,4},{4,5},{5,6},{6,7},{7,8},{8,9},{9,10},{10,1... | collective-permute-start | bytes 6291464 | tf_op jit(solution)/shard_map/ppermute | solution.py:345
  59.7 62.3 %collective-permute-start.1 = (bf16[1024,1024]{1,0:T(8,128)(2,1)}, bf16[1024,1024]{1,0:T(8,128)(2,1)}, u32[]{:S(2)}, u32[]{:S(2)}) collective-permute-start(bf16[1024,1024]{1,0:T(8,128)(2,1)} %refs_9_.7), channel_id=1, source_target_pairs={{0,1},{1,2},{2,3},{3,4},{4,5},{5,6},{6,7},{7,8},{8,9},{9,10},{10,1... | collective-permute-start | bytes 6291464 | tf_op jit(solution)/shard_map/ppermute | solution.py:346
  84.7 43.0 %collective-permute-start.4 = (bf16[1536,512]{1,0:T(8,128)(2,1)S(1)}, bf16[1536,512]{1,0:T(8,128)(2,1)S(1)}, u32[]{:S(2)}, u32[]{:S(2)}) collective-permute-start(bf16[1536,512]{1,0:T(8,128)(2,1)S(1)} %renewed_weights.1.w0), channel_id=1, source_target_pairs={{0,1},{1,0},{2,3},{3,2},{4,5},{5,4},{6,7},{7,6},{8,9},{9,8},{10,11... | collective-permute-start | bytes 4718600 | tf_op jit(solution)/shard_map/ppermute | solution.py:305
  122.1 5.6 %copy-start = (f32[2,512]{1,0:T(2,128)S(1)}, f32[2,512]{1,0:T(2,128)}, u32[]{:S(2)}) copy-start(f32[2,512]{1,0:T(2,128)} %gain.7) | copy-start | bytes 12292
  133.0 40.2 %collective-permute-start.5 = (bf16[256,1024]{1,0:T(8,128)(2,1)S(1)}, bf16[256,1024]{1,0:T(8,128)(2,1)S(1)}, u32[]{:S(2)}, u32[]{:S(2)}) collective-permute-start(bf16[256,1024]{1,0:T(8,128)(2,1)S(1)} %get-tuple-element.14.refs_10_), channel_id=1, source_target_pairs={{0,64},{64,0},{1,65},{65,1},{2,66},{66,2},{3,67},{67,3},{4,68},{68... | collective-permute-start | bytes 1572872 | tf_op jit(solution)/shard_map/ppermute | solution.py:370
  147.0 26.6 %collective-permute-start.6 = (bf16[256,1024]{1,0:T(8,128)(2,1)S(1)}, bf16[256,1024]{1,0:T(8,128)(2,1)S(1)}, u32[]{:S(2)}, u32[]{:S(2)}) collective-permute-start(bf16[256,1024]{1,0:T(8,128)(2,1)S(1)} %get-tuple-element.16.refs_10_), channel_id=1, source_target_pairs={{0,64},{64,0},{1,65},{65,1},{2,66},{66,2},{3,67},{67,3},{4,68},{68... | collective-permute-start | bytes 1572872 | tf_op jit(solution)/shard_map/ppermute | solution.py:370
  158.6 15.2 %collective-permute-start.7 = (bf16[256,1024]{1,0:T(8,128)(2,1)S(1)}, bf16[256,1024]{1,0:T(8,128)(2,1)S(1)}, u32[]{:S(2)}, u32[]{:S(2)}) collective-permute-start(bf16[256,1024]{1,0:T(8,128)(2,1)S(1)} %get-tuple-element.18.refs_10_), channel_id=1, source_target_pairs={{0,64},{64,0},{1,65},{65,1},{2,66},{66,2},{3,67},{67,3},{4,68},{68... | collective-permute-start | bytes 1572872 | tf_op jit(solution)/shard_map/ppermute | solution.py:370
  172.5 10.8 %collective-permute-start.8 = (bf16[256,1024]{1,0:T(8,128)(2,1)S(1)}, bf16[256,1024]{1,0:T(8,128)(2,1)S(1)}, u32[]{:S(2)}, u32[]{:S(2)}) collective-permute-start(bf16[256,1024]{1,0:T(8,128)(2,1)S(1)} %get-tuple-element.20), channel_id=1, source_target_pairs={{0,64},{64,0},{1,65},{65,1},{2,66},{66,2},{3,67},{67,3},{4,68},{68... | collective-permute-start | bytes 1572872 | tf_op jit(solution)/shard_map/ppermute | solution.py:370
  174.0 9.3 %copy-start.3 = (bf16[1024,1024]{1,0:T(8,128)(2,1)}, bf16[1024,1024]{1,0:T(8,128)(2,1)S(1)}, u32[]{:S(2)}) copy-start(bf16[1024,1024]{1,0:T(8,128)(2,1)S(1)} %fusion.1) | copy-start | bytes 6291460

commit v2 on v1

--- a/solution.py
+++ b/solution.py
@@ -171,133 +171,202 @@
     )(which, grads, gate, lift, down)
 
 
-def attention_chunk(at, has_edge, queries, keys, values, edge_keys, edge_values, after):
-    blocks = WINDOW // CHUNK
-    total = blocks + 1
-    from_edge = blocks - at
-    scale = HEAD ** (-0.5)
-
-    def body(flag, q_ref, *refs):
-        k_refs, v_refs, out_ref = refs[:total], refs[total : 2 * total], refs[-1]
-        q = q_ref[...]
-        row = lax.broadcasted_iota(jnp.int32, (CHUNK, CHUNK), 0)
-        col = lax.broadcasted_iota(jnp.int32, (CHUNK, CHUNK), 1)
-        scores = [dot_on(q, k_refs[j][...], ROW_BY_ROW) for j in range(total)]
-        scores[0] = jnp.where(col > row, scores[0], -jnp.inf)
-        scores[-1] = jnp.where(col <= row, scores[-1], -jnp.inf)
-        edge_on = flag[0] > 0
-
-        def rowmax(parts):
-            best = parts[0]
-            for part in parts[1:]:
-                best = jnp.maximum(best, part)
-            return jnp.max(best, axis=1, keepdims=True)
-
-        own_max = rowmax(scores[from_edge:])
-        both_max = jnp.maximum(own_max, rowmax(scores[:from_edge]))
-        largest = jnp.where(edge_on, both_max, own_max)
-        edge_largest = jnp.where(edge_on, both_max, jnp.inf)
-        weights = [
-            jnp.exp((scores[j] - (edge_largest if j < from_edge else largest)) * scale)
-            for j in range(total)
-        ]
-        together = weights[0]
-        for part in weights[1:]:
-            together = together + part
-        summed = jnp.sum(together, axis=1, keepdims=True)
-        mixed = dot(weights[0].astype(BF), v_refs[0][...])
-        for j in range(1, total):
-            mixed = mixed + dot(weights[j].astype(BF), v_refs[j][...])
-        out_ref[...] = mixed / summed
-
-    def spec(row):
-        return pl.BlockSpec((CHUNK, HEAD), lambda h, flag: (row, h))
-
-    rows = [spec(at + j) for j in range(from_edge)] + [spec(j) for j in range(at + 1)]
-    key_args = [edge_keys] * from_edge + [keys] * (at + 1)
-    value_args = [edge_values] * from_edge + [values] * (at + 1)
-    width = queries.shape[1]
+SPAN = WINDOW + CHUNK
+
+
+def scores_body(flag, q_ref, edge_ref, key_ref, out_ref, span, sems):
+    head, at = pl.program_id(0), pl.program_id(1)
+    heads = pl.num_programs(0)
+    tokens = key_ref.shape[0]
+
+    def copies(h):
+        column = pl.ds(pl.multiple_of(h * HEAD, HEAD), HEAD)
+        return (
+            pltpu.make_async_copy(
+                edge_ref.at[:, column], span.at[h, pl.ds(0, WINDOW)], sems.at[h, 0]
+            ),
+            pltpu.make_async_copy(
+                key_ref.at[:, column], span.at[h, pl.ds(WINDOW, tokens)], sems.at[h, 1]
+            ),
+        )
+
+    @pl.when((head == 0) & (at == 0))
+    def _():
+        for copy in copies(0):
+            copy.start()
+
+    @pl.when(at == 0)
+    def _():
+        for copy in copies(head):
+            copy.wait()
+
+    @pl.when((at == 0) & (head + 1 < heads))
+    def _():
+        for copy in copies(head + 1):
+            copy.start()
+
+    keys = span[head, pl.ds(pl.multiple_of(at * CHUNK, CHUNK), SPAN), :]
+    scores = dot_on(q_ref[...], keys, ROW_BY_ROW)
+    row = lax.broadcasted_iota(jnp.int32, scores.shape, 0)
+    col = lax.broadcasted_iota(jnp.int32, scores.shape, 1)
+    first = jnp.where(flag[0] > 0, 0, WINDOW - at * CHUNK)
+    allowed = (col > row) & (col <= row + WINDOW) & (col >= first)
+    scores = jnp.where(allowed, scores, -jnp.inf)
+    largest = jnp.max(scores, axis=1, keepdims=True)
+    exponent = jnp.exp((scores - largest) * (HEAD ** (-0.5)))
+    summed = jnp.sum(exponent, axis=1, keepdims=True)
+    out_ref[...] = (exponent * (1.0 / summed)).astype(BF)
+
+
+def probabilities(has_edge, queries, edge_keys, keys):
+    tokens, width = queries.shape
+    heads = width // HEAD
     return pl.pallas_call(
-        body,
-        out_shape=jax.ShapeDtypeStruct((CHUNK, width), F32),
+        scores_body,
+        out_shape=jax.ShapeDtypeStruct((tokens, heads * SPAN), BF),
         grid_spec=pltpu.PrefetchScalarGridSpec(
             num_scalar_prefetch=1,
-            grid=(width // HEAD,),
-            in_specs=[spec(at)] + rows + rows + [any_spec()] * len(after),
-            out_specs=pl.BlockSpec((CHUNK, HEAD), lambda h, flag: (0, h)),
-        ),
-        compiler_params=pltpu.CompilerParams(vmem_limit_bytes=32 * MIB),
-    )(has_edge, queries, *key_args, *value_args, *after)
-
-
-def tail_body(where, q0, q1, a0, a1, w0, w1, gain, s0, s1, o0, o1, send_ref, own_ref):
-    combined = []
-    for q_ref, a_ref, w_ref, head in ((q0, a0, w0, where[0]), (q1, a1, w1, 1 - where[0])):
+            grid=(heads, tokens // CHUNK),
+            in_specs=[
+                pl.BlockSpec((CHUNK, HEAD), lambda h, i, flag: (i, h)),
+                any_spec(),
+                any_spec(),
+            ],
+            out_specs=pl.BlockSpec((CHUNK, SPAN), lambda h, i, flag: (i, h)),
+            scratch_shapes=[
+                pltpu.VMEM((heads, WINDOW + tokens, HEAD), BF),
+                pltpu.SemaphoreType.DMA((heads, 2)),
+            ],
+        ),
+        compiler_params=pltpu.CompilerParams(
+            dimension_semantics=("arbitrary", "arbitrary"), vmem_limit_bytes=32 * MIB
+        ),
+        name="probabilities",
+    )(has_edge, queries, edge_keys, keys)
+
+
+PIECE = 2 * CHUNK
+
+
+def combined_piece(at, mirror, where, queries, probability, weights, gain, edge_values, values):
+    from_edge = WINDOW - at * PIECE
+    from_own = (at + 1) * PIECE
+
+    def head_of(w):
+        return 1 - w[0] if mirror else w[0]
+
+    def body(w, q_ref, p_ref, w_ref, gain_ref, edge_ref, value_ref, out_ref, span, sems):
+        head = head_of(w)
+        column = pl.ds(pl.multiple_of(head * HEAD, HEAD), HEAD)
+        copies = (
+            pltpu.make_async_copy(
+                edge_ref.at[pl.ds(at * PIECE, from_edge), column],
+                span.at[pl.ds(0, from_edge)],
+                sems.at[0],
+            ),
+            pltpu.make_async_copy(
+                value_ref.at[pl.ds(0, from_own), column],
+                span.at[pl.ds(from_edge, from_own)],
+                sems.at[1],
+            ),
+        )
+        for copy in copies:
+            copy.start()
         q = q_ref[...]
         gate = dot(q, w_ref[0:HEAD, :])
         lift = dot(q, w_ref[HEAD : 2 * HEAD, :])
         hidden = (gate * sigmoid(gate) * lift).astype(BF)
         out = dot(hidden, w_ref[2 * HEAD :, :])
         mean_square = jnp.mean(out * out, axis=1, keepdims=True)
-        scale = jnp.where(head == 0, gain[0:1, :], gain[1:2, :])
-        combined.append((a_ref[...] + out * lax.rsqrt(mean_square + EPSILON) * scale).astype(BF))
-    send_ref[...] = (dot(combined[0], s0[...]) + dot(combined[1], s1[...])).astype(BF)
-    own_ref[...] = dot(combined[0], o0[...]) + dot(combined[1], o1[...])
-
-
-def tail_chunk(at, where, queries, attended, mine, theirs, gain, out_weight):
-    columns = out_weight.shape[1] // 2
-    whole = pl.BlockSpec((3 * HEAD, HEAD), lambda i, w: (0, 0))
-
-    def token(row, mirror):
-        return pl.BlockSpec((CHUNK, HEAD), lambda i, w: (row, 1 - w[0] if mirror else w[0]))
-
-    def out_rows(mirror, send):
-        return pl.BlockSpec(
-            (HEAD, columns),
-            lambda i, w: (1 - w[0] if mirror else w[0], 1 - w[1] if send else w[1]),
-        )
-
-    block = pl.BlockSpec((CHUNK, columns), lambda i, w: (0, 0))
+        scale = jnp.where(head == 0, gain_ref[0:1, :], gain_ref[1:2, :])
+        normed = out * lax.rsqrt(mean_square + EPSILON) * scale
+        for copy in copies:
+            copy.wait()
+        for part in range(PIECE // CHUNK):
+            rows = slice(part * CHUNK, (part + 1) * CHUNK)
+            attended = dot(p_ref[rows, :], span[part * CHUNK : part * CHUNK + SPAN, :])
+            out_ref[rows, :] = (attended + normed[rows, :]).astype(BF)
+
     return pl.pallas_call(
-        tail_body,
-        out_shape=(
-            jax.ShapeDtypeStruct((CHUNK, columns), BF),
-            jax.ShapeDtypeStruct((CHUNK, columns), F32),
-        ),
+        body,
+        out_shape=jax.ShapeDtypeStruct((PIECE, HEAD), BF),
         grid_spec=pltpu.PrefetchScalarGridSpec(
             num_scalar_prefetch=1,
             grid=(1,),
             in_specs=[
-                token(at, False),
-                token(at, True),
-                token(0, False),
-                token(0, True),
-                whole,
-                whole,
+                pl.BlockSpec((PIECE, HEAD), lambda i, w: (at, head_of(w))),
+                pl.BlockSpec((PIECE, SPAN), lambda i, w: (at, head_of(w))),
+                pl.BlockSpec((3 * HEAD, HEAD), lambda i, w: (0, 0)),
                 pl.BlockSpec((2, HEAD), lambda i, w: (0, 0)),
-                out_rows(False, True),
-                out_rows(True, True),
-                out_rows(False, False),
-                out_rows(True, False),
-            ],
-            out_specs=[block, block],
-        ),
-        compiler_params=pltpu.CompilerParams(vmem_limit_bytes=40 * MIB),
-    )(
-        where,
-        queries,
-        queries,
-        attended,
-        attended,
-        mine,
-        theirs,
-        gain,
-        out_weight,
-        out_weight,
-        out_weight,
-        out_weight,
-    )
+                any_spec(),
+                any_spec(),
+            ],
+            out_specs=pl.BlockSpec((PIECE, HEAD), lambda i, w: (0, 0)),
+            scratch_shapes=[
+                pltpu.VMEM((WINDOW + PIECE, HEAD), BF),
+                pltpu.SemaphoreType.DMA((2,)),
+            ],
+        ),
+        compiler_params=pltpu.CompilerParams(vmem_limit_bytes=32 * MIB),
+    )(where, queries, probability, weights, gain, edge_values, values)
+
+
+def project_piece(where, combined, first_arrived, out_weight, other_weight):
+    columns = out_weight.shape[1] // 2
+    step = columns // 2
+
+    def body(w, a_ref, b_ref, c_ref, wa_ref, wb_ref, wc_ref, out_ref):
+        out_ref[...] = (
+            dot(a_ref[...], wa_ref[...]) + dot(b_ref[...], wb_ref[...]) + dot(c_ref[...], wc_ref[...])
+        )
+
+    rows = pl.BlockSpec((PIECE, HEAD), lambda i, w: (0, 0))
+    return pl.pallas_call(
+        body,
+        out_shape=jax.ShapeDtypeStruct((PIECE, columns), F32),
+        grid_spec=pltpu.PrefetchScalarGridSpec(
+            num_scalar_prefetch=1,
+            grid=(2,),
+            in_specs=[
+                rows,
+                rows,
+                rows,
+                pl.BlockSpec((HEAD, step), lambda i, w: (w[0], 2 * w[1] + i)),
+                pl.BlockSpec((HEAD, step), lambda i, w: (1 - w[0], 2 * w[1] + i)),
+                pl.BlockSpec((HEAD, step), lambda i, w: (w[0], i)),
+            ],
+            out_specs=pl.BlockSpec((PIECE, step), lambda i, w: (0, i)),
+        ),
+        compiler_params=pltpu.CompilerParams(vmem_limit_bytes=32 * MIB),
+        name="project",
+    )(where, *combined, first_arrived, out_weight, out_weight, other_weight)
+
+
+def finish_piece(at, tokens, where, partial, last_arrived, other_weight, before):
+    columns = partial.shape[1]
+    step = columns // 2
+
+    def body(w, acc_ref, a_ref, wa_ref, *refs):
+        refs[-1][...] = (acc_ref[...] + dot(a_ref[...], wa_ref[...])).astype(BF)
+
+    held = () if before is None else (before,)
+    return pl.pallas_call(
+        body,
+        out_shape=jax.ShapeDtypeStruct((tokens, columns), BF),
+        grid_spec=pltpu.PrefetchScalarGridSpec(
+            num_scalar_prefetch=1,
+            grid=(2,),
+            in_specs=[
+                pl.BlockSpec((PIECE, step), lambda i, w: (0, i)),
+                pl.BlockSpec((PIECE, HEAD), lambda i, w: (0, 0)),
+                pl.BlockSpec((HEAD, step), lambda i, w: (1 - w[0], i)),
+            ]
+            + [any_spec()] * len(held),
+            out_specs=pl.BlockSpec((PIECE, step), lambda i, w: (at, i)),
+        ),
+        compiler_params=pltpu.CompilerParams(vmem_limit_bytes=32 * MIB),
+        input_output_aliases={4: 0} if held else {},
+    )(where, partial, last_arrived, other_weight, *held)
 
 
 def partner(value, flip):
@@ -321,12 +390,21 @@
     memory_gain,
     out_weight,
 ):
-    queries, key_rows, value_rows, gate_fast, lift_fast, down_fast, out_weight = (
+    raw_out_weight = out_weight
+    queries, key_rows, value_rows, token_rates, gate_fast, lift_fast, down_fast, out_weight = (
         pltpu.with_memory_space_constraint(x, pltpu.HBM)
-        for x in (queries, key_rows, value_rows, gate_fast, lift_fast, down_fast, out_weight)
+        for x in (
+            queries,
+            key_rows,
+            value_rows,
+            token_rates,
+            gate_fast,
+            lift_fast,
+            down_fast,
+            out_weight,
+        )
     )
     tokens_here = queries.shape[0]
-    chunks = tokens_here // CHUNK
     seq = lax.axis_index("seq")
     core = (seq % 2).astype(jnp.int32)
     head = lax.axis_index("head").astype(jnp.int32)
@@ -356,23 +434,50 @@
     weights_mine = renewed_weights(where, grads, *fast)
     weights_theirs = partner(weights_mine, 1)
 
+    columns = out_weight.shape[1] // 2
+    pairs = [
+        (group * count + i, (1 - group) * count + (i ^ 2)) for group in range(2) for i in range(count)
+    ]
+    other_weight = lax.ppermute(
+        lax.dynamic_slice(
+            raw_out_weight, (0, (1 - head) * columns), (out_weight.shape[0], columns)
+        ),
+        ("head", "seq"),
+        pairs,
+    )
+
+    probability = probabilities(has_edge, queries, edge_keys, key_rows)
+
+    pieces = tokens_here // PIECE
     head_pair = [(0, 1), (1, 0)]
-    owns, arrivals = [], []
-    after = ()
-    for at in range(chunks):
-        attended = attention_chunk(
-            at, has_edge, queries, key_rows, value_rows, edge_keys, edge_values, after
+    made, arrived = {}, {}
+    for mirror, weights in ((False, weights_mine), (True, weights_theirs)):
+        for at in range(pieces):
+            piece = combined_piece(
+                at,
+                mirror,
+                where,
+                queries,
+                probability,
+                weights,
+                memory_gain,
+                edge_values,
+                value_rows,
+            )
+            made[mirror, at] = piece
+            arrived[mirror, at] = lax.ppermute(piece, "head", head_pair)
+    out = None
+    for at in range(pieces):
+        partial = project_piece(
+            where,
+            (made[False, at], made[True, at]),
+            arrived[False, at],
+            out_weight,
+            other_weight,
         )
-        send, own = tail_chunk(
-            at, where, queries, attended, weights_mine, weights_theirs, memory_gain, out_weight
+        out = finish_piece(
+            at, tokens_here, where, partial, arrived[True, at], other_weight, out
         )
-        owns.append(own)
-        arrivals.append(lax.ppermute(send, "head", head_pair))
-        after = (send,)
-    out = jnp.zeros((tokens_here, owns[0].shape[1]), BF)
-    for at in range(chunks):
-        rows = (owns[at] + arrivals[at].astype(F32)).astype(BF)
-        out = lax.dynamic_update_slice(out, rows, (at * CHUNK, 0))
     return out
 
 

time: 185 us -> 175 us (0.946)
  the two profiles are of different devices: /device:TPU:32 before, /device:TPU:0 now
where the time goes in v2:
time: 175 us; the launch traced here: 174 us
  Pallas kernels  69.4 us (40%)
  waiting for transfers between devices  45.2 us (26%)
  blocking collectives  31.3 us (18%)
  starting transfers between devices  22.7 us (13%)
  local copies, waits for them, and re-layouts  4.41 us (3%)
    ppermute x1, waiting for transfers between devices, shards(): lax.ppermute(lax.dynamic_slice(raw_out_weight, (0, (1 - head) * columns),...  32.3 us
    all_to_all x1, blocking collectives, over_planes(): lax.all_to_all(value, 'seq', 0, 0, tiled=True, axis_index_groups=groups)  31.3 us
    pallas_call x4, Pallas kernels, combined_piece(): pl.pallas_call(body, out_shape=jax.ShapeDtypeStruct((PIECE, HEAD), BF), g...  21.2 us
    pallas_call x2, Pallas kernels, head_grads(): pl.pallas_call(grads_body, out_shape=jax.ShapeDtypeStruct((3 * HEAD, HEAD...  15.6 us
    pallas_call x1, Pallas kernels, probabilities(): pl.pallas_call(scores_body, out_shape=jax.ShapeDtypeStruct((tokens, heads...  10.2 us
    all_to_all x1, waiting for transfers between devices, over_planes(): lax.all_to_all(value, 'seq', 0, 0, tiled=True, axis_index_groups=groups)  9.85 us
    pallas_call x1, Pallas kernels, renewed_weights(): pl.pallas_call(renew_body, out_shape=jax.ShapeDtypeStruct((3 * HEAD, HEAD...  9.63 us
    pallas_call x2, Pallas kernels, project_piece(): pl.pallas_call(body, out_shape=jax.ShapeDtypeStruct((PIECE, columns), F32...  7.8 us
  transfers between devices with their start and end apart: 11, of which 3 were waited for; matrix products, arithmetic and copies ran while one was open for 2% of the time, Pallas kernels for 34%

profile of v2, /device:TPU:0, one launch (start us, length us, event | category | flops | bytes accessed | tf_op | source)
XLA Modules:
  0.0 174.1 jit_solution(11047038577906394421)
XLA Ops:
  0.0 0.1 pad_add_fusion.1.where
  0.1 7.8 %head_grads.3 = bf16[1536,512]{1,0:T(8,128)(2,1)S(1)} custom-call(s32[2]{0:T(128)S(1)} %pad_add_fusion.1.where, bf16[1024,1024]{1,0:T(8,128)(2,1)} %k_ref.3, bf16[1024,1024]{1,0:T(8,128)(2,1)} %value_ref.7, f32[2,1024]{1,0:T(2,128)} %rate_ref.3, f32[2,512,512]{2,1,0:T(8,128)} %gate_ref.5, f32[2,512,512]{2,1,0:T(8,128)} %lift_ref.5, f32[2,512,512]{2,1,0:T(8,128)} %down_ref.5), custom_call_target="tpu_custom_call" | custom-call | tf_op jit(solution)/shard_map/head_grads/pallas_call | solution.py:87
  7.9 0.1 collective-permute-start.1
  8.0 0.1 pad_add_fusion.where.w
  8.0 7.8 %head_grads.2 = f32[1536,512]{1,0:T(8,128)S(1)} custom-call(s32[2]{0:T(128)S(1)} %pad_add_fusion.where.w, bf16[1024,1024]{1,0:T(8,128)(2,1)} %k_ref.3, bf16[1024,1024]{1,0:T(8,128)(2,1)} %value_ref.7, f32[2,1024]{1,0:T(2,128)} %rate_ref.3, f32[2,512,512]{2,1,0:T(8,128)} %gate_ref.5, f32[2,512,512]{2,1,0:T(8,128)} %lift_ref.5, f32[2,512,512]{2,1,0:T(8,128)} %down_ref.5), custom_call_target="tpu_custom_call" | custom-call | tf_op jit(solution)/shard_map/head_grads/pallas_call | solution.py:87
  15.9 0.0 collective-permute-done.1
  15.9 0.5 add_convert_fusion
  16.4 31.3 %all_to_all.10 = bf16[16,96,512]{2,1,0:T(8,128)(2,1)S(1)} all-to-all(bf16[16,96,512]{2,1,0:T(8,128)(2,1)S(1)} %bitcast.6), channel_id=1, replica_groups={{0,4,8,12,16,20,24,28,32,36,40,44,48,52,56,60},{1,5,9,13,17,21,25,29,33..., dimensions={0} | all-to-all | bytes 3145728 | tf_op jit(solution)/shard_map/all_to_all | solution.py:379
  47.7 0.2 reduce_sum.12
  48.0 1.7 collective-permute-start.2
  49.6 3.0 %collective-permute-done.2 = bf16[96,512]{1,0:T(8,128)(2,1)S(1)} collective-permute-done((bf16[96,512]{1,0:T(8,128)(2,1)S(1)}, bf16[96,512]{1,0:T(8,128)(2,1)S(1)}, u32[]{:S(2)}, u32[]{:S(2)}) %collective-permute-start.2) | collective-permute-done | bytes 98336 | tf_op jit(solution)/shard_map/ppermute | solution.py:374
  52.7 1.3 broadcast_in_dim.2
  54.0 4.4 %all-to-all-start.1 = ((bf16[16,96,512]{2,1,0:T(8,128)(2,1)}), bf16[16,96,512]{2,1,0:T(8,128)(2,1)}, u32[]{:S(2)}, u32[]{:S(2)}) async-start(bf16[16,96,512]{2,1,0:T(8,128)(2,1)} %broadcast_in_dim.2), calls=%async_computation.1 | async-start | bytes 3145728 | tf_op jit(solution)/shard_map/all_to_all | solution.py:379
  58.4 2.6 %collective-permute-start = (bf16[1024,1024]{1,0:T(8,128)(2,1)}, bf16[1024,1024]{1,0:T(8,128)(2,1)}, u32[]{:S(2)}, u32[]{:S(2)}) collective-permute-start(bf16[1024,1024]{1,0:T(8,128)(2,1)} %k_ref.3), channel_id=1, source_target_pairs={{0,1},{1,2},{2,3},{3,4},{4,5},{5,6},{6,7},{7,8},{8,9},{9,10},{10,1... | collective-permute-start | bytes 6291464 | tf_op jit(solution)/shard_map/ppermute | solution.py:423
  61.0 4.2 %collective-permute-start.3 = (bf16[1024,1024]{1,0:T(8,128)(2,1)}, bf16[1024,1024]{1,0:T(8,128)(2,1)}, u32[]{:S(2)}, u32[]{:S(2)}) collective-permute-start(bf16[1024,1024]{1,0:T(8,128)(2,1)} %value_ref.7), channel_id=1, source_target_pairs={{0,1},{1,2},{2,3},{3,4},{4,5},{5,6},{6,7},{7,8},{8,9},{9,10},{10,1... | collective-permute-start | bytes 6291464 | tf_op jit(solution)/shard_map/ppermute | solution.py:424
  65.3 3.1 %constant_dynamic-slice_fusion = bf16[1024,1024]{1,0:T(8,128)(2,1)} fusion(bf16[1024,2048]{1,0:T(8,128)(2,1)} %wb_ref.3, s32[]{:T(128)S(6)} %select_n.16), kind=kLoop, calls=%fused_computation.4 | loop fusion | bytes 4194308 | tf_op jit(solution)/shard_map/dynamic_slice | solution.py:442
  68.3 2.0 %collective-permute-start.6 = (bf16[1024,1024]{1,0:T(8,128)(2,1)}, bf16[1024,1024]{1,0:T(8,128)(2,1)S(1)}, u32[]{:S(2)}, u32[]{:S(2)}) collective-permute-start(bf16[1024,1024]{1,0:T(8,128)(2,1)} %constant_dynamic-slice_fusion), channel_id=1, source_target_pairs={{0,66},{1,67},{2,64},{3,65},{4,70},{5,71},{6,68},{7,69},{8,74},{9,... | collective-permute-start | bytes 6291464 | tf_op jit(solution)/shard_map/ppermute | solution.py:441
  70.4 9.8 %all-to-all-done.1 = bf16[16,96,512]{2,1,0:T(8,128)(2,1)} async-done(((bf16[16,96,512]{2,1,0:T(8,128)(2,1)}), bf16[16,96,512]{2,1,0:T(8,128)(2,1)}, u32[]{:S(2)}, u32[]{:S(2)}) %all-to-all-start.1) | async-done | bytes 1572896 | tf_op jit(solution)/shard_map/all_to_all | solution.py:379
  80.2 9.6 %renewed_weights.1.w_ref = bf16[1536,512]{1,0:T(8,128)(2,1)} custom-call(s32[2]{0:T(128)S(1)} %pad_add_fusion.where.w, bf16[1536,512]{1,0:T(8,128)(2,1)} %bitcast.5.g_ref, f32[2,512,512]{2,1,0:T(8,128)} %gate_ref.5, f32[2,512,512]{2,1,0:T(8,128)} %lift_ref.5, f32[2,512,512]{2,1,0:T(8,128)} %down_ref.5), custom_call_target="tpu_custom_call" | custom-call | tf_op jit(solution)/shard_map/renewed_weights/pallas_call | solution.py:159
  89.9 0.1 collective-permute-start.4
  90.0 0.0 collective-permute-done.edge_ref
  90.0 0.0 copy-start
  90.0 10.2 %probabilities.1.p_ref = bf16[1024,2560]{1,0:T(8,128)(2,1)S(1)} custom-call(s32[1]{0:T(128)} %bitcast.2.flag, bf16[1024,1024]{1,0:T(8,128)(2,1)} %q_ref.9, bf16[1024,1024]{1,0:T(8,128)(2,1)} %collective-permute-done.edge_ref, bf16[1024,1024]{1,0:T(8,128)(2,1)} %k_ref.3), custom_call_target="tpu_custom_call" | custom-call | tf_op jit(solution)/shard_map/probabilities/pallas_call | solution.py:224
  100.2 0.0 collective-permute-done.3.edge_ref
  100.2 0.0 copy-done
  100.2 5.3 %shard_map.91.a_ref = bf16[512,512]{1,0:T(8,128)(2,1)S(1)} custom-call(s32[2]{0:T(128)S(1)} %pad_add_fusion.where.w, bf16[1024,1024]{1,0:T(8,128)(2,1)} %q_ref.9, bf16[1024,2560]{1,0:T(8,128)(2,1)S(1)} %probabilities.1.p_ref, bf16[1536,512]{1,0:T(8,128)(2,1)} %renewed_weights.1.w_ref, f32[2,512]{1,0:T(2,128)S(1)} %copy-done, ...), custom_call_target="tpu_custom_call" | custom-call | tf_op jit(solution)/shard_map/pallas_call | solution.py:290
  105.6 3.3 %collective-permute-start.5 = (bf16[512,512]{1,0:T(8,128)(2,1)S(1)}, bf16[512,512]{1,0:T(8,128)(2,1)S(1)}, u32[]{:S(2)}, u32[]{:S(2)}) collective-permute-start(bf16[512,512]{1,0:T(8,128)(2,1)S(1)} %shard_map.91.a_ref), channel_id=1, source_target_pairs={{0,64},{64,0},{1,65},{65,1},{2,66},{66,2},{3,67},{67,3},{4,68},{68... | collective-permute-start | bytes 1572872 | tf_op jit(solution)/shard_map/ppermute | solution.py:468
  108.8 5.3 %shard_map.93.a_ref = bf16[512,512]{1,0:T(8,128)(2,1)S(1)} custom-call(s32[2]{0:T(128)S(1)} %pad_add_fusion.where.w, bf16[1024,1024]{1,0:T(8,128)(2,1)} %q_ref.9, bf16[1024,2560]{1,0:T(8,128)(2,1)S(1)} %probabilities.1.p_ref, bf16[1536,512]{1,0:T(8,128)(2,1)} %renewed_weights.1.w_ref, f32[2,512]{1,0:T(2,128)S(1)} %copy-done, ...), custom_call_target="tpu_custom_call" | custom-call | tf_op jit(solution)/shard_map/pallas_call | solution.py:290
  114.1 0.4 collective-permute-start.8
  114.5 0.0 collective-permute-done.4.w_ref
  114.5 5.3 %shard_map.94.b_ref = bf16[512,512]{1,0:T(8,128)(2,1)S(1)} custom-call(s32[2]{0:T(128)S(1)} %pad_add_fusion.where.w, bf16[1024,1024]{1,0:T(8,128)(2,1)} %q_ref.9, bf16[1024,2560]{1,0:T(8,128)(2,1)S(1)} %probabilities.1.p_ref, bf16[1536,512]{1,0:T(8,128)(2,1)} %collective-permute-done.4.w_ref, f32[2,512]{1,0:T(2,128)S(1)} %copy-done, ...), custom_call_target="tpu_custom_call" | custom-call | tf_op jit(solution)/shard_map/pallas_call | solution.py:290
  119.8 3.5 %collective-permute-start.9 = (bf16[512,512]{1,0:T(8,128)(2,1)S(1)}, bf16[512,512]{1,0:T(8,128)(2,1)S(1)}, u32[]{:S(2)}, u32[]{:S(2)}) collective-permute-start(bf16[512,512]{1,0:T(8,128)(2,1)S(1)} %shard_map.94.b_ref), channel_id=1, source_target_pairs={{0,64},{64,0},{1,65},{65,1},{2,66},{66,2},{3,67},{67,3},{4,68},{68... | collective-permute-start | bytes 1572872 | tf_op jit(solution)/shard_map/ppermute | solution.py:468
  123.3 5.3 %shard_map.92.b_ref = bf16[512,512]{1,0:T(8,128)(2,1)S(1)} custom-call(s32[2]{0:T(128)S(1)} %pad_add_fusion.where.w, bf16[1024,1024]{1,0:T(8,128)(2,1)} %q_ref.9, bf16[1024,2560]{1,0:T(8,128)(2,1)S(1)} %probabilities.1.p_ref, bf16[1536,512]{1,0:T(8,128)(2,1)} %collective-permute-done.4.w_ref, f32[2,512]{1,0:T(2,128)S(1)} %copy-done, ...), custom_call_target="tpu_custom_call" | custom-call | tf_op jit(solution)/shard_map/pallas_call | solution.py:290
  128.7 0.4 collective-permute-start.7
  129.1 32.3 %collective-permute-done.6.wc_ref.wa_ref = bf16[1024,1024]{1,0:T(8,128)(2,1)S(1)} collective-permute-done((bf16[1024,1024]{1,0:T(8,128)(2,1)}, bf16[1024,1024]{1,0:T(8,128)(2,1)S(1)}, u32[]{:S(2)}, u32[]{:S(2)}) %collective-permute-start.6) | collective-permute-done | bytes 2097184 | tf_op jit(solution)/shard_map/ppermute | solution.py:441
  161.3 0.0 collective-permute-done.5.c_ref
  161.3 3.9 %project.2.acc_ref = f32[512,1024]{1,0:T(8,128)S(1)} custom-call(s32[2]{0:T(128)S(1)} %pad_add_fusion.where.w, bf16[512,512]{1,0:T(8,128)(2,1)S(1)} %shard_map.91.a_ref, bf16[512,512]{1,0:T(8,128)(2,1)S(1)} %shard_map.92.b_ref, bf16[512,512]{1,0:T(8,128)(2,1)S(1)} %collective-permute-done.5.c_ref, bf16[1024,2048]{1,0:T(8,128)(2,1)} %wb_ref.3, ...), custom_call_target="tpu_custom_call" | custom-call | tf_op jit(solution)/shard_map/project/pallas_call | solution.py:324
  165.3 0.0 collective-permute-done.8.c_ref
  165.3 3.9 %project.3.acc_ref = f32[512,1024]{1,0:T(8,128)S(1)} custom-call(s32[2]{0:T(128)S(1)} %pad_add_fusion.where.w, bf16[512,512]{1,0:T(8,128)(2,1)S(1)} %shard_map.93.a_ref, bf16[512,512]{1,0:T(8,128)(2,1)S(1)} %shard_map.94.b_ref, bf16[512,512]{1,0:T(8,128)(2,1)S(1)} %collective-permute-done.8.c_ref, bf16[1024,2048]{1,0:T(8,128)(2,1)} %wb_ref.3, ...), custom_call_target="tpu_custom_call" | custom-call | tf_op jit(solution)/shard_map/project/pallas_call | solution.py:324
  169.2 0.0 collective-permute-done.9.a_ref
  169.2 2.5 %shard_map.95.refs_0_ = bf16[1024,1024]{1,0:T(8,128)(2,1)} custom-call(s32[2]{0:T(128)S(1)} %pad_add_fusion.where.w, f32[512,1024]{1,0:T(8,128)S(1)} %project.3.acc_ref, bf16[512,512]{1,0:T(8,128)(2,1)S(1)} %collective-permute-done.9.a_ref, bf16[1024,1024]{1,0:T(8,128)(2,1)S(1)} %collective-permute-done.6.wc_ref.wa_ref), custom_call_target="tpu_custom_call" | custom-call | tf_op jit(solution)/shard_map/pallas_call | solution.py:353
  171.7 0.0 collective-permute-done.7.a_ref
  171.7 2.5 %shard_map.96 = bf16[1024,1024]{1,0:T(8,128)(2,1)} custom-call(s32[2]{0:T(128)S(1)} %pad_add_fusion.where.w, f32[512,1024]{1,0:T(8,128)S(1)} %project.2.acc_ref, bf16[512,512]{1,0:T(8,128)(2,1)S(1)} %collective-permute-done.7.a_ref, bf16[1024,1024]{1,0:T(8,128)(2,1)S(1)} %collective-permute-done.6.wc_ref.wa_ref, ...), custom_call_target="tpu_custom_call", output_to_operand_aliasing={{}: (4, {})} | custom-call | tf_op jit(solution)/shard_map/pallas_call | solution.py:353
  (1 shorter events, 0.0 us)
Async XLA Ops:
  7.9 8.0 %collective-permute-start.1 = (bf16[1536,512]{1,0:T(8,128)(2,1)S(1)}, bf16[1536,512]{1,0:T(8,128)(2,1)S(1)}, u32[]{:S(2)}, u32[]{:S(2)}) collective-permute-start(bf16[1536,512]{1,0:T(8,128)(2,1)S(1)} %head_grads.3), channel_id=1, source_target_pairs={{0,1},{1,0},{2,3},{3,2},{4,5},{5,4},{6,7},{7,6},{8,9},{9,8},{10,11... | collective-permute-start | bytes 4718600 | tf_op jit(solution)/shard_map/ppermute | solution.py:374
  48.0 4.7 %collective-permute-start.2 = (bf16[96,512]{1,0:T(8,128)(2,1)S(1)}, bf16[96,512]{1,0:T(8,128)(2,1)S(1)}, u32[]{:S(2)}, u32[]{:S(2)}) collective-permute-start(bf16[96,512]{1,0:T(8,128)(2,1)S(1)} %reduce_sum.12), channel_id=1, source_target_pairs={{0,2},{1,3},{2,0},{3,1},{4,6},{5,7},{6,4},{7,5},{8,10},{9,11},{10,... | collective-permute-start | bytes 294920 | tf_op jit(solution)/shard_map/ppermute | solution.py:374
  54.0 26.2 %all-to-all-start.1 = ((bf16[16,96,512]{2,1,0:T(8,128)(2,1)}), bf16[16,96,512]{2,1,0:T(8,128)(2,1)}, u32[]{:S(2)}, u32[]{:S(2)}) async-start(bf16[16,96,512]{2,1,0:T(8,128)(2,1)} %broadcast_in_dim.2), calls=%async_computation.1 | async-start | bytes 3145728 | tf_op jit(solution)/shard_map/all_to_all | solution.py:379
  58.4 31.6 %collective-permute-start = (bf16[1024,1024]{1,0:T(8,128)(2,1)}, bf16[1024,1024]{1,0:T(8,128)(2,1)}, u32[]{:S(2)}, u32[]{:S(2)}) collective-permute-start(bf16[1024,1024]{1,0:T(8,128)(2,1)} %k_ref.3), channel_id=1, source_target_pairs={{0,1},{1,2},{2,3},{3,4},{4,5},{5,6},{6,7},{7,8},{8,9},{9,10},{10,1... | collective-permute-start | bytes 6291464 | tf_op jit(solution)/shard_map/ppermute | solution.py:423
  61.0 39.2 %collective-permute-start.3 = (bf16[1024,1024]{1,0:T(8,128)(2,1)}, bf16[1024,1024]{1,0:T(8,128)(2,1)}, u32[]{:S(2)}, u32[]{:S(2)}) collective-permute-start(bf16[1024,1024]{1,0:T(8,128)(2,1)} %value_ref.7), channel_id=1, source_target_pairs={{0,1},{1,2},{2,3},{3,4},{4,5},{5,6},{6,7},{7,8},{8,9},{9,10},{10,1... | collective-permute-start | bytes 6291464 | tf_op jit(solution)/shard_map/ppermute | solution.py:424
  68.3 93.0 %collective-permute-start.6 = (bf16[1024,1024]{1,0:T(8,128)(2,1)}, bf16[1024,1024]{1,0:T(8,128)(2,1)S(1)}, u32[]{:S(2)}, u32[]{:S(2)}) collective-permute-start(bf16[1024,1024]{1,0:T(8,128)(2,1)} %constant_dynamic-slice_fusion), channel_id=1, source_target_pairs={{0,66},{1,67},{2,64},{3,65},{4,70},{5,71},{6,68},{7,69},{8,74},{9,... | collective-permute-start | bytes 6291464 | tf_op jit(solution)/shard_map/ppermute | solution.py:441
  89.9 24.7 %collective-permute-start.4 = (bf16[1536,512]{1,0:T(8,128)(2,1)}, bf16[1536,512]{1,0:T(8,128)(2,1)}, u32[]{:S(2)}, u32[]{:S(2)}) collective-permute-start(bf16[1536,512]{1,0:T(8,128)(2,1)} %renewed_weights.1.w_ref), channel_id=1, source_target_pairs={{0,1},{1,0},{2,3},{3,2},{4,5},{5,4},{6,7},{7,6},{8,9},{9,8},{10,11... | collective-permute-start | bytes 4718600 | tf_op jit(solution)/shard_map/ppermute | solution.py:374
  90.0 10.2 %copy-start = (f32[2,512]{1,0:T(2,128)S(1)}, f32[2,512]{1,0:T(2,128)}, u32[]{:S(2)}) copy-start(f32[2,512]{1,0:T(2,128)} %gain_ref.7) | copy-start | bytes 12292
  105.6 55.8 %collective-permute-start.5 = (bf16[512,512]{1,0:T(8,128)(2,1)S(1)}, bf16[512,512]{1,0:T(8,128)(2,1)S(1)}, u32[]{:S(2)}, u32[]{:S(2)}) collective-permute-start(bf16[512,512]{1,0:T(8,128)(2,1)S(1)} %shard_map.91.a_ref), channel_id=1, source_target_pairs={{0,64},{64,0},{1,65},{65,1},{2,66},{66,2},{3,67},{67,3},{4,68},{68... | collective-permute-start | bytes 1572872 | tf_op jit(solution)/shard_map/ppermute | solution.py:468
  114.1 51.1 %collective-permute-start.8 = (bf16[512,512]{1,0:T(8,128)(2,1)S(1)}, bf16[512,512]{1,0:T(8,128)(2,1)S(1)}, u32[]{:S(2)}, u32[]{:S(2)}) collective-permute-start(bf16[512,512]{1,0:T(8,128)(2,1)S(1)} %shard_map.93.a_ref), channel_id=1, source_target_pairs={{0,64},{64,0},{1,65},{65,1},{2,66},{66,2},{3,67},{67,3},{4,68},{68... | collective-permute-start | bytes 1572872 | tf_op jit(solution)/shard_map/ppermute | solution.py:468
  119.8 49.3 %collective-permute-start.9 = (bf16[512,512]{1,0:T(8,128)(2,1)S(1)}, bf16[512,512]{1,0:T(8,128)(2,1)S(1)}, u32[]{:S(2)}, u32[]{:S(2)}) collective-permute-start(bf16[512,512]{1,0:T(8,128)(2,1)S(1)} %shard_map.94.b_ref), channel_id=1, source_target_pairs={{0,64},{64,0},{1,65},{65,1},{2,66},{66,2},{3,67},{67,3},{4,68},{68... | collective-permute-start | bytes 1572872 | tf_op jit(solution)/shard_map/ppermute | solution.py:468
  128.7 43.0 %collective-permute-start.7 = (bf16[512,512]{1,0:T(8,128)(2,1)S(1)}, bf16[512,512]{1,0:T(8,128)(2,1)S(1)}, u32[]{:S(2)}, u32[]{:S(2)}) collective-permute-start(bf16[512,512]{1,0:T(8,128)(2,1)S(1)} %shard_map.92.b_ref), channel_id=1, source_target_pairs={{0,64},{64,0},{1,65},{65,1},{2,66},{66,2},{3,67},{67,3},{4,68},{68... | collective-permute-start | bytes 1572872 | tf_op jit(solution)/shard_map/ppermute | solution.py:468

commit v3 on v2

--- a/solution.py
+++ b/solution.py
@@ -42,72 +42,102 @@
     return 0.5 * jnp.tanh(0.5 * x) + 0.5
 
 
-def grads_body(where, k_ref, v_ref, rate_ref, gate_ref, lift_ref, down_ref, out_ref, acc, w16, back):
-    step = pl.program_id(0)
-
-    @pl.when(step == 0)
-    def _():
-        w16[:, :HEAD] = gate_ref[0].astype(BF)
-        w16[:, HEAD : 2 * HEAD] = lift_ref[0].astype(BF)
-        w16[:, 2 * HEAD :] = down_ref[0].astype(BF)
-
-    keys = k_ref[...]
-    rates = jnp.where(where[0] == 0, rate_ref[0:1, :], rate_ref[1:2, :])
-    rate_col = jnp.broadcast_to(rates, (128, rates.shape[1])).T[:, :1]
-    target = (-rate_col * v_ref[...].astype(F32)).astype(BF)
-    gate_pre = dot(keys, w16[:, :HEAD])
-    lift_pre = dot(keys, w16[:, HEAD : 2 * HEAD])
-    back_hidden = dot_on(target, w16[:, 2 * HEAD :], ROW_BY_ROW)
-    sig = sigmoid(gate_pre)
-    activated = gate_pre * sig
-    hidden = (activated * lift_pre).astype(BF)
-    back[:, :HEAD] = (back_hidden * lift_pre * (sig + activated * (1.0 - sig))).astype(BF)
-    back[:, HEAD:] = (back_hidden * activated).astype(BF)
-    into = dot_on(keys, back[...], COL_BY_COL)
-    down = dot_on(hidden, target, COL_BY_COL)
-
-    @pl.when(step == 0)
-    def _():
-        acc[:, : 2 * HEAD] = into
-        acc[:, 2 * HEAD :] = down
-
-    @pl.when(step == pl.num_programs(0) - 1)
-    def _():
-        total_into = acc[:, : 2 * HEAD] + into
-        total_down = acc[:, 2 * HEAD :] + down
-        out_ref[:HEAD, :] = total_into[:, :HEAD].astype(out_ref.dtype)
-        out_ref[HEAD : 2 * HEAD, :] = total_into[:, HEAD:].astype(out_ref.dtype)
-        out_ref[2 * HEAD :, :] = total_down.astype(out_ref.dtype)
+def vmem_spec():
+    return pl.BlockSpec(memory_space=pltpu.VMEM)
+
+
+def grads_body(where, k_hbm, v_hbm, rate_ref, gate_hbm, lift_hbm, down_hbm, out_ref, k_ref, v_ref, fast, sems):
+    head = where[0]
+    tokens = k_ref.shape[0]
+    half = tokens // 2
+    column = pl.ds(pl.multiple_of(head * HEAD, HEAD), HEAD)
+    moves = []
+
+    def fetch(source, target):
+        copy = pltpu.make_async_copy(source, target, sems.at[len(moves)])
+        copy.start()
+        moves.append(copy)
+        return copy
+
+    def rows_of(n):
+        return pl.ds(n * half, half)
+
+    waits = {
+        "k0": fetch(k_hbm.at[rows_of(0), column], k_ref.at[rows_of(0)]),
+        "gate": fetch(gate_hbm.at[head], fast.at[0]),
+        "lift": fetch(lift_hbm.at[head], fast.at[1]),
+        "v0": fetch(v_hbm.at[rows_of(0), column], v_ref.at[rows_of(0)]),
+        "down": fetch(down_hbm.at[head], fast.at[2]),
+        "k1": fetch(k_hbm.at[rows_of(1), column], k_ref.at[rows_of(1)]),
+        "v1": fetch(v_hbm.at[rows_of(1), column], v_ref.at[rows_of(1)]),
+    }
+    rates = jnp.where(head == 0, rate_ref[0:1, :], rate_ref[1:2, :])
+    rate_col = jnp.broadcast_to(rates, (128, tokens)).T[:, :1]
+    waits["k0"].wait()
+    waits["gate"].wait()
+    gate = fast[0].astype(BF)
+    into_gate = into_lift = down_sum = None
+    lift = down = None
+    for n in range(2):
+        rows = slice(n * half, (n + 1) * half)
+        if n:
+            waits["k1"].wait()
+        keys = k_ref[rows, :]
+        gate_pre = dot(keys, gate)
+        sig = sigmoid(gate_pre)
+        activated = gate_pre * sig
+        slope = sig + activated * (1.0 - sig)
+        if lift is None:
+            waits["lift"].wait()
+            lift = fast[1].astype(BF)
+        lift_pre = dot(keys, lift)
+        hidden = (activated * lift_pre).astype(BF)
+        slope = lift_pre * slope
+        waits["v1" if n else "v0"].wait()
+        target = (-rate_col[rows, :] * v_ref[rows, :].astype(F32)).astype(BF)
+        if down is None:
+            waits["down"].wait()
+            down = fast[2].astype(BF)
+        back_hidden = dot_on(target, down, ROW_BY_ROW)
+        back_gate = (back_hidden * slope).astype(BF)
+        back_lift = (back_hidden * activated).astype(BF)
+        parts = (
+            dot_on(keys, back_gate, COL_BY_COL),
+            dot_on(keys, back_lift, COL_BY_COL),
+            dot_on(hidden, target, COL_BY_COL),
+        )
+        if n == 0:
+            into_gate, into_lift, down_sum = parts
+        else:
+            for m, (first, second) in enumerate(zip((into_gate, into_lift, down_sum), parts)):
+                out_ref[m * HEAD : (m + 1) * HEAD, :] = (first + second).astype(out_ref.dtype)
 
 
 def head_grads(which, keys, values, rates, gate, lift, down, dtype):
-    rows = keys.shape[0] // 2
-    weight = pl.BlockSpec((1, HEAD, HEAD), lambda i, w: (w[0], 0, 0))
-    token = pl.BlockSpec((rows, HEAD), lambda i, w: (i, w[0]))
+    tokens = keys.shape[0]
     return pl.pallas_call(
         grads_body,
         out_shape=jax.ShapeDtypeStruct((3 * HEAD, HEAD), dtype),
         grid_spec=pltpu.PrefetchScalarGridSpec(
             num_scalar_prefetch=1,
-            grid=(2,),
+            grid=(1,),
             in_specs=[
-                token,
-                token,
-                pl.BlockSpec((2, rows), lambda i, w: (0, i)),
-                weight,
-                weight,
-                weight,
+                any_spec(),
+                any_spec(),
+                pl.BlockSpec((2, tokens), lambda i, w: (0, 0)),
+                any_spec(),
+                any_spec(),
+                any_spec(),
             ],
-            out_specs=pl.BlockSpec((3 * HEAD, HEAD), lambda i, w: (0, 0)),
+            out_specs=vmem_spec(),
             scratch_shapes=[
-                pltpu.VMEM((HEAD, 3 * HEAD), F32),
-                pltpu.VMEM((HEAD, 3 * HEAD), BF),
-                pltpu.VMEM((rows, 2 * HEAD), BF),
+                pltpu.VMEM((tokens, HEAD), BF),
+                pltpu.VMEM((tokens, HEAD), BF),
+                pltpu.VMEM((3, HEAD, HEAD), F32),
+                pltpu.SemaphoreType.DMA((7,)),
             ],
         ),
-        compiler_params=pltpu.CompilerParams(
-            dimension_semantics=("arbitrary",), vmem_limit_bytes=40 * MIB
-        ),
+        compiler_params=pltpu.CompilerParams(vmem_limit_bytes=30 * MIB),
         name="head_grads",
     )(which, keys, values, rates, gate, lift, down)
 
@@ -155,18 +185,17 @@
 
 
 def renewed_weights(which, grads, gate, lift, down):
-    whole = pl.BlockSpec((3 * HEAD, HEAD), lambda i, w: (0, 0))
     return pl.pallas_call(
         renew_body,
         out_shape=jax.ShapeDtypeStruct((3 * HEAD, HEAD), BF),
         grid_spec=pltpu.PrefetchScalarGridSpec(
             num_scalar_prefetch=1,
             grid=(1,),
-            in_specs=[whole, any_spec(), any_spec(), any_spec()],
-            out_specs=whole,
+            in_specs=[vmem_spec(), any_spec(), any_spec(), any_spec()],
+            out_specs=vmem_spec(),
             scratch_shapes=[pltpu.VMEM((3, HEAD, HEAD), F32), pltpu.SemaphoreType.DMA((3,))],
         ),
-        compiler_params=pltpu.CompilerParams(vmem_limit_bytes=48 * MIB),
+        compiler_params=pltpu.CompilerParams(vmem_limit_bytes=24 * MIB),
         name="renewed_weights",
     )(which, grads, gate, lift, down)
 
@@ -239,7 +268,7 @@
             ],
         ),
         compiler_params=pltpu.CompilerParams(
-            dimension_semantics=("arbitrary", "arbitrary"), vmem_limit_bytes=32 * MIB
+            dimension_semantics=("arbitrary", "arbitrary"), vmem_limit_bytes=24 * MIB
         ),
         name="probabilities",
     )(has_edge, queries, edge_keys, keys)
@@ -248,30 +277,36 @@
 PIECE = 2 * CHUNK
 
 
-def combined_piece(at, mirror, where, queries, probability, weights, gain, edge_values, values):
-    from_edge = WINDOW - at * PIECE
+def combined_piece(at, mirror, where, queries, probability, weights, gain, edges, values, after):
+    from_edge = sum(edge.shape[0] for edge in edges)
     from_own = (at + 1) * PIECE
 
     def head_of(w):
         return 1 - w[0] if mirror else w[0]
 
-    def body(w, q_ref, p_ref, w_ref, gain_ref, edge_ref, value_ref, out_ref, span, sems):
+    def body(w, q_hbm, p_hbm, w_ref, gain_ref, value_hbm, *refs):
+        edge_hbm, (out_ref, q_ref, p_ref, span, sems) = refs[: len(edges)], refs[-5:]
         head = head_of(w)
         column = pl.ds(pl.multiple_of(head * HEAD, HEAD), HEAD)
-        copies = (
-            pltpu.make_async_copy(
-                edge_ref.at[pl.ds(at * PIECE, from_edge), column],
-                span.at[pl.ds(0, from_edge)],
-                sems.at[0],
-            ),
-            pltpu.make_async_copy(
-                value_ref.at[pl.ds(0, from_own), column],
-                span.at[pl.ds(from_edge, from_own)],
-                sems.at[1],
-            ),
-        )
+        chances = pl.ds(pl.multiple_of(head * SPAN, SPAN), SPAN)
+        rows = pl.ds(at * PIECE, PIECE)
+        moves = [
+            (q_hbm.at[rows, column], q_ref),
+            (p_hbm.at[rows, chances], p_ref),
+            (value_hbm.at[pl.ds(0, from_own), column], span.at[pl.ds(from_edge, from_own)]),
+        ]
+        start = 0
+        for edge in edge_hbm:
+            count = edge.shape[0]
+            moves.append((edge.at[:, column], span.at[pl.ds(start, count)]))
+            start += count
+        copies = [
+            pltpu.make_async_copy(source, target, sems.at[n])
+            for n, (source, target) in enumerate(moves)
+        ]
         for copy in copies:
             copy.start()
+        copies[0].wait()
         q = q_ref[...]
         gate = dot(q, w_ref[0:HEAD, :])
         lift = dot(q, w_ref[HEAD : 2 * HEAD, :])
@@ -280,7 +315,7 @@
         mean_square = jnp.mean(out * out, axis=1, keepdims=True)
         scale = jnp.where(head == 0, gain_ref[0:1, :], gain_ref[1:2, :])
         normed = out * lax.rsqrt(mean_square + EPSILON) * scale
-        for copy in copies:
+        for copy in copies[1:]:
             copy.wait()
         for part in range(PIECE // CHUNK):
             rows = slice(part * CHUNK, (part + 1) * CHUNK)
@@ -293,22 +328,18 @@
         grid_spec=pltpu.PrefetchScalarGridSpec(
             num_scalar_prefetch=1,
             grid=(1,),
-            in_specs=[
-                pl.BlockSpec((PIECE, HEAD), lambda i, w: (at, head_of(w))),
-                pl.BlockSpec((PIECE, SPAN), lambda i, w: (at, head_of(w))),
-                pl.BlockSpec((3 * HEAD, HEAD), lambda i, w: (0, 0)),
-                pl.BlockSpec((2, HEAD), lambda i, w: (0, 0)),
-                any_spec(),
-                any_spec(),
+            in_specs=[any_spec(), any_spec(), vmem_spec(), vmem_spec(), any_spec()]
+            + [any_spec()] * (len(edges) + len(after)),
+            out_specs=vmem_spec(),
+            scratch_shapes=[
+                pltpu.VMEM((PIECE, HEAD), BF),
+                pltpu.VMEM((PIECE, SPAN), BF),
+                pltpu.VMEM((WINDOW + PIECE, HEAD), BF),
+                pltpu.SemaphoreType.DMA((3 + len(edges),)),
             ],
-            out_specs=pl.BlockSpec((PIECE, HEAD), lambda i, w: (0, 0)),
-            scratch_shapes=[
-                pltpu.VMEM((WINDOW + PIECE, HEAD), BF),
-                pltpu.SemaphoreType.DMA((2,)),
-            ],
-        ),
-        compiler_params=pltpu.CompilerParams(vmem_limit_bytes=32 * MIB),
-    )(where, queries, probability, weights, gain, edge_values, values)
+        ),
+        compiler_params=pltpu.CompilerParams(vmem_limit_bytes=16 * MIB),
+    )(where, queries, probability, weights, gain, values, *edges, *after)
 
 
 def project_piece(where, combined, first_arrived, out_weight, other_weight):
@@ -337,7 +368,7 @@
             ],
             out_specs=pl.BlockSpec((PIECE, step), lambda i, w: (0, i)),
         ),
-        compiler_params=pltpu.CompilerParams(vmem_limit_bytes=32 * MIB),
+        compiler_params=pltpu.CompilerParams(vmem_limit_bytes=16 * MIB),
         name="project",
     )(where, *combined, first_arrived, out_weight, out_weight, other_weight)
 
@@ -347,7 +378,9 @@
     step = columns // 2
 
     def body(w, acc_ref, a_ref, wa_ref, *refs):
-        refs[-1][...] = (acc_ref[...] + dot(a_ref[...], wa_ref[...])).astype(BF)
+        here = pl.ds(pl.multiple_of(pl.program_id(0) * step, step), step)
+        rows = pl.ds(pl.multiple_of((1 - w[0]) * HEAD, HEAD), HEAD)
+        refs[-1][...] = (acc_ref[:, here] + dot(a_ref[...], wa_ref[rows, here])).astype(BF)
 
     held = () if before is None else (before,)
     return pl.pallas_call(
@@ -356,15 +389,10 @@
         grid_spec=pltpu.PrefetchScalarGridSpec(
             num_scalar_prefetch=1,
             grid=(2,),
-            in_specs=[
-                pl.BlockSpec((PIECE, step), lambda i, w: (0, i)),
-                pl.BlockSpec((PIECE, HEAD), lambda i, w: (0, 0)),
-                pl.BlockSpec((HEAD, step), lambda i, w: (1 - w[0], i)),
-            ]
-            + [any_spec()] * len(held),
+            in_specs=[vmem_spec(), vmem_spec(), vmem_spec()] + [any_spec()] * len(held),
             out_specs=pl.BlockSpec((PIECE, step), lambda i, w: (at, i)),
         ),
-        compiler_params=pltpu.CompilerParams(vmem_limit_bytes=32 * MIB),
+        compiler_params=pltpu.CompilerParams(vmem_limit_bytes=12 * MIB),
         input_output_aliases={4: 0} if held else {},
     )(where, partial, last_arrived, other_weight, *held)
 
@@ -390,7 +418,7 @@
     memory_gain,
     out_weight,
 ):
-    raw_out_weight = out_weight
+    raw_out_weight, raw_values = out_weight, value_rows
     queries, key_rows, value_rows, token_rates, gate_fast, lift_fast, down_fast, out_weight = (
         pltpu.with_memory_space_constraint(x, pltpu.HBM)
         for x in (
@@ -421,7 +449,8 @@
     count = lax.axis_size("seq")
     along = [(i, i + 1) for i in range(count - 1)]
     edge_keys = lax.ppermute(key_rows, "seq", along)
-    edge_values = lax.ppermute(value_rows, "seq", along)
+    edge_late = lax.ppermute(raw_values[PIECE:], "seq", along)
+    edge_early = lax.ppermute(raw_values[:PIECE], "seq", along)
 
     chip_sum = (grads_mine + grads_got.astype(F32)).astype(BF)
     slices = over_planes(chip_sum.reshape(PLANES, -1, HEAD))
@@ -446,28 +475,23 @@
         pairs,
     )
 
-    probability = probabilities(has_edge, queries, edge_keys, key_rows)
+    probability = pltpu.with_memory_space_constraint(
+        probabilities(has_edge, queries, edge_keys, key_rows), pltpu.HBM
+    )
 
     pieces = tokens_here // PIECE
     head_pair = [(0, 1), (1, 0)]
-    made, arrived = {}, {}
-    for mirror, weights in ((False, weights_mine), (True, weights_theirs)):
-        for at in range(pieces):
+    made, arrived, after = {}, {}, ()
+    for at in reversed(range(pieces)):
+        edges = (edge_late,) if at else (edge_early, edge_late)
+        for mirror, weights in ((False, weights_mine), (True, weights_theirs)):
             piece = combined_piece(
-                at,
-                mirror,
-                where,
-                queries,
-                probability,
-                weights,
-                memory_gain,
-                edge_values,
-                value_rows,
+                at, mirror, where, queries, probability, weights, memory_gain, edges, value_rows, after
             )
-            made[mirror, at] = piece
+            made[mirror, at], after = piece, (piece,)
             arrived[mirror, at] = lax.ppermute(piece, "head", head_pair)
     out = None
-    for at in range(pieces):
+    for at in reversed(range(pieces)):
         partial = project_piece(
             where,
             (made[False, at], made[True, at]),
@@ -475,9 +499,7 @@
             out_weight,
             other_weight,
         )
-        out = finish_piece(
-            at, tokens_here, where, partial, arrived[True, at], other_weight, out
-        )
+        out = finish_piece(at, tokens_here, where, partial, arrived[True, at], other_weight, out)
     return out
 
 

time: 175 us -> 198 us (1.13)
  waiting for transfers between devices: 45.2 us -> 64 us
  Pallas kernels: 69.4 us -> 65.4 us
  local copies, waits for them, and re-layouts: 4.41 us -> 8.2 us
  starting transfers between devices: 22.7 us -> 26.1 us
    ppermute x1, waiting for transfers between devices: 32.3 us -> 44.9 us  [shards(): lax.ppermute(lax.dynamic_slice(raw_out_weight, (0, (1 - head) * columns),...]
    all_to_all x1, waiting for transfers between devices: 9.85 us -> 16.1 us  [over_planes(): lax.all_to_all(value, 'seq', 0, 0, tiled=True, axis_index_groups=groups)]
    ppermute x1, starting transfers between devices: 2.04 us -> 5.42 us  [shards(): lax.ppermute(lax.dynamic_slice(raw_out_weight, (0, (1 - head) * columns),...]
    unnamed x2 -> x6, local copies, waits for them, and re-layouts: 0.01 us -> 2.31 us
    ppermute x1 -> x2, starting transfers between devices: 4.24 us -> 5.02 us  [the longest x1 2.93 us: shards(): edge_early = lax.ppermute(raw_values[:PIECE], 'seq', along)]
  transfers between devices with their start and end apart: 11 -> 12, of which waited for: 3 -> 3; matrix products, arithmetic and copies ran while one was open for 2% -> 2% of each run, Pallas kernels for 34% -> 28%
where the time goes in v3:
time: 198 us; the launch traced here: 196 us
  Pallas kernels  65.4 us (33%)
  waiting for transfers between devices  64 us (32%)
  blocking collectives  31.3 us (16%)
  starting transfers between devices  26.1 us (13%)
  local copies, waits for them, and re-layouts  8.2 us (4%)
    ppermute x1, waiting for transfers between devices, shards(): lax.ppermute(lax.dynamic_slice(raw_out_weight, (0, (1 - head) * columns),...  44.9 us
    all_to_all x1, blocking collectives, over_planes(): lax.all_to_all(value, 'seq', 0, 0, tiled=True, axis_index_groups=groups)  31.3 us
    pallas_call x4, Pallas kernels, combined_piece(): pl.pallas_call(body, out_shape=jax.ShapeDtypeStruct((PIECE, HEAD), BF), g...  19.9 us
    all_to_all x1, waiting for transfers between devices, over_planes(): lax.all_to_all(value, 'seq', 0, 0, tiled=True, axis_index_groups=groups)  16.1 us
    pallas_call x2, Pallas kernels, head_grads(): pl.pallas_call(grads_body, out_shape=jax.ShapeDtypeStruct((3 * HEAD, HEAD...  14.7 us
    pallas_call x1, Pallas kernels, probabilities(): pl.pallas_call(scores_body, out_shape=jax.ShapeDtypeStruct((tokens, heads...  10.2 us
    pallas_call x1, Pallas kernels, renewed_weights(): pl.pallas_call(renew_body, out_shape=jax.ShapeDtypeStruct((3 * HEAD, HEAD...  8.29 us
    pallas_call x2, Pallas kernels, project_piece(): pl.pallas_call(body, out_shape=jax.ShapeDtypeStruct((PIECE, columns), F32...  7.81 us
  transfers between devices with their start and end apart: 12, of which 3 were waited for; matrix products, arithmetic and copies ran while one was open for 2% of the time, Pallas kernels for 28%

profile of v3, /device:TPU:0, one launch (start us, length us, event | category | flops | bytes accessed | tf_op | source)
XLA Modules:
  0.0 196.2 jit_solution(3597828548391183731)
XLA Ops:
  0.0 0.1 pad_add_fusion.1.where
  0.1 7.4 %head_grads.3 = bf16[1536,512]{1,0:T(8,128)(2,1)S(1)} custom-call(s32[2]{0:T(128)S(1)} %pad_add_fusion.1.where, bf16[1024,1024]{1,0:T(8,128)(2,1)} %k_hbm.3, bf16[1024,1024]{1,0:T(8,128)(2,1)} %value_hbm.7, f32[2,1024]{1,0:T(2,128)} %rate_ref.3, f32[2,512,512]{2,1,0:T(8,128)} %gate_ref.1, f32[2,512,512]{2,1,0:T(8,128)} %lift_ref.1, f32[2,512,512]{2,1,0:T(8,128)} %down_ref.1), custom_call_target="tpu_custom_call" | custom-call | tf_op jit(solution)/shard_map/head_grads/pallas_call | solution.py:118
  7.5 0.1 collective-permute-start.1
  7.5 0.1 pad_add_fusion.where.w
  7.6 7.4 %head_grads.2 = f32[1536,512]{1,0:T(8,128)S(1)} custom-call(s32[2]{0:T(128)S(1)} %pad_add_fusion.where.w, bf16[1024,1024]{1,0:T(8,128)(2,1)} %k_hbm.3, bf16[1024,1024]{1,0:T(8,128)(2,1)} %value_hbm.7, f32[2,1024]{1,0:T(2,128)} %rate_ref.3, f32[2,512,512]{2,1,0:T(8,128)} %gate_ref.1, f32[2,512,512]{2,1,0:T(8,128)} %lift_ref.1, f32[2,512,512]{2,1,0:T(8,128)} %down_ref.1), custom_call_target="tpu_custom_call" | custom-call | tf_op jit(solution)/shard_map/head_grads/pallas_call | solution.py:118
  15.0 0.0 collective-permute-done.1
  15.0 0.6 add_convert_fusion
  15.6 31.3 %all_to_all.10 = bf16[16,96,512]{2,1,0:T(8,128)(2,1)S(1)} all-to-all(bf16[16,96,512]{2,1,0:T(8,128)(2,1)S(1)} %bitcast.7), channel_id=1, replica_groups={{0,4,8,12,16,20,24,28,32,36,40,44,48,52,56,60},{1,5,9,13,17,21,25,29,33..., dimensions={0} | all-to-all | bytes 3145728 | tf_op jit(solution)/shard_map/all_to_all | solution.py:407
  46.9 0.2 reduce_sum.12
  47.1 1.7 collective-permute-start.2
  48.8 3.0 %collective-permute-done.2 = bf16[96,512]{1,0:T(8,128)(2,1)S(1)} collective-permute-done((bf16[96,512]{1,0:T(8,128)(2,1)S(1)}, bf16[96,512]{1,0:T(8,128)(2,1)S(1)}, u32[]{:S(2)}, u32[]{:S(2)}) %collective-permute-start.2) | collective-permute-done | bytes 98336 | tf_op jit(solution)/shard_map/ppermute | solution.py:402
  51.9 1.3 broadcast_in_dim.2
  53.2 3.7 %all-to-all-start.1 = ((bf16[16,96,512]{2,1,0:T(8,128)(2,1)}), bf16[16,96,512]{2,1,0:T(8,128)(2,1)S(1)}, u32[]{:S(2)}, u32[]{:S(2)}) async-start(bf16[16,96,512]{2,1,0:T(8,128)(2,1)} %broadcast_in_dim.2), calls=%async_computation.1 | async-start | bytes 3145728 | tf_op jit(solution)/shard_map/all_to_all | solution.py:407
  56.9 2.6 %collective-permute-start = (bf16[1024,1024]{1,0:T(8,128)(2,1)}, bf16[1024,1024]{1,0:T(8,128)(2,1)}, u32[]{:S(2)}, u32[]{:S(2)}) collective-permute-start(bf16[1024,1024]{1,0:T(8,128)(2,1)} %k_hbm.3), channel_id=1, source_target_pairs={{0,1},{1,2},{2,3},{3,4},{4,5},{5,6},{6,7},{7,8},{8,9},{9,10},{10,1... | collective-permute-start | bytes 6291464 | tf_op jit(solution)/shard_map/ppermute | solution.py:451
  59.5 3.1 %constant_dynamic-slice_fusion = bf16[1024,1024]{1,0:T(8,128)(2,1)} fusion(bf16[1024,2048]{1,0:T(8,128)(2,1)} %wb_ref.3, s32[]{:T(128)S(6)} %select_n.16), kind=kLoop, calls=%fused_computation.4 | loop fusion | bytes 4194308 | tf_op jit(solution)/shard_map/dynamic_slice | solution.py:471
  62.6 16.1 %all-to-all-done.1 = bf16[16,96,512]{2,1,0:T(8,128)(2,1)S(1)} async-done(((bf16[16,96,512]{2,1,0:T(8,128)(2,1)}), bf16[16,96,512]{2,1,0:T(8,128)(2,1)S(1)}, u32[]{:S(2)}, u32[]{:S(2)}) %all-to-all-start.1) | async-done | bytes 1572896 | tf_op jit(solution)/shard_map/all_to_all | solution.py:407
  78.7 0.0 copy-start.2
  78.7 8.3 %renewed_weights.1.w_ref = bf16[1536,512]{1,0:T(8,128)(2,1)} custom-call(s32[2]{0:T(128)S(1)} %pad_add_fusion.where.w, bf16[1536,512]{1,0:T(8,128)(2,1)S(1)} %bitcast.6, f32[2,512,512]{2,1,0:T(8,128)} %gate_ref.1, f32[2,512,512]{2,1,0:T(8,128)} %lift_ref.1, f32[2,512,512]{2,1,0:T(8,128)} %down_ref.1), custom_call_target="tpu_custom_call" | custom-call | tf_op jit(solution)/shard_map/renewed_weights/pallas_call | solution.py:188
  87.0 0.1 collective-permute-start.5
  87.1 5.4 %collective-permute-start.7 = (bf16[1024,1024]{1,0:T(8,128)(2,1)}, bf16[1024,1024]{1,0:T(8,128)(2,1)S(1)}, u32[]{:S(2)}, u32[]{:S(2)}) collective-permute-start(bf16[1024,1024]{1,0:T(8,128)(2,1)} %constant_dynamic-slice_fusion), channel_id=1, source_target_pairs={{0,66},{1,67},{2,64},{3,65},{4,70},{5,71},{6,68},{7,69},{8,74},{9,... | collective-permute-start | bytes 6291464 | tf_op jit(solution)/shard_map/ppermute | solution.py:470
  92.5 0.0 copy-done.2
  92.5 1.5 fusion
  94.0 2.1 %collective-permute-start.4 = (bf16[512,1024]{1,0:T(8,128)(2,1)}, bf16[512,1024]{1,0:T(8,128)(2,1)S(1)}, u32[]{:S(2)}, u32[]{:S(2)}) collective-permute-start(bf16[512,1024]{1,0:T(8,128)(2,1)} %get-tuple-element.5), channel_id=1, source_target_pairs={{0,1},{1,2},{2,3},{3,4},{4,5},{5,6},{6,7},{7,8},{8,9},{9,10},{10,1... | collective-permute-start | bytes 3145736 | tf_op jit(solution)/shard_map/ppermute | solution.py:452
  96.1 2.9 %collective-permute-start.3 = (bf16[512,1024]{1,0:T(8,128)(2,1)}, bf16[512,1024]{1,0:T(8,128)(2,1)}, u32[]{:S(2)}, u32[]{:S(2)}) collective-permute-start(bf16[512,1024]{1,0:T(8,128)(2,1)} %get-tuple-element.6), channel_id=1, source_target_pairs={{0,1},{1,2},{2,3},{3,4},{4,5},{5,6},{6,7},{7,8},{8,9},{9,10},{10,1... | collective-permute-start | bytes 3145736 | tf_op jit(solution)/shard_map/ppermute | solution.py:453
  99.0 0.0 collective-permute-done.edge_ref
  99.0 0.0 copy-start.1
  99.0 10.2 %probabilities.1.p_hbm = bf16[1024,2560]{1,0:T(8,128)(2,1)S(1)} custom-call(s32[1]{0:T(128)} %bitcast.2.flag, bf16[1024,1024]{1,0:T(8,128)(2,1)} %q_hbm.7, bf16[1024,1024]{1,0:T(8,128)(2,1)} %collective-permute-done.edge_ref, bf16[1024,1024]{1,0:T(8,128)(2,1)} %k_hbm.3), custom_call_target="tpu_custom_call" | custom-call | tf_op jit(solution)/shard_map/probabilities/pallas_call | solution.py:253
  109.2 0.0 copy-start
  109.2 2.3 %copy-done = bf16[1024,2560]{1,0:T(8,128)(2,1)} copy-done((bf16[1024,2560]{1,0:T(8,128)(2,1)}, bf16[1024,2560]{1,0:T(8,128)(2,1)S(1)}, u32[]{:S(2)}) %copy-start) | copy-done | bytes 5242904
  111.5 0.0 collective-permute-done.4.refs_0_.refs_1_
  111.5 0.0 copy-done.1
  111.5 5.0 %shard_map.91.refs_1_.a_ref = bf16[512,512]{1,0:T(8,128)(2,1)S(1)} custom-call(s32[2]{0:T(128)S(1)} %pad_add_fusion.where.w, bf16[1024,1024]{1,0:T(8,128)(2,1)} %q_hbm.7, bf16[1024,2560]{1,0:T(8,128)(2,1)} %copy-done, bf16[1536,512]{1,0:T(8,128)(2,1)} %renewed_weights.1.w_ref, f32[2,512]{1,0:T(2,128)S(1)} %copy-done.1, bf16[1024,1024]{1,0:T(8,128)(2,1)} %value_hbm.7, ...), custom_call_target="tpu_custom_call" | custom-call | tf_op jit(solution)/shard_map/pallas_call | solution.py:325
  116.5 1.7 collective-permute-start.9
  118.2 0.0 collective-permute-done.5.w_ref
  118.2 5.0 %shard_map.92.refs_2_.b_ref = bf16[512,512]{1,0:T(8,128)(2,1)S(1)} custom-call(s32[2]{0:T(128)S(1)} %pad_add_fusion.where.w, bf16[1024,1024]{1,0:T(8,128)(2,1)} %q_hbm.7, bf16[1024,2560]{1,0:T(8,128)(2,1)} %copy-done, bf16[1536,512]{1,0:T(8,128)(2,1)} %collective-permute-done.5.w_ref, f32[2,512]{1,0:T(2,128)S(1)} %copy-done.1, bf16[1024,1024]{1,0:T(8,128)(2,1)} %value_hbm.7, ...), custom_call_target="tpu_custom_call" | custom-call | tf_op jit(solution)/shard_map/pallas_call | solution.py:325
  123.2 0.0 collective-permute-done.3.refs_0_
  123.2 5.0 %shard_map.93.refs_2_.a_ref = bf16[512,512]{1,0:T(8,128)(2,1)S(1)} custom-call(s32[2]{0:T(128)S(1)} %pad_add_fusion.where.w, bf16[1024,1024]{1,0:T(8,128)(2,1)} %q_hbm.7, bf16[1024,2560]{1,0:T(8,128)(2,1)} %copy-done, bf16[1536,512]{1,0:T(8,128)(2,1)} %renewed_weights.1.w_ref, f32[2,512]{1,0:T(2,128)S(1)} %copy-done.1, bf16[1024,1024]{1,0:T(8,128)(2,1)} %value_hbm.7, ...), custom_call_target="tpu_custom_call" | custom-call | tf_op jit(solution)/shard_map/pallas_call | solution.py:325
  128.2 2.2 %collective-permute-start.6 = (bf16[512,512]{1,0:T(8,128)(2,1)S(1)}, bf16[512,512]{1,0:T(8,128)(2,1)S(1)}, u32[]{:S(2)}, u32[]{:S(2)}) collective-permute-start(bf16[512,512]{1,0:T(8,128)(2,1)S(1)} %shard_map.93.refs_2_.a_ref), channel_id=1, source_target_pairs={{0,64},{64,0},{1,65},{65,1},{2,66},{66,2},{3,67},{67,3},{4,68},{68... | collective-permute-start | bytes 1572872 | tf_op jit(solution)/shard_map/ppermute | solution.py:492
  130.4 1.4 collective-permute-start.10
  131.8 5.0 %shard_map.94.b_ref = bf16[512,512]{1,0:T(8,128)(2,1)S(1)} custom-call(s32[2]{0:T(128)S(1)} %pad_add_fusion.where.w, bf16[1024,1024]{1,0:T(8,128)(2,1)} %q_hbm.7, bf16[1024,2560]{1,0:T(8,128)(2,1)} %copy-done, bf16[1536,512]{1,0:T(8,128)(2,1)} %collective-permute-done.5.w_ref, f32[2,512]{1,0:T(2,128)S(1)} %copy-done.1, bf16[1024,1024]{1,0:T(8,128)(2,1)} %value_hbm.7, ...), custom_call_target="tpu_custom_call" | custom-call | tf_op jit(solution)/shard_map/pallas_call | solution.py:325
  136.8 2.2 %collective-permute-start.8 = (bf16[512,512]{1,0:T(8,128)(2,1)S(1)}, bf16[512,512]{1,0:T(8,128)(2,1)S(1)}, u32[]{:S(2)}, u32[]{:S(2)}) collective-permute-start(bf16[512,512]{1,0:T(8,128)(2,1)S(1)} %shard_map.94.b_ref), channel_id=1, source_target_pairs={{0,64},{64,0},{1,65},{65,1},{2,66},{66,2},{3,67},{67,3},{4,68},{68... | collective-permute-start | bytes 1572872 | tf_op jit(solution)/shard_map/ppermute | solution.py:492
  138.9 44.9 %collective-permute-done.7.wc_ref.wa_ref = bf16[1024,1024]{1,0:T(8,128)(2,1)S(1)} collective-permute-done((bf16[1024,1024]{1,0:T(8,128)(2,1)}, bf16[1024,1024]{1,0:T(8,128)(2,1)S(1)}, u32[]{:S(2)}, u32[]{:S(2)}) %collective-permute-start.7) | collective-permute-done | bytes 2097184 | tf_op jit(solution)/shard_map/ppermute | solution.py:470
  183.8 0.0 collective-permute-done.9.c_ref
  183.8 3.9 %project.3.acc_ref = f32[512,1024]{1,0:T(8,128)S(1)} custom-call(s32[2]{0:T(128)S(1)} %pad_add_fusion.where.w, bf16[512,512]{1,0:T(8,128)(2,1)S(1)} %shard_map.91.refs_1_.a_ref, bf16[512,512]{1,0:T(8,128)(2,1)S(1)} %shard_map.92.refs_2_.b_ref, bf16[512,512]{1,0:T(8,128)(2,1)S(1)} %collective-permute-done.9.c_ref, bf16[1024,2048]{1,0:T(8,128)(2,1)} %wb_ref.3, ...), custom_call_target="tpu_custom_call" | custom-call | tf_op jit(solution)/shard_map/project/pallas_call | solution.py:355
  187.8 0.0 collective-permute-done.6.c_ref
  187.8 3.9 %project.2.acc_ref = f32[512,1024]{1,0:T(8,128)S(1)} custom-call(s32[2]{0:T(128)S(1)} %pad_add_fusion.where.w, bf16[512,512]{1,0:T(8,128)(2,1)S(1)} %shard_map.93.refs_2_.a_ref, bf16[512,512]{1,0:T(8,128)(2,1)S(1)} %shard_map.94.b_ref, bf16[512,512]{1,0:T(8,128)(2,1)S(1)} %collective-permute-done.6.c_ref, bf16[1024,2048]{1,0:T(8,128)(2,1)} %wb_ref.3, ...), custom_call_target="tpu_custom_call" | custom-call | tf_op jit(solution)/shard_map/project/pallas_call | solution.py:355
  191.7 0.0 collective-permute-done.10.a_ref
  191.7 2.3 %shard_map.95.refs_0_ = bf16[1024,1024]{1,0:T(8,128)(2,1)} custom-call(s32[2]{0:T(128)S(1)} %pad_add_fusion.where.w, f32[512,1024]{1,0:T(8,128)S(1)} %project.3.acc_ref, bf16[512,512]{1,0:T(8,128)(2,1)S(1)} %collective-permute-done.10.a_ref, bf16[1024,1024]{1,0:T(8,128)(2,1)S(1)} %collective-permute-done.7.wc_ref.wa_ref), custom_call_target="tpu_custom_call" | custom-call | tf_op jit(solution)/shard_map/pallas_call | solution.py:386
  194.0 0.0 collective-permute-done.8.a_ref
  194.0 2.3 %shard_map.96 = bf16[1024,1024]{1,0:T(8,128)(2,1)} custom-call(s32[2]{0:T(128)S(1)} %pad_add_fusion.where.w, f32[512,1024]{1,0:T(8,128)S(1)} %project.2.acc_ref, bf16[512,512]{1,0:T(8,128)(2,1)S(1)} %collective-permute-done.8.a_ref, bf16[1024,1024]{1,0:T(8,128)(2,1)S(1)} %collective-permute-done.7.wc_ref.wa_ref, ...), custom_call_target="tpu_custom_call", output_to_operand_aliasing={{}: (4, {})} | custom-call | tf_op jit(solution)/shard_map/pallas_call | solution.py:386
  (1 shorter events, 0.0 us)
Async XLA Ops:
  7.5 7.6 %collective-permute-start.1 = (bf16[1536,512]{1,0:T(8,128)(2,1)S(1)}, bf16[1536,512]{1,0:T(8,128)(2,1)S(1)}, u32[]{:S(2)}, u32[]{:S(2)}) collective-permute-start(bf16[1536,512]{1,0:T(8,128)(2,1)S(1)} %head_grads.3), channel_id=1, source_target_pairs={{0,1},{1,0},{2,3},{3,2},{4,5},{5,4},{6,7},{7,6},{8,9},{9,8},{10,11... | collective-permute-start | bytes 4718600 | tf_op jit(solution)/shard_map/ppermute | solution.py:402
  47.1 4.7 %collective-permute-start.2 = (bf16[96,512]{1,0:T(8,128)(2,1)S(1)}, bf16[96,512]{1,0:T(8,128)(2,1)S(1)}, u32[]{:S(2)}, u32[]{:S(2)}) collective-permute-start(bf16[96,512]{1,0:T(8,128)(2,1)S(1)} %reduce_sum.12), channel_id=1, source_target_pairs={{0,2},{1,3},{2,0},{3,1},{4,6},{5,7},{6,4},{7,5},{8,10},{9,11},{10,... | collective-permute-start | bytes 294920 | tf_op jit(solution)/shard_map/ppermute | solution.py:402
  53.2 25.5 %all-to-all-start.1 = ((bf16[16,96,512]{2,1,0:T(8,128)(2,1)}), bf16[16,96,512]{2,1,0:T(8,128)(2,1)S(1)}, u32[]{:S(2)}, u32[]{:S(2)}) async-start(bf16[16,96,512]{2,1,0:T(8,128)(2,1)} %broadcast_in_dim.2), calls=%async_computation.1 | async-start | bytes 3145728 | tf_op jit(solution)/shard_map/all_to_all | solution.py:407
  56.9 42.1 %collective-permute-start = (bf16[1024,1024]{1,0:T(8,128)(2,1)}, bf16[1024,1024]{1,0:T(8,128)(2,1)}, u32[]{:S(2)}, u32[]{:S(2)}) collective-permute-start(bf16[1024,1024]{1,0:T(8,128)(2,1)} %k_hbm.3), channel_id=1, source_target_pairs={{0,1},{1,2},{2,3},{3,4},{4,5},{5,6},{6,7},{7,8},{8,9},{9,10},{10,1... | collective-permute-start | bytes 6291464 | tf_op jit(solution)/shard_map/ppermute | solution.py:451
  78.7 13.8 %copy-start.2 = (bf16[1024,1024]{1,0:T(8,128)(2,1)S(1)}, bf16[1024,1024]{1,0:T(8,128)(2,1)}, u32[]{:S(2)}) copy-start(bf16[1024,1024]{1,0:T(8,128)(2,1)} %value_hbm.7) | copy-start | bytes 6291460
  87.0 31.3 %collective-permute-start.5 = (bf16[1536,512]{1,0:T(8,128)(2,1)}, bf16[1536,512]{1,0:T(8,128)(2,1)}, u32[]{:S(2)}, u32[]{:S(2)}) collective-permute-start(bf16[1536,512]{1,0:T(8,128)(2,1)} %renewed_weights.1.w_ref), channel_id=1, source_target_pairs={{0,1},{1,0},{2,3},{3,2},{4,5},{5,4},{6,7},{7,6},{8,9},{9,8},{10,11... | collective-permute-start | bytes 4718600 | tf_op jit(solution)/shard_map/ppermute | solution.py:402
  87.1 96.8 %collective-permute-start.7 = (bf16[1024,1024]{1,0:T(8,128)(2,1)}, bf16[1024,1024]{1,0:T(8,128)(2,1)S(1)}, u32[]{:S(2)}, u32[]{:S(2)}) collective-permute-start(bf16[1024,1024]{1,0:T(8,128)(2,1)} %constant_dynamic-slice_fusion), channel_id=1, source_target_pairs={{0,66},{1,67},{2,64},{3,65},{4,70},{5,71},{6,68},{7,69},{8,74},{9,... | collective-permute-start | bytes 6291464 | tf_op jit(solution)/shard_map/ppermute | solution.py:470
  94.0 17.5 %collective-permute-start.4 = (bf16[512,1024]{1,0:T(8,128)(2,1)}, bf16[512,1024]{1,0:T(8,128)(2,1)S(1)}, u32[]{:S(2)}, u32[]{:S(2)}) collective-permute-start(bf16[512,1024]{1,0:T(8,128)(2,1)} %get-tuple-element.5), channel_id=1, source_target_pairs={{0,1},{1,2},{2,3},{3,4},{4,5},{5,6},{6,7},{7,8},{8,9},{9,10},{10,1... | collective-permute-start | bytes 3145736 | tf_op jit(solution)/shard_map/ppermute | solution.py:452
  96.1 27.1 %collective-permute-start.3 = (bf16[512,1024]{1,0:T(8,128)(2,1)}, bf16[512,1024]{1,0:T(8,128)(2,1)}, u32[]{:S(2)}, u32[]{:S(2)}) collective-permute-start(bf16[512,1024]{1,0:T(8,128)(2,1)} %get-tuple-element.6), channel_id=1, source_target_pairs={{0,1},{1,2},{2,3},{3,4},{4,5},{5,6},{6,7},{7,8},{8,9},{9,10},{10,1... | collective-permute-start | bytes 3145736 | tf_op jit(solution)/shard_map/ppermute | solution.py:453
  99.0 12.5 %copy-start.1 = (f32[2,512]{1,0:T(2,128)S(1)}, f32[2,512]{1,0:T(2,128)}, u32[]{:S(2)}) copy-start(f32[2,512]{1,0:T(2,128)} %gain_ref.7) | copy-start | bytes 12292
  109.2 2.3 %copy-start = (bf16[1024,2560]{1,0:T(8,128)(2,1)}, bf16[1024,2560]{1,0:T(8,128)(2,1)S(1)}, u32[]{:S(2)}) copy-start(bf16[1024,2560]{1,0:T(8,128)(2,1)S(1)} %probabilities.1.p_hbm) | copy-start | bytes 15728644
  116.5 67.4 %collective-permute-start.9 = (bf16[512,512]{1,0:T(8,128)(2,1)S(1)}, bf16[512,512]{1,0:T(8,128)(2,1)S(1)}, u32[]{:S(2)}, u32[]{:S(2)}) collective-permute-start(bf16[512,512]{1,0:T(8,128)(2,1)S(1)} %shard_map.91.refs_1_.a_ref), channel_id=1, source_target_pairs={{0,64},{64,0},{1,65},{65,1},{2,66},{66,2},{3,67},{67,3},{4,68},{68... | collective-permute-start | bytes 1572872 | tf_op jit(solution)/shard_map/ppermute | solution.py:492
  128.2 59.6 %collective-permute-start.6 = (bf16[512,512]{1,0:T(8,128)(2,1)S(1)}, bf16[512,512]{1,0:T(8,128)(2,1)S(1)}, u32[]{:S(2)}, u32[]{:S(2)}) collective-permute-start(bf16[512,512]{1,0:T(8,128)(2,1)S(1)} %shard_map.93.refs_2_.a_ref), channel_id=1, source_target_pairs={{0,64},{64,0},{1,65},{65,1},{2,66},{66,2},{3,67},{67,3},{4,68},{68... | collective-permute-start | bytes 1572872 | tf_op jit(solution)/shard_map/ppermute | solution.py:492
  130.4 61.3 %collective-permute-start.10 = (bf16[512,512]{1,0:T(8,128)(2,1)S(1)}, bf16[512,512]{1,0:T(8,128)(2,1)S(1)}, u32[]{:S(2)}, u32[]{:S(2)}) collective-permute-start(bf16[512,512]{1,0:T(8,128)(2,1)S(1)} %shard_map.92.refs_2_.b_ref), channel_id=1, source_target_pairs={{0,64},{64,0},{1,65},{65,1},{2,66},{66,2},{3,67},{67,3},{4,68},{68... | collective-permute-start | bytes 1572872 | tf_op jit(solution)/shard_map/ppermute | solution.py:492
  136.8 57.2 %collective-permute-start.8 = (bf16[512,512]{1,0:T(8,128)(2,1)S(1)}, bf16[512,512]{1,0:T(8,128)(2,1)S(1)}, u32[]{:S(2)}, u32[]{:S(2)}) collective-permute-start(bf16[512,512]{1,0:T(8,128)(2,1)S(1)} %shard_map.94.b_ref), channel_id=1, source_target_pairs={{0,64},{64,0},{1,65},{65,1},{2,66},{66,2},{3,67},{67,3},{4,68},{68... | collective-permute-start | bytes 1572872 | tf_op jit(solution)/shard_map/ppermute | solution.py:492

commit v4 on v3

--- a/solution.py
+++ b/solution.py
@@ -19,8 +19,9 @@
 F32 = jnp.float32
 MIB = 1 << 20
 
-PLANE = 4
-PLANES = 16
+CORES = 2
+CHIPS = 32
+OWNED = HEAD // CHIPS
 
 ROW_BY_ROW = (((1,), (1,)), ((), ()))
 COL_BY_COL = (((0,), (0,)), ((), ()))
@@ -110,14 +111,15 @@
             into_gate, into_lift, down_sum = parts
         else:
             for m, (first, second) in enumerate(zip((into_gate, into_lift, down_sum), parts)):
-                out_ref[m * HEAD : (m + 1) * HEAD, :] = (first + second).astype(out_ref.dtype)
+                total = (first + second).astype(out_ref.dtype)
+                out_ref[:, m * OWNED : (m + 1) * OWNED, :] = total.reshape(CHIPS, OWNED, HEAD)
 
 
 def head_grads(which, keys, values, rates, gate, lift, down, dtype):
     tokens = keys.shape[0]
     return pl.pallas_call(
         grads_body,
-        out_shape=jax.ShapeDtypeStruct((3 * HEAD, HEAD), dtype),
+        out_shape=jax.ShapeDtypeStruct((CHIPS, 3 * OWNED, HEAD), dtype),
         grid_spec=pltpu.PrefetchScalarGridSpec(
             num_scalar_prefetch=1,
             grid=(1,),
@@ -142,62 +144,103 @@
     )(which, keys, values, rates, gate, lift, down)
 
 
-def renew_body(where, g_ref, gate_ref, lift_ref, down_ref, out_ref, olds, sems):
-    copies = [
-        pltpu.make_async_copy(ref.at[where[0]], olds.at[i], sems.at[i])
-        for i, ref in enumerate((gate_ref, lift_ref, down_ref))
-    ]
-    for copy in copies:
-        copy.start()
-    eye = (
-        lax.broadcasted_iota(jnp.int32, (HEAD, HEAD), 0)
-        == lax.broadcasted_iota(jnp.int32, (HEAD, HEAD), 1)
-    ).astype(F32)
-    iterates, grams = [], []
-    for i in range(3):
-        g = g_ref[i * HEAD : (i + 1) * HEAD, :]
-        wide = g.astype(F32)
-        gram = dot_on(g, g, COL_BY_COL)
-        squares = jnp.sum(wide * wide, axis=0, keepdims=True)
-        inverse = lax.rsqrt(jnp.sum(squares, axis=1, keepdims=True) + EPSILON)
-        iterates.append((wide * inverse).astype(BF))
-        grams.append(gram * (inverse * inverse))
-    for sweep in range(NS_STEPS):
-        polys = []
-        for i in range(3):
-            half = grams[i].astype(BF)
-            square = dot(half, half)
-            polys.append((COEF_A * eye + COEF_B * grams[i] + COEF_C * square).astype(BF))
-        for i in range(3):
-            iterates[i] = dot(iterates[i], polys[i]).astype(BF)
-        if sweep + 1 < NS_STEPS:
-            for i in range(3):
-                grams[i] = dot_on(iterates[i], iterates[i], COL_BY_COL)
-    for i in range(3):
-        copies[i].wait()
-        old = olds[i]
-        change = old - iterates[i].astype(F32)
-        old_square = jnp.sum(old * old, axis=0, keepdims=True)
-        new_square = jnp.sum(change * change, axis=0, keepdims=True)
-        out_ref[i * HEAD : (i + 1) * HEAD, :] = (
-            change * jnp.sqrt(old_square / (new_square + EPSILON))
-        ).astype(BF)
-
-
-def renewed_weights(which, grads, gate, lift, down):
-    return pl.pallas_call(
-        renew_body,
-        out_shape=jax.ShapeDtypeStruct((3 * HEAD, HEAD), BF),
+def renewed_weights(which, grads, fast):
+    count = len(fast)
+
+    def body(where, g_ref, *refs):
+        fast_hbm, (out_ref, olds, sems) = refs[:count], refs[count:]
+        copies = [
+            pltpu.make_async_copy(ref.at[where[0]], olds.at[i], sems.at[i])
+            for i, ref in enumerate(fast_hbm)
+        ]
+        for copy in copies:
+            copy.start()
+        diagonal = jnp.where(
+            lax.broadcasted_iota(jnp.int32, (HEAD, HEAD), 0)
+            == lax.broadcasted_iota(jnp.int32, (HEAD, HEAD), 1),
+            COEF_A,
+            0.0,
+        )
+        iterates, grams = [], []
+        for i in range(count):
+            g = g_ref[:, i * OWNED : (i + 1) * OWNED, :].reshape(HEAD, HEAD)
+            wide = g.astype(F32)
+            gram = dot_on(g, g, COL_BY_COL)
+            squares = jnp.sum(wide * wide, axis=0, keepdims=True)
+            inverse = lax.rsqrt(jnp.sum(squares, axis=1, keepdims=True) + EPSILON)
+            iterates.append((wide * inverse).astype(BF))
+            grams.append(gram * (inverse * inverse))
+        for sweep in range(NS_STEPS):
+            polys = []
+            for i in range(count):
+                half = grams[i].astype(BF)
+                square = dot(half, half)
+                polys.append((diagonal + COEF_B * grams[i] + COEF_C * square).astype(BF))
+            for i in range(count):
+                iterates[i] = dot(iterates[i], polys[i]).astype(BF)
+            if sweep + 1 < NS_STEPS:
+                for i in range(count):
+                    grams[i] = dot_on(iterates[i], iterates[i], COL_BY_COL)
+        for i in range(count):
+            copies[i].wait()
+            old = olds[i]
+            change = old - iterates[i].astype(F32)
+            old_square = jnp.sum(old * old, axis=0, keepdims=True)
+            new_square = jnp.sum(change * change, axis=0, keepdims=True)
+            out_ref[i * HEAD : (i + 1) * HEAD, :] = (
+                change * jnp.sqrt(old_square / (new_square + EPSILON))
+            ).astype(BF)
+
+    return pl.pallas_call(
+        body,
+        out_shape=jax.ShapeDtypeStruct((count * HEAD, HEAD), BF),
         grid_spec=pltpu.PrefetchScalarGridSpec(
             num_scalar_prefetch=1,
             grid=(1,),
-            in_specs=[vmem_spec(), any_spec(), any_spec(), any_spec()],
+            in_specs=[vmem_spec()] + [any_spec()] * count,
             out_specs=vmem_spec(),
-            scratch_shapes=[pltpu.VMEM((3, HEAD, HEAD), F32), pltpu.SemaphoreType.DMA((3,))],
+            scratch_shapes=[
+                pltpu.VMEM((count, HEAD, HEAD), F32),
+                pltpu.SemaphoreType.DMA((count,)),
+            ],
         ),
         compiler_params=pltpu.CompilerParams(vmem_limit_bytes=24 * MIB),
-        name="renewed_weights",
-    )(which, grads, gate, lift, down)
+    )(which, grads, *fast)
+
+
+def cut_blocks(where, out_weight, values):
+    columns = out_weight.shape[1] // 2
+    rows = values.shape[0] // 2
+
+    def body(w, weight_ref, value_ref, weight_out, late_out, early_out, sems):
+        other = pl.ds(pl.multiple_of((1 - w[1]) * columns, columns), columns)
+        copies = (
+            pltpu.make_async_copy(value_ref.at[pl.ds(rows, rows)], late_out, sems.at[0]),
+            pltpu.make_async_copy(weight_ref.at[:, other], weight_out, sems.at[1]),
+            pltpu.make_async_copy(value_ref.at[pl.ds(0, rows)], early_out, sems.at[2]),
+        )
+        for copy in copies:
+            copy.start()
+        for copy in copies:
+            copy.wait()
+
+    width = values.shape[1]
+    return pl.pallas_call(
+        body,
+        out_shape=(
+            pltpu.HBM((out_weight.shape[0], columns), BF),
+            pltpu.HBM((rows, width), BF),
+            pltpu.HBM((rows, width), BF),
+        ),
+        grid_spec=pltpu.PrefetchScalarGridSpec(
+            num_scalar_prefetch=1,
+            grid=(1,),
+            in_specs=[any_spec(), any_spec()],
+            out_specs=[any_spec(), any_spec(), any_spec()],
+            scratch_shapes=[pltpu.SemaphoreType.DMA((3,))],
+        ),
+        name="cut_blocks",
+    )(where, out_weight, values)
 
 
 SPAN = WINDOW + CHUNK
@@ -402,9 +445,13 @@
     return lax.ppermute(value, "seq", [(i, i ^ flip) for i in range(count)])
 
 
-def over_planes(value):
-    groups = [[p * PLANE + r for p in range(PLANES)] for r in range(PLANE)]
+def over_chips(value):
+    groups = [[p * CORES + r for p in range(CHIPS)] for r in range(CORES)]
     return lax.all_to_all(value, "seq", 0, 0, tiled=True, axis_index_groups=groups)
+
+
+def to_all_chips(part):
+    return over_chips(jnp.broadcast_to(part[None], (CHIPS, *part.shape)))
 
 
 def shards(
@@ -418,7 +465,6 @@
     memory_gain,
     out_weight,
 ):
-    raw_out_weight, raw_values = out_weight, value_rows
     queries, key_rows, value_rows, token_rates, gate_fast, lift_fast, down_fast, out_weight = (
         pltpu.with_memory_space_constraint(x, pltpu.HBM)
         for x in (
@@ -449,31 +495,21 @@
     count = lax.axis_size("seq")
     along = [(i, i + 1) for i in range(count - 1)]
     edge_keys = lax.ppermute(key_rows, "seq", along)
-    edge_late = lax.ppermute(raw_values[PIECE:], "seq", along)
-    edge_early = lax.ppermute(raw_values[:PIECE], "seq", along)
-
-    chip_sum = (grads_mine + grads_got.astype(F32)).astype(BF)
-    slices = over_planes(chip_sum.reshape(PLANES, -1, HEAD))
-    part = slices.astype(F32).sum(axis=0).astype(BF)
-    other = partner(part, 2)
-    part = (part.astype(F32) + other.astype(F32)).astype(BF)
-    spread = jnp.broadcast_to(part[None], (PLANES, *part.shape))
-    grads = over_planes(spread).reshape(3 * HEAD, HEAD)
-
-    weights_mine = renewed_weights(where, grads, *fast)
-    weights_theirs = partner(weights_mine, 1)
-
-    columns = out_weight.shape[1] // 2
+    other_columns, late, early = cut_blocks(where, out_weight, value_rows)
+    edge_late = lax.ppermute(late, "seq", along)
+    edge_early = lax.ppermute(early, "seq", along)
     pairs = [
         (group * count + i, (1 - group) * count + (i ^ 2)) for group in range(2) for i in range(count)
     ]
-    other_weight = lax.ppermute(
-        lax.dynamic_slice(
-            raw_out_weight, (0, (1 - head) * columns), (out_weight.shape[0], columns)
-        ),
-        ("head", "seq"),
-        pairs,
-    )
+    other_weight = lax.ppermute(other_columns, ("head", "seq"), pairs)
+
+    chip_sum = (grads_mine + grads_got.astype(F32)).astype(BF)
+    slices = over_chips(chip_sum)
+    part = slices.astype(F32).sum(axis=0).astype(BF)
+    grads = to_all_chips(part)
+
+    weights_mine = renewed_weights(where, grads, (gate_fast, lift_fast, down_fast))
+    weights_theirs = partner(weights_mine, 1)
 
     probability = pltpu.with_memory_space_constraint(
         probabilities(has_edge, queries, edge_keys, key_rows), pltpu.HBM

time: 198 us -> 303 us (1.53)
  Pallas kernels: 65.4 us -> 194 us
  waiting for transfers between devices: 64 us -> 46.3 us
  local copies, waits for them, and re-layouts: 8.2 us -> 3.66 us
    pallas_call x3 -> x4, Pallas kernels: 23 us -> 152 us  [the longest x1 129 us: cut_blocks(): pl.pallas_call(body, out_shape=(pltpu.HBM((out_weight.shape[0], columns),...]
    all_to_all x1, waiting for transfers between devices: 16.1 us -> 0.01 us  [over_chips(): lax.all_to_all(value, 'seq', 0, 0, tiled=True, axis_index_groups=groups)]
    dynamic_slice x1 -> x0, local copies, waits for them, and re-layouts: 3.08 us -> none  [shards(): lax.dynamic_slice(raw_out_weight, (0, (1 - head) * columns), (out_weight....]
    ppermute x3 -> x2, waiting for transfers between devices: 3.04 us -> 0.01 us  [partner(): return lax.ppermute(value, 'seq', [(i, i ^ flip) for i in range(count)])]
  transfers between devices with their start and end apart: 12 -> 11, of which waited for: 3 -> 1; matrix products, arithmetic and copies ran while one was open for 2% -> 0% of each run, Pallas kernels for 28% -> 61%
where the time goes in v4:
time: 303 us; the launch traced here: 302 us
  Pallas kernels  194 us (64%)
  waiting for transfers between devices  46.3 us (15%)
  blocking collectives  33.2 us (11%)
  starting transfers between devices  23.3 us (8%)
  local copies, waits for them, and re-layouts  3.66 us (1%)
    pallas_call x1, Pallas kernels, cut_blocks(): pl.pallas_call(body, out_shape=(pltpu.HBM((out_weight.shape[0], columns),...  129 us
    ppermute x1, waiting for transfers between devices, shards(): other_weight = lax.ppermute(other_columns, ('head', 'seq'), pairs)  46.3 us
    all_to_all x1, blocking collectives, over_chips(): lax.all_to_all(value, 'seq', 0, 0, tiled=True, axis_index_groups=groups)  33.2 us
    pallas_call x4, Pallas kernels, combined_piece(): pl.pallas_call(body, out_shape=jax.ShapeDtypeStruct((PIECE, HEAD), BF), g...  19.9 us
    pallas_call x2, Pallas kernels, head_grads(): pl.pallas_call(grads_body, out_shape=jax.ShapeDtypeStruct((CHIPS, 3 * OWN...  14.7 us
    pallas_call x1, Pallas kernels, probabilities(): pl.pallas_call(scores_body, out_shape=jax.ShapeDtypeStruct((tokens, heads...  10.2 us
    pallas_call x1, Pallas kernels, renewed_weights(): pl.pallas_call(body, out_shape=jax.ShapeDtypeStruct((count * HEAD, HEAD),...  8.24 us
    pallas_call x2, Pallas kernels, project_piece(): pl.pallas_call(body, out_shape=jax.ShapeDtypeStruct((PIECE, columns), F32...  7.8 us
  transfers between devices with their start and end apart: 11, of which 1 were waited for; matrix products, arithmetic and copies ran while one was open for 0% of the time, Pallas kernels for 61%

profile of v4, /device:TPU:0, one launch (start us, length us, event | category | flops | bytes accessed | tf_op | source)
XLA Modules:
  0.0 301.9 jit_solution(4600281390463537325)
XLA Ops:
  0.0 0.1 pad_add_fusion.1.where
  0.1 7.4 %head_grads.3 = bf16[32,48,512]{2,1,0:T(8,128)(2,1)S(1)} custom-call(s32[2]{0:T(128)S(1)} %pad_add_fusion.1.where, bf16[1024,1024]{1,0:T(8,128)(2,1)} %k_hbm.3, bf16[1024,1024]{1,0:T(8,128)(2,1)} %value_hbm.7, f32[2,1024]{1,0:T(2,128)} %rate_ref.3, f32[2,512,512]{2,1,0:T(8,128)} %refs_0_.1, f32[2,512,512]{2,1,0:T(8,128)} %refs_1_.1, f32[2,512,512]{2,1,0:T(8,128)} %refs_2_.1), custom_call_target="tpu_custom_call" | custom-call | tf_op jit(solution)/shard_map/head_grads/pallas_call | solution.py:120
  7.5 0.1 collective-permute-start.1
  7.5 0.1 pad_add_fusion.where.w
  7.6 0.0 copy-start.2
  7.6 7.4 %head_grads.2 = f32[32,48,512]{2,1,0:T(8,128)S(1)} custom-call(s32[2]{0:T(128)S(1)} %pad_add_fusion.where.w, bf16[1024,1024]{1,0:T(8,128)(2,1)} %k_hbm.3, bf16[1024,1024]{1,0:T(8,128)(2,1)} %value_hbm.7, f32[2,1024]{1,0:T(2,128)} %rate_ref.3, f32[2,512,512]{2,1,0:T(8,128)} %refs_0_.1, f32[2,512,512]{2,1,0:T(8,128)} %refs_1_.1, f32[2,512,512]{2,1,0:T(8,128)} %refs_2_.1), custom_call_target="tpu_custom_call" | custom-call | tf_op jit(solution)/shard_map/head_grads/pallas_call | solution.py:120
  15.0 0.0 copy-done.2
  15.0 0.0 collective-permute-done.1
  15.0 0.6 add_convert_fusion
  15.7 33.2 %all_to_all.10 = bf16[32,48,512]{2,1,0:T(8,128)(2,1)S(1)} all-to-all(bf16[32,48,512]{2,1,0:T(8,128)(2,1)S(1)} %add_convert_fusion), channel_id=1, replica_groups={{0,2,4,6,8,10,12,14,16,18,20,22,24,26,28,30,32,34,36,38,40,42,44,46,48,..., dimensions={0} | all-to-all | bytes 3145728 | tf_op jit(solution)/shard_map/all_to_all | solution.py:450
  48.9 0.2 reduce_sum.12
  49.1 1.3 broadcast_in_dim.2
  50.5 4.0 %all-to-all-start.1 = ((bf16[32,48,512]{2,1,0:T(8,128)(2,1)}), bf16[32,48,512]{2,1,0:T(8,128)(2,1)S(1)}, u32[]{:S(2)}, u32[]{:S(2)}) async-start(bf16[32,48,512]{2,1,0:T(8,128)(2,1)} %broadcast_in_dim.2), calls=%async_computation.1 | async-start | bytes 3145728 | tf_op jit(solution)/shard_map/all_to_all | solution.py:450
  54.4 0.0 copy-start.3
  54.4 2.6 collective-permute-start
  57.1 128.8 %cut_blocks.1 = (bf16[1024,1024]{1,0:T(8,128)(2,1)}, bf16[512,1024]{1,0:T(8,128)(2,1)}, bf16[512,1024]{1,0:T(8,128)(2,1)}) custom-call(s32[2]{0:T(128)} %copy-done.2, bf16[1024,2048]{1,0:T(8,128)(2,1)} %wb_ref.3, bf16[1024,1024]{1,0:T(8,128)(2,1)} %value_hbm.7), custom_call_target="tpu_custom_call" | custom-call | tf_op jit(solution)/shard_map/cut_blocks/pallas_call | solution.py:228
  185.9 0.0 all-to-all-done.1.g_ref
  185.9 0.0 copy-done.3
  186.0 8.2 %shard_map.91.w_ref = bf16[1536,512]{1,0:T(8,128)(2,1)} custom-call(s32[2]{0:T(128)S(1)} %copy-done.3, bf16[32,48,512]{2,1,0:T(8,128)(2,1)S(1)} %all-to-all-done.1.g_ref, f32[2,512,512]{2,1,0:T(8,128)} %refs_0_.1, f32[2,512,512]{2,1,0:T(8,128)} %refs_1_.1, f32[2,512,512]{2,1,0:T(8,128)} %refs_2_.1), custom_call_target="tpu_custom_call" | custom-call | tf_op jit(solution)/shard_map/pallas_call | solution.py:194
  194.2 1.3 collective-permute-start.4
  195.5 2.9 collective-permute-start.6
  198.4 1.8 collective-permute-start.3
  200.2 3.1 %collective-permute-start.2 = (bf16[512,1024]{1,0:T(8,128)(2,1)}, bf16[512,1024]{1,0:T(8,128)(2,1)}, u32[]{:S(2)}, u32[]{:S(2)}) collective-permute-start(bf16[512,1024]{1,0:T(8,128)(2,1)} %get-tuple-element.8), channel_id=1, source_target_pairs={{0,1},{1,2},{2,3},{3,4},{4,5},{5,6},{6,7},{7,8},{8,9},{9,10},{10,1... | collective-permute-start | bytes 3145736 | tf_op jit(solution)/shard_map/ppermute | solution.py:500
  203.3 0.0 collective-permute-done.edge_ref
  203.3 0.0 copy-start.1
  203.3 10.2 %probabilities.1.p_hbm = bf16[1024,2560]{1,0:T(8,128)(2,1)S(1)} custom-call(s32[1]{0:T(128)} %bitcast.2.flag, bf16[1024,1024]{1,0:T(8,128)(2,1)} %q_hbm.7, bf16[1024,1024]{1,0:T(8,128)(2,1)} %collective-permute-done.edge_ref, bf16[1024,1024]{1,0:T(8,128)(2,1)} %k_hbm.3), custom_call_target="tpu_custom_call" | custom-call | tf_op jit(solution)/shard_map/probabilities/pallas_call | solution.py:296
  213.5 0.0 copy-start
  213.5 2.3 copy-done
  215.8 0.0 collective-permute-done.3.refs_0_.refs_1_
  215.8 0.0 copy-done.1
  215.8 5.0 %shard_map.92.refs_1_.a_ref = bf16[512,512]{1,0:T(8,128)(2,1)S(1)} custom-call(s32[2]{0:T(128)S(1)} %copy-done.3, bf16[1024,1024]{1,0:T(8,128)(2,1)} %q_hbm.7, bf16[1024,2560]{1,0:T(8,128)(2,1)} %copy-done, bf16[1536,512]{1,0:T(8,128)(2,1)} %shard_map.91.w_ref, f32[2,512]{1,0:T(2,128)S(1)} %copy-done.1, bf16[1024,1024]{1,0:T(8,128)(2,1)} %value_hbm.7, ...), custom_call_target="tpu_custom_call" | custom-call | tf_op jit(solution)/shard_map/pallas_call | solution.py:368
  220.8 2.1 collective-permute-start.8
  222.9 0.0 collective-permute-done.4.w_ref
  222.9 5.0 %shard_map.93.refs_2_.b_ref = bf16[512,512]{1,0:T(8,128)(2,1)S(1)} custom-call(s32[2]{0:T(128)S(1)} %copy-done.3, bf16[1024,1024]{1,0:T(8,128)(2,1)} %q_hbm.7, bf16[1024,2560]{1,0:T(8,128)(2,1)} %copy-done, bf16[1536,512]{1,0:T(8,128)(2,1)} %collective-permute-done.4.w_ref, f32[2,512]{1,0:T(2,128)S(1)} %copy-done.1, bf16[1024,1024]{1,0:T(8,128)(2,1)} %value_hbm.7, ...), custom_call_target="tpu_custom_call" | custom-call | tf_op jit(solution)/shard_map/pallas_call | solution.py:368
  227.9 0.0 collective-permute-done.2.refs_0_
  227.9 5.0 %shard_map.94.refs_2_.a_ref = bf16[512,512]{1,0:T(8,128)(2,1)S(1)} custom-call(s32[2]{0:T(128)S(1)} %copy-done.3, bf16[1024,1024]{1,0:T(8,128)(2,1)} %q_hbm.7, bf16[1024,2560]{1,0:T(8,128)(2,1)} %copy-done, bf16[1536,512]{1,0:T(8,128)(2,1)} %shard_map.91.w_ref, f32[2,512]{1,0:T(2,128)S(1)} %copy-done.1, bf16[1024,1024]{1,0:T(8,128)(2,1)} %value_hbm.7, ...), custom_call_target="tpu_custom_call" | custom-call | tf_op jit(solution)/shard_map/pallas_call | solution.py:368
  232.9 1.8 collective-permute-start.5
  234.7 1.8 collective-permute-start.9
  236.5 5.0 %shard_map.95.b_ref = bf16[512,512]{1,0:T(8,128)(2,1)S(1)} custom-call(s32[2]{0:T(128)S(1)} %copy-done.3, bf16[1024,1024]{1,0:T(8,128)(2,1)} %q_hbm.7, bf16[1024,2560]{1,0:T(8,128)(2,1)} %copy-done, bf16[1536,512]{1,0:T(8,128)(2,1)} %collective-permute-done.4.w_ref, f32[2,512]{1,0:T(2,128)S(1)} %copy-done.1, bf16[1024,1024]{1,0:T(8,128)(2,1)} %value_hbm.7, ...), custom_call_target="tpu_custom_call" | custom-call | tf_op jit(solution)/shard_map/pallas_call | solution.py:368
  241.5 1.8 collective-permute-start.7
  243.3 46.3 %collective-permute-done.6.wc_ref.wa_ref = bf16[1024,1024]{1,0:T(8,128)(2,1)S(1)} collective-permute-done((bf16[1024,1024]{1,0:T(8,128)(2,1)}, bf16[1024,1024]{1,0:T(8,128)(2,1)S(1)}, u32[]{:S(2)}, u32[]{:S(2)}) %collective-permute-start.6) | collective-permute-done | bytes 2097184 | tf_op jit(solution)/shard_map/ppermute | solution.py:504
  289.5 0.0 collective-permute-done.8.c_ref
  289.5 3.9 %project.3.acc_ref = f32[512,1024]{1,0:T(8,128)S(1)} custom-call(s32[2]{0:T(128)S(1)} %copy-done.3, bf16[512,512]{1,0:T(8,128)(2,1)S(1)} %shard_map.92.refs_1_.a_ref, bf16[512,512]{1,0:T(8,128)(2,1)S(1)} %shard_map.93.refs_2_.b_ref, bf16[512,512]{1,0:T(8,128)(2,1)S(1)} %collective-permute-done.8.c_ref, bf16[1024,2048]{1,0:T(8,128)(2,1)} %wb_ref.3, ...), custom_call_target="tpu_custom_call" | custom-call | tf_op jit(solution)/shard_map/project/pallas_call | solution.py:398
  293.4 0.0 collective-permute-done.5.c_ref
  293.4 3.9 %project.2.acc_ref = f32[512,1024]{1,0:T(8,128)S(1)} custom-call(s32[2]{0:T(128)S(1)} %copy-done.3, bf16[512,512]{1,0:T(8,128)(2,1)S(1)} %shard_map.94.refs_2_.a_ref, bf16[512,512]{1,0:T(8,128)(2,1)S(1)} %shard_map.95.b_ref, bf16[512,512]{1,0:T(8,128)(2,1)S(1)} %collective-permute-done.5.c_ref, bf16[1024,2048]{1,0:T(8,128)(2,1)} %wb_ref.3, ...), custom_call_target="tpu_custom_call" | custom-call | tf_op jit(solution)/shard_map/project/pallas_call | solution.py:398
  297.4 0.0 collective-permute-done.9.a_ref
  297.4 2.3 shard_map.96.refs_0_
  299.6 0.0 collective-permute-done.7.a_ref
  299.6 2.3 shard_map.97
Async XLA Ops:
  7.5 7.6 %collective-permute-start.1 = (bf16[32,48,512]{2,1,0:T(8,128)(2,1)S(1)}, bf16[32,48,512]{2,1,0:T(8,128)(2,1)S(1)}, u32[]{:S(2)}, u32[]{:S(2)}) collective-permute-start(bf16[32,48,512]{2,1,0:T(8,128)(2,1)S(1)} %head_grads.3), channel_id=1, source_target_pairs={{0,1},{1,0},{2,3},{3,2},{4,5},{5,4},{6,7},{7,6},{8,9},{9,8},{10,11... | collective-permute-start | bytes 4718600 | tf_op jit(solution)/shard_map/ppermute | solution.py:445
  7.6 7.4 %copy-start.2 = (s32[2]{0:T(128)}, s32[2]{0:T(128)S(1)}, u32[]{:S(2)}) copy-start(s32[2]{0:T(128)S(1)} %pad_add_fusion.where.w) | copy-start | bytes 28
  50.5 135.5 %all-to-all-start.1 = ((bf16[32,48,512]{2,1,0:T(8,128)(2,1)}), bf16[32,48,512]{2,1,0:T(8,128)(2,1)S(1)}, u32[]{:S(2)}, u32[]{:S(2)}) async-start(bf16[32,48,512]{2,1,0:T(8,128)(2,1)} %broadcast_in_dim.2), calls=%async_computation.1 | async-start | bytes 3145728 | tf_op jit(solution)/shard_map/all_to_all | solution.py:450
  54.4 131.5 %copy-start.3 = (s32[2]{0:T(128)S(1)}, s32[2]{0:T(128)}, u32[]{:S(2)}) copy-start(s32[2]{0:T(128)} %copy-done.2) | copy-start | bytes 28
  54.4 148.9 %collective-permute-start = (bf16[1024,1024]{1,0:T(8,128)(2,1)}, bf16[1024,1024]{1,0:T(8,128)(2,1)}, u32[]{:S(2)}, u32[]{:S(2)}) collective-permute-start(bf16[1024,1024]{1,0:T(8,128)(2,1)} %k_hbm.3), channel_id=1, source_target_pairs={{0,1},{1,2},{2,3},{3,4},{4,5},{5,6},{6,7},{7,8},{8,9},{9,10},{10,1... | collective-permute-start | bytes 6291464 | tf_op jit(solution)/shard_map/ppermute | solution.py:497
  194.2 28.7 %collective-permute-start.4 = (bf16[1536,512]{1,0:T(8,128)(2,1)}, bf16[1536,512]{1,0:T(8,128)(2,1)}, u32[]{:S(2)}, u32[]{:S(2)}) collective-permute-start(bf16[1536,512]{1,0:T(8,128)(2,1)} %shard_map.91.w_ref), channel_id=1, source_target_pairs={{0,1},{1,0},{2,3},{3,2},{4,5},{5,4},{6,7},{7,6},{8,9},{9,8},{10,11... | collective-permute-start | bytes 4718600 | tf_op jit(solution)/shard_map/ppermute | solution.py:445
  195.5 94.0 %collective-permute-start.6 = (bf16[1024,1024]{1,0:T(8,128)(2,1)}, bf16[1024,1024]{1,0:T(8,128)(2,1)S(1)}, u32[]{:S(2)}, u32[]{:S(2)}) collective-permute-start(bf16[1024,1024]{1,0:T(8,128)(2,1)} %get-tuple-element.10), channel_id=1, source_target_pairs={{0,66},{1,67},{2,64},{3,65},{4,70},{5,71},{6,68},{7,69},{8,74},{9,... | collective-permute-start | bytes 6291464 | tf_op jit(solution)/shard_map/ppermute | solution.py:504
  198.4 17.4 %collective-permute-start.3 = (bf16[512,1024]{1,0:T(8,128)(2,1)}, bf16[512,1024]{1,0:T(8,128)(2,1)S(1)}, u32[]{:S(2)}, u32[]{:S(2)}) collective-permute-start(bf16[512,1024]{1,0:T(8,128)(2,1)} %get-tuple-element.9), channel_id=1, source_target_pairs={{0,1},{1,2},{2,3},{3,4},{4,5},{5,6},{6,7},{7,8},{8,9},{9,10},{10,1... | collective-permute-start | bytes 3145736 | tf_op jit(solution)/shard_map/ppermute | solution.py:499
  200.2 27.7 %collective-permute-start.2 = (bf16[512,1024]{1,0:T(8,128)(2,1)}, bf16[512,1024]{1,0:T(8,128)(2,1)}, u32[]{:S(2)}, u32[]{:S(2)}) collective-permute-start(bf16[512,1024]{1,0:T(8,128)(2,1)} %get-tuple-element.8), channel_id=1, source_target_pairs={{0,1},{1,2},{2,3},{3,4},{4,5},{5,6},{6,7},{7,8},{8,9},{9,10},{10,1... | collective-permute-start | bytes 3145736 | tf_op jit(solution)/shard_map/ppermute | solution.py:500
  203.3 12.5 %copy-start.1 = (f32[2,512]{1,0:T(2,128)S(1)}, f32[2,512]{1,0:T(2,128)}, u32[]{:S(2)}) copy-start(f32[2,512]{1,0:T(2,128)} %gain_ref.7) | copy-start | bytes 12292
  213.5 2.3 copy-start
  220.8 68.7 %collective-permute-start.8 = (bf16[512,512]{1,0:T(8,128)(2,1)S(1)}, bf16[512,512]{1,0:T(8,128)(2,1)S(1)}, u32[]{:S(2)}, u32[]{:S(2)}) collective-permute-start(bf16[512,512]{1,0:T(8,128)(2,1)S(1)} %shard_map.92.refs_1_.a_ref), channel_id=1, source_target_pairs={{0,64},{64,0},{1,65},{65,1},{2,66},{66,2},{3,67},{67,3},{4,68},{68... | collective-permute-start | bytes 1572872 | tf_op jit(solution)/shard_map/ppermute | solution.py:528
  232.9 60.5 %collective-permute-start.5 = (bf16[512,512]{1,0:T(8,128)(2,1)S(1)}, bf16[512,512]{1,0:T(8,128)(2,1)S(1)}, u32[]{:S(2)}, u32[]{:S(2)}) collective-permute-start(bf16[512,512]{1,0:T(8,128)(2,1)S(1)} %shard_map.94.refs_2_.a_ref), channel_id=1, source_target_pairs={{0,64},{64,0},{1,65},{65,1},{2,66},{66,2},{3,67},{67,3},{4,68},{68... | collective-permute-start | bytes 1572872 | tf_op jit(solution)/shard_map/ppermute | solution.py:528
  234.7 62.7 %collective-permute-start.9 = (bf16[512,512]{1,0:T(8,128)(2,1)S(1)}, bf16[512,512]{1,0:T(8,128)(2,1)S(1)}, u32[]{:S(2)}, u32[]{:S(2)}) collective-permute-start(bf16[512,512]{1,0:T(8,128)(2,1)S(1)} %shard_map.93.refs_2_.b_ref), channel_id=1, source_target_pairs={{0,64},{64,0},{1,65},{65,1},{2,66},{66,2},{3,67},{67,3},{4,68},{68... | collective-permute-start | bytes 1572872 | tf_op jit(solution)/shard_map/ppermute | solution.py:528
  241.5 58.2 %collective-permute-start.7 = (bf16[512,512]{1,0:T(8,128)(2,1)S(1)}, bf16[512,512]{1,0:T(8,128)(2,1)S(1)}, u32[]{:S(2)}, u32[]{:S(2)}) collective-permute-start(bf16[512,512]{1,0:T(8,128)(2,1)S(1)} %shard_map.95.b_ref), channel_id=1, source_target_pairs={{0,64},{64,0},{1,65},{65,1},{2,66},{66,2},{3,67},{67,3},{4,68},{68... | collective-permute-start | bytes 1572872 | tf_op jit(solution)/shard_map/ppermute | solution.py:528

commit v5 on v3

--- a/solution.py
+++ b/solution.py
@@ -142,19 +142,29 @@
     )(which, keys, values, rates, gate, lift, down)
 
 
-def renew_body(where, g_ref, gate_ref, lift_ref, down_ref, out_ref, olds, sems):
+def renew_body(where, g_hbm, gate_ref, lift_ref, down_ref, out_ref, g_ref, olds, sems):
+    loads = [
+        pltpu.make_async_copy(
+            g_hbm.at[pl.ds(i * HEAD, HEAD)], g_ref.at[pl.ds(i * HEAD, HEAD)], sems.at[3 + i]
+        )
+        for i in range(3)
+    ]
+    for load in loads:
+        load.start()
     copies = [
         pltpu.make_async_copy(ref.at[where[0]], olds.at[i], sems.at[i])
         for i, ref in enumerate((gate_ref, lift_ref, down_ref))
     ]
-    for copy in copies:
-        copy.start()
     eye = (
         lax.broadcasted_iota(jnp.int32, (HEAD, HEAD), 0)
         == lax.broadcasted_iota(jnp.int32, (HEAD, HEAD), 1)
     ).astype(F32)
     iterates, grams = [], []
     for i in range(3):
+        loads[i].wait()
+        if i == 2:
+            for copy in copies:
+                copy.start()
         g = g_ref[i * HEAD : (i + 1) * HEAD, :]
         wide = g.astype(F32)
         gram = dot_on(g, g, COL_BY_COL)
@@ -191,13 +201,111 @@
         grid_spec=pltpu.PrefetchScalarGridSpec(
             num_scalar_prefetch=1,
             grid=(1,),
-            in_specs=[vmem_spec(), any_spec(), any_spec(), any_spec()],
+            in_specs=[any_spec(), any_spec(), any_spec(), any_spec()],
             out_specs=vmem_spec(),
-            scratch_shapes=[pltpu.VMEM((3, HEAD, HEAD), F32), pltpu.SemaphoreType.DMA((3,))],
+            scratch_shapes=[
+                pltpu.VMEM((3 * HEAD, HEAD), BF),
+                pltpu.VMEM((3, HEAD, HEAD), F32),
+                pltpu.SemaphoreType.DMA((6,)),
+            ],
         ),
         compiler_params=pltpu.CompilerParams(vmem_limit_bytes=24 * MIB),
         name="renewed_weights",
     )(which, grads, gate, lift, down)
+
+
+def cut_blocks(where, out_weight, values):
+    columns = out_weight.shape[1] // 2
+    rows = values.shape[0] // 2
+
+    def body(w, weight_ref, value_ref, weight_out, late_out, early_out, weight, value, sems):
+        other = pl.ds(pl.multiple_of((1 - w[1]) * columns, columns), columns)
+        low, high = pl.ds(0, rows), pl.ds(rows, rows)
+        moves = (
+            (weight_ref.at[:, other], weight, weight_out),
+            (value_ref.at[high], value.at[high], late_out),
+            (value_ref.at[low], value.at[low], early_out),
+        )
+        into = [pltpu.make_async_copy(a, b, sems.at[0, n]) for n, (a, b, _) in enumerate(moves)]
+        back = [pltpu.make_async_copy(b, c, sems.at[1, n]) for n, (_, b, c) in enumerate(moves)]
+        for copy in into:
+            copy.start()
+        for first, second in zip(into, back):
+            first.wait()
+            second.start()
+        for copy in back:
+            copy.wait()
+
+    width = values.shape[1]
+    return pl.pallas_call(
+        body,
+        out_shape=(
+            pltpu.HBM((out_weight.shape[0], columns), BF),
+            pltpu.HBM((rows, width), BF),
+            pltpu.HBM((rows, width), BF),
+        ),
+        grid_spec=pltpu.PrefetchScalarGridSpec(
+            num_scalar_prefetch=1,
+            grid=(1,),
+            in_specs=[any_spec(), any_spec()],
+            out_specs=[any_spec(), any_spec(), any_spec()],
+            scratch_shapes=[
+                pltpu.VMEM((out_weight.shape[0], columns), BF),
+                pltpu.VMEM(values.shape, BF),
+                pltpu.SemaphoreType.DMA((2, 3)),
+            ],
+        ),
+        compiler_params=pltpu.CompilerParams(vmem_limit_bytes=8 * MIB),
+        name="cut_blocks",
+    )(where, out_weight, values)
+
+
+def add_blocks(mine, got):
+    parts = 4
+    rows = mine.shape[0] // parts
+
+    def body(mine_ref, got_ref, out_hbm, held, sems):
+        copies = []
+        for n in range(parts):
+            here = slice(n * rows, (n + 1) * rows)
+            held[here, :] = (mine_ref[here, :] + got_ref[here, :].astype(F32)).astype(BF)
+            where = pl.ds(n * rows, rows)
+            copies.append(pltpu.make_async_copy(held.at[where], out_hbm.at[where], sems.at[n]))
+            copies[-1].start()
+        for copy in copies:
+            copy.wait()
+
+    return pl.pallas_call(
+        body,
+        out_shape=pltpu.HBM(mine.shape, BF),
+        in_specs=[vmem_spec(), vmem_spec()],
+        out_specs=any_spec(),
+        scratch_shapes=[pltpu.VMEM(mine.shape, BF), pltpu.SemaphoreType.DMA((parts,))],
+        compiler_params=pltpu.CompilerParams(vmem_limit_bytes=8 * MIB),
+        name="add_blocks",
+    )(mine, got)
+
+
+def add_and_repeat(part, other):
+    def body(part_ref, other_ref, out_hbm, held, sems):
+        held[...] = (part_ref[...].astype(F32) + other_ref[...].astype(F32)).astype(BF)
+        copies = [
+            pltpu.make_async_copy(held, out_hbm.at[n], sems.at[n]) for n in range(PLANES)
+        ]
+        for copy in copies:
+            copy.start()
+        for copy in copies:
+            copy.wait()
+
+    return pl.pallas_call(
+        body,
+        out_shape=pltpu.HBM((PLANES, *part.shape), BF),
+        in_specs=[vmem_spec(), vmem_spec()],
+        out_specs=any_spec(),
+        scratch_shapes=[pltpu.VMEM(part.shape, BF), pltpu.SemaphoreType.DMA((PLANES,))],
+        compiler_params=pltpu.CompilerParams(vmem_limit_bytes=4 * MIB),
+        name="add_and_repeat",
+    )(part, other)
 
 
 SPAN = WINDOW + CHUNK
@@ -274,12 +382,12 @@
     )(has_edge, queries, edge_keys, keys)
 
 
-PIECE = 2 * CHUNK
-
-
-def combined_piece(at, mirror, where, queries, probability, weights, gain, edges, values, after):
-    from_edge = sum(edge.shape[0] for edge in edges)
-    from_own = (at + 1) * PIECE
+def combined_piece(start, rows, mirror, where, queries, probability, weights, gain, edges, values, after):
+    half = WINDOW // 2
+    from_edge = WINDOW - start
+    from_own = start + rows
+    edge_rows = ((start, half), (0, half)) if start < half else ((start - half, half),)
+    edges = edges[-len(edge_rows) :]
 
     def head_of(w):
         return 1 - w[0] if mirror else w[0]
@@ -289,17 +397,17 @@
         head = head_of(w)
         column = pl.ds(pl.multiple_of(head * HEAD, HEAD), HEAD)
         chances = pl.ds(pl.multiple_of(head * SPAN, SPAN), SPAN)
-        rows = pl.ds(at * PIECE, PIECE)
+        here = pl.ds(start, rows)
         moves = [
-            (q_hbm.at[rows, column], q_ref),
-            (p_hbm.at[rows, chances], p_ref),
+            (q_hbm.at[here, column], q_ref),
+            (p_hbm.at[here, chances], p_ref),
             (value_hbm.at[pl.ds(0, from_own), column], span.at[pl.ds(from_edge, from_own)]),
         ]
-        start = 0
-        for edge in edge_hbm:
-            count = edge.shape[0]
-            moves.append((edge.at[:, column], span.at[pl.ds(start, count)]))
-            start += count
+        filled = 0
+        for edge, (first, last) in zip(edge_hbm, edge_rows):
+            count = last - first
+            moves.append((edge.at[pl.ds(first, count), column], span.at[pl.ds(filled, count)]))
+            filled += count
         copies = [
             pltpu.make_async_copy(source, target, sems.at[n])
             for n, (source, target) in enumerate(moves)
@@ -317,14 +425,14 @@
         normed = out * lax.rsqrt(mean_square + EPSILON) * scale
         for copy in copies[1:]:
             copy.wait()
-        for part in range(PIECE // CHUNK):
-            rows = slice(part * CHUNK, (part + 1) * CHUNK)
-            attended = dot(p_ref[rows, :], span[part * CHUNK : part * CHUNK + SPAN, :])
-            out_ref[rows, :] = (attended + normed[rows, :]).astype(BF)
+        for part in range(rows // CHUNK):
+            some = slice(part * CHUNK, (part + 1) * CHUNK)
+            attended = dot(p_ref[some, :], span[part * CHUNK : part * CHUNK + SPAN, :])
+            out_ref[some, :] = (attended + normed[some, :]).astype(BF)
 
     return pl.pallas_call(
         body,
-        out_shape=jax.ShapeDtypeStruct((PIECE, HEAD), BF),
+        out_shape=jax.ShapeDtypeStruct((rows, HEAD), BF),
         grid_spec=pltpu.PrefetchScalarGridSpec(
             num_scalar_prefetch=1,
             grid=(1,),
@@ -332,9 +440,9 @@
             + [any_spec()] * (len(edges) + len(after)),
             out_specs=vmem_spec(),
             scratch_shapes=[
-                pltpu.VMEM((PIECE, HEAD), BF),
-                pltpu.VMEM((PIECE, SPAN), BF),
-                pltpu.VMEM((WINDOW + PIECE, HEAD), BF),
+                pltpu.VMEM((rows, HEAD), BF),
+                pltpu.VMEM((rows, SPAN), BF),
+                pltpu.VMEM((WINDOW + rows, HEAD), BF),
                 pltpu.SemaphoreType.DMA((3 + len(edges),)),
             ],
         ),
@@ -342,59 +450,75 @@
     )(where, queries, probability, weights, gain, values, *edges, *after)
 
 
-def project_piece(where, combined, first_arrived, out_weight, other_weight):
+def project_chunk(where, operands, out_weight, other_weight, after):
     columns = out_weight.shape[1] // 2
     step = columns // 2
 
-    def body(w, a_ref, b_ref, c_ref, wa_ref, wb_ref, wc_ref, out_ref):
-        out_ref[...] = (
+    def body(w, a_ref, b_ref, c_ref, wa_ref, wb_ref, wc_ref, *refs):
+        refs[-1][...] = (
             dot(a_ref[...], wa_ref[...]) + dot(b_ref[...], wb_ref[...]) + dot(c_ref[...], wc_ref[...])
         )
 
-    rows = pl.BlockSpec((PIECE, HEAD), lambda i, w: (0, 0))
+    def rows(block):
+        return pl.BlockSpec((CHUNK, HEAD), lambda i, w: (block, 0))
+
     return pl.pallas_call(
         body,
-        out_shape=jax.ShapeDtypeStruct((PIECE, columns), F32),
+        out_shape=jax.ShapeDtypeStruct((CHUNK, columns), F32),
         grid_spec=pltpu.PrefetchScalarGridSpec(
             num_scalar_prefetch=1,
             grid=(2,),
-            in_specs=[
-                rows,
-                rows,
-                rows,
+            in_specs=[rows(block) for _, block in operands]
+            + [
                 pl.BlockSpec((HEAD, step), lambda i, w: (w[0], 2 * w[1] + i)),
                 pl.BlockSpec((HEAD, step), lambda i, w: (1 - w[0], 2 * w[1] + i)),
                 pl.BlockSpec((HEAD, step), lambda i, w: (w[0], i)),
-            ],
-            out_specs=pl.BlockSpec((PIECE, step), lambda i, w: (0, i)),
+            ]
+            + [any_spec()] * len(after),
+            out_specs=pl.BlockSpec((CHUNK, step), lambda i, w: (0, i)),
         ),
         compiler_params=pltpu.CompilerParams(vmem_limit_bytes=16 * MIB),
         name="project",
-    )(where, *combined, first_arrived, out_weight, out_weight, other_weight)
-
-
-def finish_piece(at, tokens, where, partial, last_arrived, other_weight, before):
+    )(where, *(array for array, _ in operands), out_weight, out_weight, other_weight, *after)
+
+
+def finish_chunk(at, tokens, where, partial, arrived, block, other_weight, before):
     columns = partial.shape[1]
-    step = columns // 2
+    parts = 2
+    step = columns // parts
+    held = () if before is None else (before,)
 
     def body(w, acc_ref, a_ref, wa_ref, *refs):
-        here = pl.ds(pl.multiple_of(pl.program_id(0) * step, step), step)
+        out_hbm, done, sems = refs[-3:]
         rows = pl.ds(pl.multiple_of((1 - w[0]) * HEAD, HEAD), HEAD)
-        refs[-1][...] = (acc_ref[:, here] + dot(a_ref[...], wa_ref[rows, here])).astype(BF)
-
-    held = () if before is None else (before,)
+        came = a_ref[block * CHUNK : (block + 1) * CHUNK, :]
+        copies = []
+        for n in range(parts):
+            here = slice(n * step, (n + 1) * step)
+            done[:, here] = (acc_ref[:, here] + dot(came, wa_ref[rows, here])).astype(BF)
+            some = pl.ds(n * step, step)
+            copies.append(
+                pltpu.make_async_copy(
+                    done.at[:, some], out_hbm.at[pl.ds(at * CHUNK, CHUNK), some], sems.at[n]
+                )
+            )
+            copies[-1].start()
+        for copy in copies:
+            copy.wait()
+
     return pl.pallas_call(
         body,
         out_shape=jax.ShapeDtypeStruct((tokens, columns), BF),
         grid_spec=pltpu.PrefetchScalarGridSpec(
             num_scalar_prefetch=1,
-            grid=(2,),
+            grid=(1,),
             in_specs=[vmem_spec(), vmem_spec(), vmem_spec()] + [any_spec()] * len(held),
-            out_specs=pl.BlockSpec((PIECE, step), lambda i, w: (at, i)),
+            out_specs=any_spec(),
+            scratch_shapes=[pltpu.VMEM((CHUNK, columns), BF), pltpu.SemaphoreType.DMA((parts,))],
         ),
         compiler_params=pltpu.CompilerParams(vmem_limit_bytes=12 * MIB),
         input_output_aliases={4: 0} if held else {},
-    )(where, partial, last_arrived, other_weight, *held)
+    )(where, partial, arrived, other_weight, *held)
 
 
 def partner(value, flip):
@@ -418,7 +542,6 @@
     memory_gain,
     out_weight,
 ):
-    raw_out_weight, raw_values = out_weight, value_rows
     queries, key_rows, value_rows, token_rates, gate_fast, lift_fast, down_fast, out_weight = (
         pltpu.with_memory_space_constraint(x, pltpu.HBM)
         for x in (
@@ -449,57 +572,69 @@
     count = lax.axis_size("seq")
     along = [(i, i + 1) for i in range(count - 1)]
     edge_keys = lax.ppermute(key_rows, "seq", along)
-    edge_late = lax.ppermute(raw_values[PIECE:], "seq", along)
-    edge_early = lax.ppermute(raw_values[:PIECE], "seq", along)
-
-    chip_sum = (grads_mine + grads_got.astype(F32)).astype(BF)
+    other_columns, late, early = cut_blocks(where, out_weight, value_rows)
+    edge_late = lax.ppermute(late, "seq", along)
+    edge_early = lax.ppermute(early, "seq", along)
+    pairs = [
+        (group * count + i, (1 - group) * count + (i ^ 2)) for group in range(2) for i in range(count)
+    ]
+    other_weight = lax.ppermute(other_columns, ("head", "seq"), pairs)
+
+    chip_sum = add_blocks(grads_mine, grads_got)
     slices = over_planes(chip_sum.reshape(PLANES, -1, HEAD))
     part = slices.astype(F32).sum(axis=0).astype(BF)
     other = partner(part, 2)
-    part = (part.astype(F32) + other.astype(F32)).astype(BF)
-    spread = jnp.broadcast_to(part[None], (PLANES, *part.shape))
+    spread = add_and_repeat(part, other)
     grads = over_planes(spread).reshape(3 * HEAD, HEAD)
 
     weights_mine = renewed_weights(where, grads, *fast)
     weights_theirs = partner(weights_mine, 1)
-
-    columns = out_weight.shape[1] // 2
-    pairs = [
-        (group * count + i, (1 - group) * count + (i ^ 2)) for group in range(2) for i in range(count)
-    ]
-    other_weight = lax.ppermute(
-        lax.dynamic_slice(
-            raw_out_weight, (0, (1 - head) * columns), (out_weight.shape[0], columns)
-        ),
-        ("head", "seq"),
-        pairs,
-    )
 
     probability = pltpu.with_memory_space_constraint(
         probabilities(has_edge, queries, edge_keys, key_rows), pltpu.HBM
     )
 
-    pieces = tokens_here // PIECE
     head_pair = [(0, 1), (1, 0)]
+    half = tokens_here // 2
+    plan = (
+        (half, CHUNK, False),
+        (half + CHUNK, CHUNK, False),
+        (half, half, True),
+        (0, half, False),
+        (0, CHUNK, True),
+        (CHUNK, CHUNK, True),
+    )
     made, arrived, after = {}, {}, ()
-    for at in reversed(range(pieces)):
-        edges = (edge_late,) if at else (edge_early, edge_late)
-        for mirror, weights in ((False, weights_mine), (True, weights_theirs)):
-            piece = combined_piece(
-                at, mirror, where, queries, probability, weights, memory_gain, edges, value_rows, after
+    for start, rows, mirror in plan:
+        piece = combined_piece(
+            start,
+            rows,
+            mirror,
+            where,
+            queries,
+            probability,
+            weights_theirs if mirror else weights_mine,
+            memory_gain,
+            (edge_early, edge_late),
+            value_rows,
+            after,
+        )
+        after = (piece,)
+        came = lax.ppermute(piece, "head", head_pair)
+        for block in range(rows // CHUNK):
+            made[mirror, start // CHUNK + block] = (piece, block)
+            arrived[mirror, start // CHUNK + block] = (came, block)
+    out, after = None, ()
+    for pair in ((2, 3), (0, 1)):
+        partials = {}
+        for at in pair:
+            operands = (made[False, at], made[True, at], arrived[False, at])
+            partials[at] = project_chunk(where, operands, out_weight, other_weight, after)
+        for at in pair:
+            out = finish_chunk(
+                at, tokens_here, where, partials[at], *arrived[True, at], other_weight, out
             )
-            made[mirror, at], after = piece, (piece,)
-            arrived[mirror, at] = lax.ppermute(piece, "head", head_pair)
-    out = None
-    for at in reversed(range(pieces)):
-        partial = project_piece(
-            where,
-            (made[False, at], made[True, at]),
-            arrived[False, at],
-            out_weight,
-            other_weight,
-        )
-        out = finish_piece(at, tokens_here, where, partial, arrived[True, at], other_weight, out)
+        after = (out,)
     return out
 
 

time: 198 us -> 184 us (0.929)
  waiting for transfers between devices: 64 us -> 24.9 us
  Pallas kernels: 65.4 us -> 87.3 us
  starting transfers between devices: 26.1 us -> 33.6 us
  local copies, waits for them, and re-layouts: 8.2 us -> 3.88 us
    ppermute x7 -> x9, waiting for transfers between devices: 44.9 us -> 9.44 us  [the longest x6 9.43 us: shards(): came = lax.ppermute(piece, 'head', head_pair)]
    pallas_call x8 -> x17, Pallas kernels: 32.2 us -> 52.5 us  [the longest x6 26.7 us: combined_piece(): pl.pallas_call(body, out_shape=jax.ShapeDtypeStruct((rows, HEAD), BF), gr...]
    ppermute x7 -> x9, starting transfers between devices: 18 us -> 24.7 us  [the longest x6 13.3 us: shards(): came = lax.ppermute(piece, 'head', head_pair)]
    all_to_all x1, waiting for transfers between devices: 16.1 us -> 12.4 us  [over_planes(): lax.all_to_all(value, 'seq', 0, 0, tiled=True, axis_index_groups=groups)]
    dynamic_slice x1 -> x0, local copies, waits for them, and re-layouts: 3.08 us -> none  [shards(): lax.dynamic_slice(raw_out_weight, (0, (1 - head) * columns), (out_weight....]
  transfers between devices with their start and end apart: 12 -> 14, of which waited for: 3 -> 3; matrix products, arithmetic and copies ran while one was open for 2% -> 0% of each run, Pallas kernels for 28% -> 42%
where the time goes in v5:
time: 184 us; the launch traced here: 182 us
  Pallas kernels  87.3 us (47%)
  starting transfers between devices  33.6 us (18%)
  blocking collectives  31.5 us (17%)
  waiting for transfers between devices  24.9 us (14%)
  local copies, waits for them, and re-layouts  3.88 us (2%)
    all_to_all x1, blocking collectives, over_planes(): lax.all_to_all(value, 'seq', 0, 0, tiled=True, axis_index_groups=groups)  31.5 us
    pallas_call x6, Pallas kernels, combined_piece(): pl.pallas_call(body, out_shape=jax.ShapeDtypeStruct((rows, HEAD), BF), gr...  26.7 us
    pallas_call x2, Pallas kernels, head_grads(): pl.pallas_call(grads_body, out_shape=jax.ShapeDtypeStruct((3 * HEAD, HEAD...  14.7 us
    ppermute x6, starting transfers between devices, shards(): came = lax.ppermute(piece, 'head', head_pair)  13.3 us
    all_to_all x1, waiting for transfers between devices, over_planes(): lax.all_to_all(value, 'seq', 0, 0, tiled=True, axis_index_groups=groups)  12.4 us
    pallas_call x4, Pallas kernels, project_chunk(): pl.pallas_call(body, out_shape=jax.ShapeDtypeStruct((CHUNK, columns), F32...  12.2 us
    pallas_call x1, Pallas kernels, probabilities(): pl.pallas_call(scores_body, out_shape=jax.ShapeDtypeStruct((tokens, heads...  10.2 us
    pallas_call x1, Pallas kernels, renewed_weights(): pl.pallas_call(renew_body, out_shape=jax.ShapeDtypeStruct((3 * HEAD, HEAD...  9.82 us
  transfers between devices with their start and end apart: 14, of which 3 were waited for; matrix products, arithmetic and copies ran while one was open for 0% of the time, Pallas kernels for 42%

profile of v5, /device:TPU:0, one launch (start us, length us, event | category | flops | bytes accessed | tf_op | source)
XLA Modules:
  0.0 182.0 jit_solution(7749321051365095966)
XLA Ops:
  0.0 0.1 pad_add_fusion.1.where
  0.1 7.4 %head_grads.3 = bf16[1536,512]{1,0:T(8,128)(2,1)S(1)} custom-call(s32[2]{0:T(128)S(1)} %pad_add_fusion.1.where, bf16[1024,1024]{1,0:T(8,128)(2,1)} %k_hbm.3, bf16[1024,1024]{1,0:T(8,128)(2,1)} %value_hbm.11, f32[2,1024]{1,0:T(2,128)} %rate_ref.3, f32[2,512,512]{2,1,0:T(8,128)} %gate_ref.1, f32[2,512,512]{2,1,0:T(8,128)} %lift_ref.1, f32[2,512,512]{2,1,0:T(8,128)} %down_ref.1), custom_call_target="tpu_custom_call" | custom-call | tf_op jit(solution)/shard_map/head_grads/pallas_call | solution.py:118
  7.5 0.1 collective-permute-start.1
  7.5 0.1 pad_add_fusion.where.w
  7.6 7.4 %head_grads.2.mine_ref = f32[1536,512]{1,0:T(8,128)S(1)} custom-call(s32[2]{0:T(128)S(1)} %pad_add_fusion.where.w, bf16[1024,1024]{1,0:T(8,128)(2,1)} %k_hbm.3, bf16[1024,1024]{1,0:T(8,128)(2,1)} %value_hbm.11, f32[2,1024]{1,0:T(2,128)} %rate_ref.3, f32[2,512,512]{2,1,0:T(8,128)} %gate_ref.1, f32[2,512,512]{2,1,0:T(8,128)} %lift_ref.1, f32[2,512,512]{2,1,0:T(8,128)} %down_ref.1), custom_call_target="tpu_custom_call" | custom-call | tf_op jit(solution)/shard_map/head_grads/pallas_call | solution.py:118
  15.0 0.0 collective-permute-done.1.got_ref
  15.0 1.2 add_blocks.1
  16.3 31.5 %all_to_all.10 = bf16[16,96,512]{2,1,0:T(8,128)(2,1)S(1)} all-to-all(bf16[16,96,512]{2,1,0:T(8,128)(2,1)} %bitcast.6), channel_id=1, replica_groups={{0,4,8,12,16,20,24,28,32,36,40,44,48,52,56,60},{1,5,9,13,17,21,25,29,33..., dimensions={0} | all-to-all | bytes 3145728 | tf_op jit(solution)/shard_map/all_to_all | solution.py:531
  47.8 0.2 reduce_sum.12.part_ref
  48.0 1.7 collective-permute-start.2
  49.7 3.0 %collective-permute-done.2.other_ref = bf16[96,512]{1,0:T(8,128)(2,1)S(1)} collective-permute-done((bf16[96,512]{1,0:T(8,128)(2,1)S(1)}, bf16[96,512]{1,0:T(8,128)(2,1)S(1)}, u32[]{:S(2)}, u32[]{:S(2)}) %collective-permute-start.2) | collective-permute-done | bytes 98336 | tf_op jit(solution)/shard_map/ppermute | solution.py:526
  52.7 1.3 add_and_repeat.1
  54.0 4.4 %all-to-all-start.1 = ((bf16[16,96,512]{2,1,0:T(8,128)(2,1)}), bf16[16,96,512]{2,1,0:T(8,128)(2,1)}, u32[]{:S(2)}, u32[]{:S(2)}) async-start(bf16[16,96,512]{2,1,0:T(8,128)(2,1)} %add_and_repeat.1), calls=%async_computation.1 | async-start | bytes 3145728 | tf_op jit(solution)/shard_map/all_to_all | solution.py:531
  58.5 2.6 %collective-permute-start = (bf16[1024,1024]{1,0:T(8,128)(2,1)}, bf16[1024,1024]{1,0:T(8,128)(2,1)}, u32[]{:S(2)}, u32[]{:S(2)}) collective-permute-start(bf16[1024,1024]{1,0:T(8,128)(2,1)} %k_hbm.3), channel_id=1, source_target_pairs={{0,1},{1,2},{2,3},{3,4},{4,5},{5,6},{6,7},{7,8},{8,9},{9,10},{10,1... | collective-permute-start | bytes 6291464 | tf_op jit(solution)/shard_map/ppermute | solution.py:574
  61.1 4.2 %cut_blocks.1 = (bf16[1024,1024]{1,0:T(8,128)(2,1)}, bf16[512,1024]{1,0:T(8,128)(2,1)}, bf16[512,1024]{1,0:T(8,128)(2,1)}) custom-call(s32[2]{0:T(128)S(1)} %pad_add_fusion.where.w, bf16[1024,2048]{1,0:T(8,128)(2,1)} %wb_ref.7, bf16[1024,1024]{1,0:T(8,128)(2,1)} %value_hbm.11), custom_call_target="tpu_custom_call" | custom-call | tf_op jit(solution)/shard_map/cut_blocks/pallas_call | solution.py:240
  65.3 2.6 %collective-permute-start.7 = (bf16[1024,1024]{1,0:T(8,128)(2,1)}, bf16[1024,1024]{1,0:T(8,128)(2,1)S(1)}, u32[]{:S(2)}, u32[]{:S(2)}) collective-permute-start(bf16[1024,1024]{1,0:T(8,128)(2,1)} %get-tuple-element.10), channel_id=1, source_target_pairs={{0,66},{1,67},{2,64},{3,65},{4,70},{5,71},{6,68},{7,69},{8,74},{9,... | collective-permute-start | bytes 6291464 | tf_op jit(solution)/shard_map/ppermute | solution.py:581
  67.9 12.4 %all-to-all-done.1 = bf16[16,96,512]{2,1,0:T(8,128)(2,1)} async-done(((bf16[16,96,512]{2,1,0:T(8,128)(2,1)}), bf16[16,96,512]{2,1,0:T(8,128)(2,1)}, u32[]{:S(2)}, u32[]{:S(2)}) %all-to-all-start.1) | async-done | bytes 1572896 | tf_op jit(solution)/shard_map/all_to_all | solution.py:531
  80.3 9.8 %renewed_weights.1.w_ref = bf16[1536,512]{1,0:T(8,128)(2,1)} custom-call(s32[2]{0:T(128)S(1)} %pad_add_fusion.where.w, bf16[1536,512]{1,0:T(8,128)(2,1)} %bitcast.5.g_hbm, f32[2,512,512]{2,1,0:T(8,128)} %gate_ref.1, f32[2,512,512]{2,1,0:T(8,128)} %lift_ref.1, f32[2,512,512]{2,1,0:T(8,128)} %down_ref.1), custom_call_target="tpu_custom_call" | custom-call | tf_op jit(solution)/shard_map/renewed_weights/pallas_call | solution.py:198
  90.1 0.1 collective-permute-start.5
  90.2 2.5 %collective-permute-start.4 = (bf16[512,1024]{1,0:T(8,128)(2,1)}, bf16[512,1024]{1,0:T(8,128)(2,1)S(1)}, u32[]{:S(2)}, u32[]{:S(2)}) collective-permute-start(bf16[512,1024]{1,0:T(8,128)(2,1)} %get-tuple-element.9), channel_id=1, source_target_pairs={{0,1},{1,2},{2,3},{3,4},{4,5},{5,6},{6,7},{7,8},{8,9},{9,10},{10,1... | collective-permute-start | bytes 3145736 | tf_op jit(solution)/shard_map/ppermute | solution.py:576
  92.7 6.4 %collective-permute-start.3 = (bf16[512,1024]{1,0:T(8,128)(2,1)}, bf16[512,1024]{1,0:T(8,128)(2,1)}, u32[]{:S(2)}, u32[]{:S(2)}) collective-permute-start(bf16[512,1024]{1,0:T(8,128)(2,1)} %get-tuple-element.8), channel_id=1, source_target_pairs={{0,1},{1,2},{2,3},{3,4},{4,5},{5,6},{6,7},{7,8},{8,9},{9,10},{10,1... | collective-permute-start | bytes 3145736 | tf_op jit(solution)/shard_map/ppermute | solution.py:577
  99.0 0.0 collective-permute-done.edge_ref
  99.0 0.0 copy-start.2
  99.0 10.2 %probabilities.1.p_hbm = bf16[1024,2560]{1,0:T(8,128)(2,1)S(1)} custom-call(s32[1]{0:T(128)} %bitcast.2.flag, bf16[1024,1024]{1,0:T(8,128)(2,1)} %q_hbm.11, bf16[1024,1024]{1,0:T(8,128)(2,1)} %collective-permute-done.edge_ref, bf16[1024,1024]{1,0:T(8,128)(2,1)} %k_hbm.3), custom_call_target="tpu_custom_call" | custom-call | tf_op jit(solution)/shard_map/probabilities/pallas_call | solution.py:361
  109.2 0.0 copy-start
  109.2 2.3 %copy-done = bf16[1024,2560]{1,0:T(8,128)(2,1)} copy-done((bf16[1024,2560]{1,0:T(8,128)(2,1)}, bf16[1024,2560]{1,0:T(8,128)(2,1)S(1)}, u32[]{:S(2)}) %copy-start) | copy-done | bytes 5242904
  111.5 0.0 collective-permute-done.4.refs_0_.refs_1_
  111.5 0.0 copy-done.2
  111.5 4.2 %shard_map.91.refs_1_.a_ref = bf16[256,512]{1,0:T(8,128)(2,1)S(1)} custom-call(s32[2]{0:T(128)S(1)} %pad_add_fusion.where.w, bf16[1024,1024]{1,0:T(8,128)(2,1)} %q_hbm.11, bf16[1024,2560]{1,0:T(8,128)(2,1)} %copy-done, bf16[1536,512]{1,0:T(8,128)(2,1)} %renewed_weights.1.w_ref, f32[2,512]{1,0:T(2,128)S(1)} %copy-done.2, bf16[1024,1024]{1,0:T(8,128)(2,1)} %value_hbm.11, ...), custom_call_target="tpu_custom_call" | custom-call | tf_op jit(solution)/shard_map/pallas_call | solution.py:433
  115.7 4.2 %shard_map.92.refs_1_.a_ref = bf16[256,512]{1,0:T(8,128)(2,1)S(1)} custom-call(s32[2]{0:T(128)S(1)} %pad_add_fusion.where.w, bf16[1024,1024]{1,0:T(8,128)(2,1)} %q_hbm.11, bf16[1024,2560]{1,0:T(8,128)(2,1)} %copy-done, bf16[1536,512]{1,0:T(8,128)(2,1)} %renewed_weights.1.w_ref, f32[2,512]{1,0:T(2,128)S(1)} %copy-done.2, bf16[1024,1024]{1,0:T(8,128)(2,1)} %value_hbm.11, ...), custom_call_target="tpu_custom_call" | custom-call | tf_op jit(solution)/shard_map/pallas_call | solution.py:433
  119.9 0.0 collective-permute-done.5.w_ref
  119.9 5.0 %shard_map.93.refs_2_.b_ref = bf16[512,512]{1,0:T(8,128)(2,1)S(1)} custom-call(s32[2]{0:T(128)S(1)} %pad_add_fusion.where.w, bf16[1024,1024]{1,0:T(8,128)(2,1)} %q_hbm.11, bf16[1024,2560]{1,0:T(8,128)(2,1)} %copy-done, bf16[1536,512]{1,0:T(8,128)(2,1)} %collective-permute-done.5.w_ref, f32[2,512]{1,0:T(2,128)S(1)} %copy-done.2, ...), custom_call_target="tpu_custom_call" | custom-call | tf_op jit(solution)/shard_map/pallas_call | solution.py:433
  124.9 3.0 %collective-permute-start.9 = (bf16[512,512]{1,0:T(8,128)(2,1)S(1)}, bf16[512,512]{1,0:T(8,128)(2,1)S(1)}, u32[]{:S(2)}, u32[]{:S(2)}) collective-permute-start(bf16[512,512]{1,0:T(8,128)(2,1)S(1)} %shard_map.93.refs_2_.b_ref), channel_id=1, source_target_pairs={{0,64},{64,0},{1,65},{65,1},{2,66},{66,2},{3,67},{67,3},{4,68},{68... | collective-permute-start | bytes 1572872 | tf_op jit(solution)/shard_map/ppermute | solution.py:623
  127.9 0.0 collective-permute-done.3.refs_0_
  127.9 5.0 %shard_map.94.refs_2_.a_ref = bf16[512,512]{1,0:T(8,128)(2,1)S(1)} custom-call(s32[2]{0:T(128)S(1)} %pad_add_fusion.where.w, bf16[1024,1024]{1,0:T(8,128)(2,1)} %q_hbm.11, bf16[1024,2560]{1,0:T(8,128)(2,1)} %copy-done, bf16[1536,512]{1,0:T(8,128)(2,1)} %renewed_weights.1.w_ref, f32[2,512]{1,0:T(2,128)S(1)} %copy-done.2, bf16[1024,1024]{1,0:T(8,128)(2,1)} %value_hbm.11, ...), custom_call_target="tpu_custom_call" | custom-call | tf_op jit(solution)/shard_map/pallas_call | solution.py:433
  132.9 0.9 collective-permute-start.6
  133.8 2.9 %collective-permute-start.8 = (bf16[256,512]{1,0:T(8,128)(2,1)S(1)}, bf16[256,512]{1,0:T(8,128)(2,1)S(1)}, u32[]{:S(2)}, u32[]{:S(2)}) collective-permute-start(bf16[256,512]{1,0:T(8,128)(2,1)S(1)} %shard_map.92.refs_1_.a_ref), channel_id=1, source_target_pairs={{0,64},{64,0},{1,65},{65,1},{2,66},{66,2},{3,67},{67,3},{4,68},{68... | collective-permute-start | bytes 786440 | tf_op jit(solution)/shard_map/ppermute | solution.py:623
  136.7 0.6 collective-permute-start.10
  137.3 4.2 %shard_map.95.refs_2_.b_ref = bf16[256,512]{1,0:T(8,128)(2,1)S(1)} custom-call(s32[2]{0:T(128)S(1)} %pad_add_fusion.where.w, bf16[1024,1024]{1,0:T(8,128)(2,1)} %q_hbm.11, bf16[1024,2560]{1,0:T(8,128)(2,1)} %copy-done, bf16[1536,512]{1,0:T(8,128)(2,1)} %collective-permute-done.5.w_ref, f32[2,512]{1,0:T(2,128)S(1)} %copy-done.2, ...), custom_call_target="tpu_custom_call" | custom-call | tf_op jit(solution)/shard_map/pallas_call | solution.py:433
  141.5 4.2 %shard_map.96.b_ref = bf16[256,512]{1,0:T(8,128)(2,1)S(1)} custom-call(s32[2]{0:T(128)S(1)} %pad_add_fusion.where.w, bf16[1024,1024]{1,0:T(8,128)(2,1)} %q_hbm.11, bf16[1024,2560]{1,0:T(8,128)(2,1)} %copy-done, bf16[1536,512]{1,0:T(8,128)(2,1)} %collective-permute-done.5.w_ref, f32[2,512]{1,0:T(2,128)S(1)} %copy-done.2, bf16[1024,1024]{1,0:T(8,128)(2,1)} %value_hbm.11, ...), custom_call_target="tpu_custom_call" | custom-call | tf_op jit(solution)/shard_map/pallas_call | solution.py:433
  145.7 0.0 collective-permute-done.7.wc_ref.wa_ref
  145.8 3.0 %collective-permute-start.12 = (bf16[256,512]{1,0:T(8,128)(2,1)S(1)}, bf16[256,512]{1,0:T(8,128)(2,1)S(1)}, u32[]{:S(2)}, u32[]{:S(2)}) collective-permute-start(bf16[256,512]{1,0:T(8,128)(2,1)S(1)} %shard_map.95.refs_2_.b_ref), channel_id=1, source_target_pairs={{0,64},{64,0},{1,65},{65,1},{2,66},{66,2},{3,67},{67,3},{4,68},{68... | collective-permute-start | bytes 786440 | tf_op jit(solution)/shard_map/ppermute | solution.py:623
  148.7 9.4 %collective-permute-done.8.c_ref = bf16[256,512]{1,0:T(8,128)(2,1)S(1)} collective-permute-done((bf16[256,512]{1,0:T(8,128)(2,1)S(1)}, bf16[256,512]{1,0:T(8,128)(2,1)S(1)}, u32[]{:S(2)}, u32[]{:S(2)}) %collective-permute-start.8) | collective-permute-done | bytes 262176 | tf_op jit(solution)/shard_map/ppermute | solution.py:623
  158.1 2.9 %collective-permute-start.11 = (bf16[256,512]{1,0:T(8,128)(2,1)S(1)}, bf16[256,512]{1,0:T(8,128)(2,1)S(1)}, u32[]{:S(2)}, u32[]{:S(2)}) collective-permute-start(bf16[256,512]{1,0:T(8,128)(2,1)S(1)} %shard_map.96.b_ref), channel_id=1, source_target_pairs={{0,64},{64,0},{1,65},{65,1},{2,66},{66,2},{3,67},{67,3},{4,68},{68... | collective-permute-start | bytes 786440 | tf_op jit(solution)/shard_map/ppermute | solution.py:623
  161.0 3.0 %project.4.acc_ref = f32[256,1024]{1,0:T(8,128)S(1)} custom-call(s32[2]{0:T(128)S(1)} %pad_add_fusion.where.w, bf16[256,512]{1,0:T(8,128)(2,1)S(1)} %shard_map.92.refs_1_.a_ref, bf16[512,512]{1,0:T(8,128)(2,1)S(1)} %shard_map.93.refs_2_.b_ref, bf16[256,512]{1,0:T(8,128)(2,1)S(1)} %collective-permute-done.8.c_ref, bf16[1024,2048]{1,0:T(8,128)(2,1)} %wb_ref.7, ...), custom_call_target="tpu_custom_call" | custom-call | tf_op jit(solution)/shard_map/project/pallas_call | solution.py:465
  164.1 0.0 collective-permute-done.10.c_ref
  164.1 3.1 %project.5.acc_ref = f32[256,1024]{1,0:T(8,128)S(1)} custom-call(s32[2]{0:T(128)S(1)} %pad_add_fusion.where.w, bf16[256,512]{1,0:T(8,128)(2,1)S(1)} %shard_map.91.refs_1_.a_ref, bf16[512,512]{1,0:T(8,128)(2,1)S(1)} %shard_map.93.refs_2_.b_ref, bf16[256,512]{1,0:T(8,128)(2,1)S(1)} %collective-permute-done.10.c_ref, bf16[1024,2048]{1,0:T(8,128)(2,1)} %wb_ref.7, ...), custom_call_target="tpu_custom_call" | custom-call | tf_op jit(solution)/shard_map/project/pallas_call | solution.py:465
  167.2 0.0 collective-permute-done.9.a_ref
  167.2 1.7 shard_map.97.refs_0_
  168.9 1.7 shard_map.98.refs_0_
  170.6 0.0 collective-permute-done.6.c_ref
  170.6 0.0 copy-start.1
  170.6 1.6 copy-done.1
  172.2 3.0 %project.6.acc_ref = f32[256,1024]{1,0:T(8,128)S(1)} custom-call(s32[2]{0:T(128)S(1)} %pad_add_fusion.where.w, bf16[512,512]{1,0:T(8,128)(2,1)S(1)} %shard_map.94.refs_2_.a_ref, bf16[256,512]{1,0:T(8,128)(2,1)S(1)} %shard_map.96.b_ref, bf16[512,512]{1,0:T(8,128)(2,1)S(1)} %collective-permute-done.6.c_ref, bf16[1024,2048]{1,0:T(8,128)(2,1)} %wb_ref.7, ...), custom_call_target="tpu_custom_call" | custom-call | tf_op jit(solution)/shard_map/project/pallas_call | solution.py:465
  175.3 3.1 %project.7.acc_ref = f32[256,1024]{1,0:T(8,128)S(1)} custom-call(s32[2]{0:T(128)S(1)} %pad_add_fusion.where.w, bf16[512,512]{1,0:T(8,128)(2,1)S(1)} %shard_map.94.refs_2_.a_ref, bf16[256,512]{1,0:T(8,128)(2,1)S(1)} %shard_map.95.refs_2_.b_ref, bf16[512,512]{1,0:T(8,128)(2,1)S(1)} %collective-permute-done.6.c_ref, bf16[1024,2048]{1,0:T(8,128)(2,1)} %wb_ref.7, ...), custom_call_target="tpu_custom_call" | custom-call | tf_op jit(solution)/shard_map/project/pallas_call | solution.py:465
  178.3 0.0 collective-permute-done.12.a_ref
  178.4 1.7 shard_map.99.refs_0_
  180.1 0.0 collective-permute-done.11.a_ref
  180.1 1.7 shard_map.100
Async XLA Ops:
  7.5 7.6 %collective-permute-start.1 = (bf16[1536,512]{1,0:T(8,128)(2,1)S(1)}, bf16[1536,512]{1,0:T(8,128)(2,1)S(1)}, u32[]{:S(2)}, u32[]{:S(2)}) collective-permute-start(bf16[1536,512]{1,0:T(8,128)(2,1)S(1)} %head_grads.3), channel_id=1, source_target_pairs={{0,1},{1,0},{2,3},{3,2},{4,5},{5,4},{6,7},{7,6},{8,9},{9,8},{10,11... | collective-permute-start | bytes 4718600 | tf_op jit(solution)/shard_map/ppermute | solution.py:526
  48.0 4.7 %collective-permute-start.2 = (bf16[96,512]{1,0:T(8,128)(2,1)S(1)}, bf16[96,512]{1,0:T(8,128)(2,1)S(1)}, u32[]{:S(2)}, u32[]{:S(2)}) collective-permute-start(bf16[96,512]{1,0:T(8,128)(2,1)S(1)} %reduce_sum.12.part_ref), channel_id=1, source_target_pairs={{0,2},{1,3},{2,0},{3,1},{4,6},{5,7},{6,4},{7,5},{8,10},{9,11},{10,... | collective-permute-start | bytes 294920 | tf_op jit(solution)/shard_map/ppermute | solution.py:526
  54.0 26.3 %all-to-all-start.1 = ((bf16[16,96,512]{2,1,0:T(8,128)(2,1)}), bf16[16,96,512]{2,1,0:T(8,128)(2,1)}, u32[]{:S(2)}, u32[]{:S(2)}) async-start(bf16[16,96,512]{2,1,0:T(8,128)(2,1)} %add_and_repeat.1), calls=%async_computation.1 | async-start | bytes 3145728 | tf_op jit(solution)/shard_map/all_to_all | solution.py:531
  58.5 40.6 %collective-permute-start = (bf16[1024,1024]{1,0:T(8,128)(2,1)}, bf16[1024,1024]{1,0:T(8,128)(2,1)}, u32[]{:S(2)}, u32[]{:S(2)}) collective-permute-start(bf16[1024,1024]{1,0:T(8,128)(2,1)} %k_hbm.3), channel_id=1, source_target_pairs={{0,1},{1,2},{2,3},{3,4},{4,5},{5,6},{6,7},{7,8},{8,9},{9,10},{10,1... | collective-permute-start | bytes 6291464 | tf_op jit(solution)/shard_map/ppermute | solution.py:574
  65.3 80.5 %collective-permute-start.7 = (bf16[1024,1024]{1,0:T(8,128)(2,1)}, bf16[1024,1024]{1,0:T(8,128)(2,1)S(1)}, u32[]{:S(2)}, u32[]{:S(2)}) collective-permute-start(bf16[1024,1024]{1,0:T(8,128)(2,1)} %get-tuple-element.10), channel_id=1, source_target_pairs={{0,66},{1,67},{2,64},{3,65},{4,70},{5,71},{6,68},{7,69},{8,74},{9,... | collective-permute-start | bytes 6291464 | tf_op jit(solution)/shard_map/ppermute | solution.py:581
  90.1 29.8 %collective-permute-start.5 = (bf16[1536,512]{1,0:T(8,128)(2,1)}, bf16[1536,512]{1,0:T(8,128)(2,1)}, u32[]{:S(2)}, u32[]{:S(2)}) collective-permute-start(bf16[1536,512]{1,0:T(8,128)(2,1)} %renewed_weights.1.w_ref), channel_id=1, source_target_pairs={{0,1},{1,0},{2,3},{3,2},{4,5},{5,4},{6,7},{7,6},{8,9},{9,8},{10,11... | collective-permute-start | bytes 4718600 | tf_op jit(solution)/shard_map/ppermute | solution.py:526
  90.2 21.3 %collective-permute-start.4 = (bf16[512,1024]{1,0:T(8,128)(2,1)}, bf16[512,1024]{1,0:T(8,128)(2,1)S(1)}, u32[]{:S(2)}, u32[]{:S(2)}) collective-permute-start(bf16[512,1024]{1,0:T(8,128)(2,1)} %get-tuple-element.9), channel_id=1, source_target_pairs={{0,1},{1,2},{2,3},{3,4},{4,5},{5,6},{6,7},{7,8},{8,9},{9,10},{10,1... | collective-permute-start | bytes 3145736 | tf_op jit(solution)/shard_map/ppermute | solution.py:576
  92.7 35.2 %collective-permute-start.3 = (bf16[512,1024]{1,0:T(8,128)(2,1)}, bf16[512,1024]{1,0:T(8,128)(2,1)}, u32[]{:S(2)}, u32[]{:S(2)}) collective-permute-start(bf16[512,1024]{1,0:T(8,128)(2,1)} %get-tuple-element.8), channel_id=1, source_target_pairs={{0,1},{1,2},{2,3},{3,4},{4,5},{5,6},{6,7},{7,8},{8,9},{9,10},{10,1... | collective-permute-start | bytes 3145736 | tf_op jit(solution)/shard_map/ppermute | solution.py:577
  99.0 12.5 %copy-start.2 = (f32[2,512]{1,0:T(2,128)S(1)}, f32[2,512]{1,0:T(2,128)}, u32[]{:S(2)}) copy-start(f32[2,512]{1,0:T(2,128)} %gain_ref.11) | copy-start | bytes 12292
  109.2 2.3 %copy-start = (bf16[1024,2560]{1,0:T(8,128)(2,1)}, bf16[1024,2560]{1,0:T(8,128)(2,1)S(1)}, u32[]{:S(2)}) copy-start(bf16[1024,2560]{1,0:T(8,128)(2,1)S(1)} %probabilities.1.p_hbm) | copy-start | bytes 15728644
  124.9 42.3 %collective-permute-start.9 = (bf16[512,512]{1,0:T(8,128)(2,1)S(1)}, bf16[512,512]{1,0:T(8,128)(2,1)S(1)}, u32[]{:S(2)}, u32[]{:S(2)}) collective-permute-start(bf16[512,512]{1,0:T(8,128)(2,1)S(1)} %shard_map.93.refs_2_.b_ref), channel_id=1, source_target_pairs={{0,64},{64,0},{1,65},{65,1},{2,66},{66,2},{3,67},{67,3},{4,68},{68... | collective-permute-start | bytes 1572872 | tf_op jit(solution)/shard_map/ppermute | solution.py:623
  132.9 37.8 %collective-permute-start.6 = (bf16[512,512]{1,0:T(8,128)(2,1)S(1)}, bf16[512,512]{1,0:T(8,128)(2,1)S(1)}, u32[]{:S(2)}, u32[]{:S(2)}) collective-permute-start(bf16[512,512]{1,0:T(8,128)(2,1)S(1)} %shard_map.94.refs_2_.a_ref), channel_id=1, source_target_pairs={{0,64},{64,0},{1,65},{65,1},{2,66},{66,2},{3,67},{67,3},{4,68},{68... | collective-permute-start | bytes 1572872 | tf_op jit(solution)/shard_map/ppermute | solution.py:623
  133.8 24.3 %collective-permute-start.8 = (bf16[256,512]{1,0:T(8,128)(2,1)S(1)}, bf16[256,512]{1,0:T(8,128)(2,1)S(1)}, u32[]{:S(2)}, u32[]{:S(2)}) collective-permute-start(bf16[256,512]{1,0:T(8,128)(2,1)S(1)} %shard_map.92.refs_1_.a_ref), channel_id=1, source_target_pairs={{0,64},{64,0},{1,65},{65,1},{2,66},{66,2},{3,67},{67,3},{4,68},{68... | collective-permute-start | bytes 786440 | tf_op jit(solution)/shard_map/ppermute | solution.py:623
  136.7 27.4 %collective-permute-start.10 = (bf16[256,512]{1,0:T(8,128)(2,1)S(1)}, bf16[256,512]{1,0:T(8,128)(2,1)S(1)}, u32[]{:S(2)}, u32[]{:S(2)}) collective-permute-start(bf16[256,512]{1,0:T(8,128)(2,1)S(1)} %shard_map.91.refs_1_.a_ref), channel_id=1, source_target_pairs={{0,64},{64,0},{1,65},{65,1},{2,66},{66,2},{3,67},{67,3},{4,68},{68... | collective-permute-start | bytes 786440 | tf_op jit(solution)/shard_map/ppermute | solution.py:623
  145.8 32.6 %collective-permute-start.12 = (bf16[256,512]{1,0:T(8,128)(2,1)S(1)}, bf16[256,512]{1,0:T(8,128)(2,1)S(1)}, u32[]{:S(2)}, u32[]{:S(2)}) collective-permute-start(bf16[256,512]{1,0:T(8,128)(2,1)S(1)} %shard_map.95.refs_2_.b_ref), channel_id=1, source_target_pairs={{0,64},{64,0},{1,65},{65,1},{2,66},{66,2},{3,67},{67,3},{4,68},{68... | collective-permute-start | bytes 786440 | tf_op jit(solution)/shard_map/ppermute | solution.py:623
  158.1 21.9 %collective-permute-start.11 = (bf16[256,512]{1,0:T(8,128)(2,1)S(1)}, bf16[256,512]{1,0:T(8,128)(2,1)S(1)}, u32[]{:S(2)}, u32[]{:S(2)}) collective-permute-start(bf16[256,512]{1,0:T(8,128)(2,1)S(1)} %shard_map.96.b_ref), channel_id=1, source_target_pairs={{0,64},{64,0},{1,65},{65,1},{2,66},{66,2},{3,67},{67,3},{4,68},{68... | collective-permute-start | bytes 786440 | tf_op jit(solution)/shard_map/ppermute | solution.py:623
  170.6 1.6 copy-start.1

commit v6 on v5

--- a/solution.py
+++ b/solution.py
@@ -39,7 +39,7 @@
 
 
 def sigmoid(x):
-    return 0.5 * jnp.tanh(0.5 * x) + 0.5
+    return 1.0 / (1.0 + jnp.exp(-x))
 
 
 def vmem_spec():
@@ -286,6 +286,35 @@
     )(mine, got)
 
 
+def sum_planes(slices):
+    parts = 4
+    step = PLANES // parts
+
+    def body(slices_hbm, out_ref, held, sems):
+        copies = []
+        for n in range(parts):
+            some = pl.ds(n * step, step)
+            copies.append(pltpu.make_async_copy(slices_hbm.at[some], held.at[some], sems.at[n]))
+            copies[-1].start()
+        total = None
+        for n in range(parts):
+            copies[n].wait()
+            for m in range(n * step, (n + 1) * step):
+                plane = held[m].astype(F32)
+                total = plane if total is None else total + plane
+        out_ref[...] = total.astype(BF)
+
+    return pl.pallas_call(
+        body,
+        out_shape=jax.ShapeDtypeStruct(slices.shape[1:], BF),
+        in_specs=[any_spec()],
+        out_specs=vmem_spec(),
+        scratch_shapes=[pltpu.VMEM(slices.shape, BF), pltpu.SemaphoreType.DMA((parts,))],
+        compiler_params=pltpu.CompilerParams(vmem_limit_bytes=8 * MIB),
+        name="sum_planes",
+    )(slices)
+
+
 def add_and_repeat(part, other):
     def body(part_ref, other_ref, out_hbm, held, sems):
         held[...] = (part_ref[...].astype(F32) + other_ref[...].astype(F32)).astype(BF)
@@ -582,7 +611,7 @@
 
     chip_sum = add_blocks(grads_mine, grads_got)
     slices = over_planes(chip_sum.reshape(PLANES, -1, HEAD))
-    part = slices.astype(F32).sum(axis=0).astype(BF)
+    part = sum_planes(slices)
     other = partner(part, 2)
     spread = add_and_repeat(part, other)
     grads = over_planes(spread).reshape(3 * HEAD, HEAD)

time: 184 us -> 185 us (level)
  transfers between devices with their start and end apart: 14 -> 14, of which waited for: 3 -> 3; matrix products, arithmetic and copies ran while one was open for 0% -> 0% of each run, Pallas kernels for 42% -> 41%
where the time goes in v6:
time: 185 us; the launch traced here: 183 us
  Pallas kernels  88.4 us (48%)
  starting transfers between devices  33.6 us (18%)
  blocking collectives  31.5 us (17%)
  waiting for transfers between devices  25 us (14%)
  local copies, waits for them, and re-layouts  3.89 us (2%)
    all_to_all x1, blocking collectives, over_planes(): lax.all_to_all(value, 'seq', 0, 0, tiled=True, axis_index_groups=groups)  31.5 us
    pallas_call x6, Pallas kernels, combined_piece(): pl.pallas_call(body, out_shape=jax.ShapeDtypeStruct((rows, HEAD), BF), gr...  26.9 us
    pallas_call x2, Pallas kernels, head_grads(): pl.pallas_call(grads_body, out_shape=jax.ShapeDtypeStruct((3 * HEAD, HEAD...  14.7 us
    ppermute x6, starting transfers between devices, shards(): came = lax.ppermute(piece, 'head', head_pair)  13.3 us
    all_to_all x1, waiting for transfers between devices, over_planes(): lax.all_to_all(value, 'seq', 0, 0, tiled=True, axis_index_groups=groups)  12.4 us
    pallas_call x4, Pallas kernels, project_chunk(): pl.pallas_call(body, out_shape=jax.ShapeDtypeStruct((CHUNK, columns), F32...  12.2 us
    pallas_call x1, Pallas kernels, probabilities(): pl.pallas_call(scores_body, out_shape=jax.ShapeDtypeStruct((tokens, heads...  10.2 us
    pallas_call x1, Pallas kernels, renewed_weights(): pl.pallas_call(renew_body, out_shape=jax.ShapeDtypeStruct((3 * HEAD, HEAD...  9.82 us
  transfers between devices with their start and end apart: 14, of which 3 were waited for; matrix products, arithmetic and copies ran while one was open for 0% of the time, Pallas kernels for 41%

profile of v6, /device:TPU:0, one launch (start us, length us, event | category | flops | bytes accessed | tf_op | source)
XLA Modules:
  0.0 183.1 jit_solution(16900964457671271166)
XLA Ops:
  0.0 0.1 pad_add_fusion.1.where
  0.1 7.3 %head_grads.3 = bf16[1536,512]{1,0:T(8,128)(2,1)S(1)} custom-call(s32[2]{0:T(128)S(1)} %pad_add_fusion.1.where, bf16[1024,1024]{1,0:T(8,128)(2,1)} %k_hbm.3, bf16[1024,1024]{1,0:T(8,128)(2,1)} %value_hbm.11, f32[2,1024]{1,0:T(2,128)} %rate_ref.3, f32[2,512,512]{2,1,0:T(8,128)} %gate_ref.1, f32[2,512,512]{2,1,0:T(8,128)} %lift_ref.1, f32[2,512,512]{2,1,0:T(8,128)} %down_ref.1), custom_call_target="tpu_custom_call" | custom-call | tf_op jit(solution)/shard_map/head_grads/pallas_call | solution.py:118
  7.4 0.1 collective-permute-start.1
  7.5 0.1 pad_add_fusion.where.w
  7.6 7.3 %head_grads.2.mine_ref = f32[1536,512]{1,0:T(8,128)S(1)} custom-call(s32[2]{0:T(128)S(1)} %pad_add_fusion.where.w, bf16[1024,1024]{1,0:T(8,128)(2,1)} %k_hbm.3, bf16[1024,1024]{1,0:T(8,128)(2,1)} %value_hbm.11, f32[2,1024]{1,0:T(2,128)} %rate_ref.3, f32[2,512,512]{2,1,0:T(8,128)} %gate_ref.1, f32[2,512,512]{2,1,0:T(8,128)} %lift_ref.1, f32[2,512,512]{2,1,0:T(8,128)} %down_ref.1), custom_call_target="tpu_custom_call" | custom-call | tf_op jit(solution)/shard_map/head_grads/pallas_call | solution.py:118
  14.9 0.0 collective-permute-done.1.got_ref
  15.0 1.2 add_blocks.1
  16.2 31.5 %all_to_all.10.slices_hbm = bf16[16,96,512]{2,1,0:T(8,128)(2,1)S(1)} all-to-all(bf16[16,96,512]{2,1,0:T(8,128)(2,1)} %bitcast.6), channel_id=1, replica_groups={{0,4,8,12,16,20,24,28,32,36,40,44,48,52,56,60},{1,5,9,13,17,21,25,29,33..., dimensions={0} | all-to-all | bytes 3145728 | tf_op jit(solution)/shard_map/all_to_all | solution.py:560
  47.7 1.0 sum_planes.1.part_ref
  48.8 1.7 collective-permute-start.2
  50.4 3.0 %collective-permute-done.2.other_ref = bf16[96,512]{1,0:T(8,128)(2,1)S(1)} collective-permute-done((bf16[96,512]{1,0:T(8,128)(2,1)S(1)}, bf16[96,512]{1,0:T(8,128)(2,1)S(1)}, u32[]{:S(2)}, u32[]{:S(2)}) %collective-permute-start.2) | collective-permute-done | bytes 98336 | tf_op jit(solution)/shard_map/ppermute | solution.py:555
  53.5 1.3 add_and_repeat.1
  54.8 4.4 %all-to-all-start.1 = ((bf16[16,96,512]{2,1,0:T(8,128)(2,1)}), bf16[16,96,512]{2,1,0:T(8,128)(2,1)}, u32[]{:S(2)}, u32[]{:S(2)}) async-start(bf16[16,96,512]{2,1,0:T(8,128)(2,1)} %add_and_repeat.1), calls=%async_computation.1 | async-start | bytes 3145728 | tf_op jit(solution)/shard_map/all_to_all | solution.py:560
  59.2 2.6 %collective-permute-start = (bf16[1024,1024]{1,0:T(8,128)(2,1)}, bf16[1024,1024]{1,0:T(8,128)(2,1)}, u32[]{:S(2)}, u32[]{:S(2)}) collective-permute-start(bf16[1024,1024]{1,0:T(8,128)(2,1)} %k_hbm.3), channel_id=1, source_target_pairs={{0,1},{1,2},{2,3},{3,4},{4,5},{5,6},{6,7},{7,8},{8,9},{9,10},{10,1... | collective-permute-start | bytes 6291464 | tf_op jit(solution)/shard_map/ppermute | solution.py:603
  61.9 4.2 %cut_blocks.1 = (bf16[1024,1024]{1,0:T(8,128)(2,1)}, bf16[512,1024]{1,0:T(8,128)(2,1)}, bf16[512,1024]{1,0:T(8,128)(2,1)}) custom-call(s32[2]{0:T(128)S(1)} %pad_add_fusion.where.w, bf16[1024,2048]{1,0:T(8,128)(2,1)} %wb_ref.7, bf16[1024,1024]{1,0:T(8,128)(2,1)} %value_hbm.11), custom_call_target="tpu_custom_call" | custom-call | tf_op jit(solution)/shard_map/cut_blocks/pallas_call | solution.py:240
  66.1 2.6 %collective-permute-start.7 = (bf16[1024,1024]{1,0:T(8,128)(2,1)}, bf16[1024,1024]{1,0:T(8,128)(2,1)S(1)}, u32[]{:S(2)}, u32[]{:S(2)}) collective-permute-start(bf16[1024,1024]{1,0:T(8,128)(2,1)} %get-tuple-element.10), channel_id=1, source_target_pairs={{0,66},{1,67},{2,64},{3,65},{4,70},{5,71},{6,68},{7,69},{8,74},{9,... | collective-permute-start | bytes 6291464 | tf_op jit(solution)/shard_map/ppermute | solution.py:610
  68.6 12.4 %all-to-all-done.1 = bf16[16,96,512]{2,1,0:T(8,128)(2,1)} async-done(((bf16[16,96,512]{2,1,0:T(8,128)(2,1)}), bf16[16,96,512]{2,1,0:T(8,128)(2,1)}, u32[]{:S(2)}, u32[]{:S(2)}) %all-to-all-start.1) | async-done | bytes 1572896 | tf_op jit(solution)/shard_map/all_to_all | solution.py:560
  81.1 9.8 %renewed_weights.1.w_ref = bf16[1536,512]{1,0:T(8,128)(2,1)} custom-call(s32[2]{0:T(128)S(1)} %pad_add_fusion.where.w, bf16[1536,512]{1,0:T(8,128)(2,1)} %bitcast.5.g_hbm, f32[2,512,512]{2,1,0:T(8,128)} %gate_ref.1, f32[2,512,512]{2,1,0:T(8,128)} %lift_ref.1, f32[2,512,512]{2,1,0:T(8,128)} %down_ref.1), custom_call_target="tpu_custom_call" | custom-call | tf_op jit(solution)/shard_map/renewed_weights/pallas_call | solution.py:198
  90.9 0.1 collective-permute-start.5
  91.0 2.5 %collective-permute-start.4 = (bf16[512,1024]{1,0:T(8,128)(2,1)}, bf16[512,1024]{1,0:T(8,128)(2,1)S(1)}, u32[]{:S(2)}, u32[]{:S(2)}) collective-permute-start(bf16[512,1024]{1,0:T(8,128)(2,1)} %get-tuple-element.9), channel_id=1, source_target_pairs={{0,1},{1,2},{2,3},{3,4},{4,5},{5,6},{6,7},{7,8},{8,9},{9,10},{10,1... | collective-permute-start | bytes 3145736 | tf_op jit(solution)/shard_map/ppermute | solution.py:605
  93.4 6.4 %collective-permute-start.3 = (bf16[512,1024]{1,0:T(8,128)(2,1)}, bf16[512,1024]{1,0:T(8,128)(2,1)}, u32[]{:S(2)}, u32[]{:S(2)}) collective-permute-start(bf16[512,1024]{1,0:T(8,128)(2,1)} %get-tuple-element.8), channel_id=1, source_target_pairs={{0,1},{1,2},{2,3},{3,4},{4,5},{5,6},{6,7},{7,8},{8,9},{9,10},{10,1... | collective-permute-start | bytes 3145736 | tf_op jit(solution)/shard_map/ppermute | solution.py:606
  99.8 0.0 collective-permute-done.edge_ref
  99.8 0.0 copy-start.2
  99.8 10.2 %probabilities.1.p_hbm = bf16[1024,2560]{1,0:T(8,128)(2,1)S(1)} custom-call(s32[1]{0:T(128)} %bitcast.2.flag, bf16[1024,1024]{1,0:T(8,128)(2,1)} %q_hbm.11, bf16[1024,1024]{1,0:T(8,128)(2,1)} %collective-permute-done.edge_ref, bf16[1024,1024]{1,0:T(8,128)(2,1)} %k_hbm.3), custom_call_target="tpu_custom_call" | custom-call | tf_op jit(solution)/shard_map/probabilities/pallas_call | solution.py:390
  110.0 0.0 copy-start
  110.0 2.3 %copy-done = bf16[1024,2560]{1,0:T(8,128)(2,1)} copy-done((bf16[1024,2560]{1,0:T(8,128)(2,1)}, bf16[1024,2560]{1,0:T(8,128)(2,1)S(1)}, u32[]{:S(2)}) %copy-start) | copy-done | bytes 5242904
  112.3 0.0 collective-permute-done.4.refs_0_.refs_1_
  112.3 0.0 copy-done.2
  112.3 4.2 %shard_map.91.refs_1_.a_ref = bf16[256,512]{1,0:T(8,128)(2,1)S(1)} custom-call(s32[2]{0:T(128)S(1)} %pad_add_fusion.where.w, bf16[1024,1024]{1,0:T(8,128)(2,1)} %q_hbm.11, bf16[1024,2560]{1,0:T(8,128)(2,1)} %copy-done, bf16[1536,512]{1,0:T(8,128)(2,1)} %renewed_weights.1.w_ref, f32[2,512]{1,0:T(2,128)S(1)} %copy-done.2, bf16[1024,1024]{1,0:T(8,128)(2,1)} %value_hbm.11, ...), custom_call_target="tpu_custom_call" | custom-call | tf_op jit(solution)/shard_map/pallas_call | solution.py:462
  116.5 4.2 %shard_map.92.refs_1_.a_ref = bf16[256,512]{1,0:T(8,128)(2,1)S(1)} custom-call(s32[2]{0:T(128)S(1)} %pad_add_fusion.where.w, bf16[1024,1024]{1,0:T(8,128)(2,1)} %q_hbm.11, bf16[1024,2560]{1,0:T(8,128)(2,1)} %copy-done, bf16[1536,512]{1,0:T(8,128)(2,1)} %renewed_weights.1.w_ref, f32[2,512]{1,0:T(2,128)S(1)} %copy-done.2, bf16[1024,1024]{1,0:T(8,128)(2,1)} %value_hbm.11, ...), custom_call_target="tpu_custom_call" | custom-call | tf_op jit(solution)/shard_map/pallas_call | solution.py:462
  120.7 0.0 collective-permute-done.5.w_ref
  120.7 5.1 %shard_map.93.refs_2_.b_ref = bf16[512,512]{1,0:T(8,128)(2,1)S(1)} custom-call(s32[2]{0:T(128)S(1)} %pad_add_fusion.where.w, bf16[1024,1024]{1,0:T(8,128)(2,1)} %q_hbm.11, bf16[1024,2560]{1,0:T(8,128)(2,1)} %copy-done, bf16[1536,512]{1,0:T(8,128)(2,1)} %collective-permute-done.5.w_ref, f32[2,512]{1,0:T(2,128)S(1)} %copy-done.2, ...), custom_call_target="tpu_custom_call" | custom-call | tf_op jit(solution)/shard_map/pallas_call | solution.py:462
  125.8 3.2 %collective-permute-start.9 = (bf16[512,512]{1,0:T(8,128)(2,1)S(1)}, bf16[512,512]{1,0:T(8,128)(2,1)S(1)}, u32[]{:S(2)}, u32[]{:S(2)}) collective-permute-start(bf16[512,512]{1,0:T(8,128)(2,1)S(1)} %shard_map.93.refs_2_.b_ref), channel_id=1, source_target_pairs={{0,64},{64,0},{1,65},{65,1},{2,66},{66,2},{3,67},{67,3},{4,68},{68... | collective-permute-start | bytes 1572872 | tf_op jit(solution)/shard_map/ppermute | solution.py:652
  129.0 0.0 collective-permute-done.3.refs_0_
  129.0 5.1 %shard_map.94.refs_2_.a_ref = bf16[512,512]{1,0:T(8,128)(2,1)S(1)} custom-call(s32[2]{0:T(128)S(1)} %pad_add_fusion.where.w, bf16[1024,1024]{1,0:T(8,128)(2,1)} %q_hbm.11, bf16[1024,2560]{1,0:T(8,128)(2,1)} %copy-done, bf16[1536,512]{1,0:T(8,128)(2,1)} %renewed_weights.1.w_ref, f32[2,512]{1,0:T(2,128)S(1)} %copy-done.2, bf16[1024,1024]{1,0:T(8,128)(2,1)} %value_hbm.11, ...), custom_call_target="tpu_custom_call" | custom-call | tf_op jit(solution)/shard_map/pallas_call | solution.py:462
  134.0 0.7 collective-permute-start.6
  134.8 2.9 %collective-permute-start.8 = (bf16[256,512]{1,0:T(8,128)(2,1)S(1)}, bf16[256,512]{1,0:T(8,128)(2,1)S(1)}, u32[]{:S(2)}, u32[]{:S(2)}) collective-permute-start(bf16[256,512]{1,0:T(8,128)(2,1)S(1)} %shard_map.92.refs_1_.a_ref), channel_id=1, source_target_pairs={{0,64},{64,0},{1,65},{65,1},{2,66},{66,2},{3,67},{67,3},{4,68},{68... | collective-permute-start | bytes 786440 | tf_op jit(solution)/shard_map/ppermute | solution.py:652
  137.7 0.6 collective-permute-start.10
  138.3 4.2 %shard_map.95.refs_2_.b_ref = bf16[256,512]{1,0:T(8,128)(2,1)S(1)} custom-call(s32[2]{0:T(128)S(1)} %pad_add_fusion.where.w, bf16[1024,1024]{1,0:T(8,128)(2,1)} %q_hbm.11, bf16[1024,2560]{1,0:T(8,128)(2,1)} %copy-done, bf16[1536,512]{1,0:T(8,128)(2,1)} %collective-permute-done.5.w_ref, f32[2,512]{1,0:T(2,128)S(1)} %copy-done.2, ...), custom_call_target="tpu_custom_call" | custom-call | tf_op jit(solution)/shard_map/pallas_call | solution.py:462
  142.5 4.2 %shard_map.96.b_ref = bf16[256,512]{1,0:T(8,128)(2,1)S(1)} custom-call(s32[2]{0:T(128)S(1)} %pad_add_fusion.where.w, bf16[1024,1024]{1,0:T(8,128)(2,1)} %q_hbm.11, bf16[1024,2560]{1,0:T(8,128)(2,1)} %copy-done, bf16[1536,512]{1,0:T(8,128)(2,1)} %collective-permute-done.5.w_ref, f32[2,512]{1,0:T(2,128)S(1)} %copy-done.2, bf16[1024,1024]{1,0:T(8,128)(2,1)} %value_hbm.11, ...), custom_call_target="tpu_custom_call" | custom-call | tf_op jit(solution)/shard_map/pallas_call | solution.py:462
  146.7 0.0 collective-permute-done.7.wc_ref.wa_ref
  146.7 3.0 %collective-permute-start.12 = (bf16[256,512]{1,0:T(8,128)(2,1)S(1)}, bf16[256,512]{1,0:T(8,128)(2,1)S(1)}, u32[]{:S(2)}, u32[]{:S(2)}) collective-permute-start(bf16[256,512]{1,0:T(8,128)(2,1)S(1)} %shard_map.95.refs_2_.b_ref), channel_id=1, source_target_pairs={{0,64},{64,0},{1,65},{65,1},{2,66},{66,2},{3,67},{67,3},{4,68},{68... | collective-permute-start | bytes 786440 | tf_op jit(solution)/shard_map/ppermute | solution.py:652
  149.7 9.5 %collective-permute-done.8.c_ref = bf16[256,512]{1,0:T(8,128)(2,1)S(1)} collective-permute-done((bf16[256,512]{1,0:T(8,128)(2,1)S(1)}, bf16[256,512]{1,0:T(8,128)(2,1)S(1)}, u32[]{:S(2)}, u32[]{:S(2)}) %collective-permute-start.8) | collective-permute-done | bytes 262176 | tf_op jit(solution)/shard_map/ppermute | solution.py:652
  159.2 2.9 %collective-permute-start.11 = (bf16[256,512]{1,0:T(8,128)(2,1)S(1)}, bf16[256,512]{1,0:T(8,128)(2,1)S(1)}, u32[]{:S(2)}, u32[]{:S(2)}) collective-permute-start(bf16[256,512]{1,0:T(8,128)(2,1)S(1)} %shard_map.96.b_ref), channel_id=1, source_target_pairs={{0,64},{64,0},{1,65},{65,1},{2,66},{66,2},{3,67},{67,3},{4,68},{68... | collective-permute-start | bytes 786440 | tf_op jit(solution)/shard_map/ppermute | solution.py:652
  162.1 3.0 %project.4.acc_ref = f32[256,1024]{1,0:T(8,128)S(1)} custom-call(s32[2]{0:T(128)S(1)} %pad_add_fusion.where.w, bf16[256,512]{1,0:T(8,128)(2,1)S(1)} %shard_map.92.refs_1_.a_ref, bf16[512,512]{1,0:T(8,128)(2,1)S(1)} %shard_map.93.refs_2_.b_ref, bf16[256,512]{1,0:T(8,128)(2,1)S(1)} %collective-permute-done.8.c_ref, bf16[1024,2048]{1,0:T(8,128)(2,1)} %wb_ref.7, ...), custom_call_target="tpu_custom_call" | custom-call | tf_op jit(solution)/shard_map/project/pallas_call | solution.py:494
  165.2 0.0 collective-permute-done.10.c_ref
  165.2 3.1 %project.5.acc_ref = f32[256,1024]{1,0:T(8,128)S(1)} custom-call(s32[2]{0:T(128)S(1)} %pad_add_fusion.where.w, bf16[256,512]{1,0:T(8,128)(2,1)S(1)} %shard_map.91.refs_1_.a_ref, bf16[512,512]{1,0:T(8,128)(2,1)S(1)} %shard_map.93.refs_2_.b_ref, bf16[256,512]{1,0:T(8,128)(2,1)S(1)} %collective-permute-done.10.c_ref, bf16[1024,2048]{1,0:T(8,128)(2,1)} %wb_ref.7, ...), custom_call_target="tpu_custom_call" | custom-call | tf_op jit(solution)/shard_map/project/pallas_call | solution.py:494
  168.3 0.0 collective-permute-done.9.a_ref
  168.3 1.7 shard_map.97.refs_0_
  170.0 1.7 shard_map.98.refs_0_
  171.7 0.0 collective-permute-done.6.c_ref
  171.7 0.0 copy-start.1
  171.7 1.6 copy-done.1
  173.3 3.0 %project.6.acc_ref = f32[256,1024]{1,0:T(8,128)S(1)} custom-call(s32[2]{0:T(128)S(1)} %pad_add_fusion.where.w, bf16[512,512]{1,0:T(8,128)(2,1)S(1)} %shard_map.94.refs_2_.a_ref, bf16[256,512]{1,0:T(8,128)(2,1)S(1)} %shard_map.96.b_ref, bf16[512,512]{1,0:T(8,128)(2,1)S(1)} %collective-permute-done.6.c_ref, bf16[1024,2048]{1,0:T(8,128)(2,1)} %wb_ref.7, ...), custom_call_target="tpu_custom_call" | custom-call | tf_op jit(solution)/shard_map/project/pallas_call | solution.py:494
  176.4 3.1 %project.7.acc_ref = f32[256,1024]{1,0:T(8,128)S(1)} custom-call(s32[2]{0:T(128)S(1)} %pad_add_fusion.where.w, bf16[512,512]{1,0:T(8,128)(2,1)S(1)} %shard_map.94.refs_2_.a_ref, bf16[256,512]{1,0:T(8,128)(2,1)S(1)} %shard_map.95.refs_2_.b_ref, bf16[512,512]{1,0:T(8,128)(2,1)S(1)} %collective-permute-done.6.c_ref, bf16[1024,2048]{1,0:T(8,128)(2,1)} %wb_ref.7, ...), custom_call_target="tpu_custom_call" | custom-call | tf_op jit(solution)/shard_map/project/pallas_call | solution.py:494
  179.4 0.0 collective-permute-done.12.a_ref
  179.4 1.7 shard_map.99.refs_0_
  181.2 0.0 collective-permute-done.11.a_ref
  181.2 1.7 shard_map.100
Async XLA Ops:
  7.4 7.5 %collective-permute-start.1 = (bf16[1536,512]{1,0:T(8,128)(2,1)S(1)}, bf16[1536,512]{1,0:T(8,128)(2,1)S(1)}, u32[]{:S(2)}, u32[]{:S(2)}) collective-permute-start(bf16[1536,512]{1,0:T(8,128)(2,1)S(1)} %head_grads.3), channel_id=1, source_target_pairs={{0,1},{1,0},{2,3},{3,2},{4,5},{5,4},{6,7},{7,6},{8,9},{9,8},{10,11... | collective-permute-start | bytes 4718600 | tf_op jit(solution)/shard_map/ppermute | solution.py:555
  48.8 4.7 %collective-permute-start.2 = (bf16[96,512]{1,0:T(8,128)(2,1)S(1)}, bf16[96,512]{1,0:T(8,128)(2,1)S(1)}, u32[]{:S(2)}, u32[]{:S(2)}) collective-permute-start(bf16[96,512]{1,0:T(8,128)(2,1)S(1)} %sum_planes.1.part_ref), channel_id=1, source_target_pairs={{0,2},{1,3},{2,0},{3,1},{4,6},{5,7},{6,4},{7,5},{8,10},{9,11},{10,... | collective-permute-start | bytes 294920 | tf_op jit(solution)/shard_map/ppermute | solution.py:555
  54.8 26.3 %all-to-all-start.1 = ((bf16[16,96,512]{2,1,0:T(8,128)(2,1)}), bf16[16,96,512]{2,1,0:T(8,128)(2,1)}, u32[]{:S(2)}, u32[]{:S(2)}) async-start(bf16[16,96,512]{2,1,0:T(8,128)(2,1)} %add_and_repeat.1), calls=%async_computation.1 | async-start | bytes 3145728 | tf_op jit(solution)/shard_map/all_to_all | solution.py:560
  59.2 40.6 %collective-permute-start = (bf16[1024,1024]{1,0:T(8,128)(2,1)}, bf16[1024,1024]{1,0:T(8,128)(2,1)}, u32[]{:S(2)}, u32[]{:S(2)}) collective-permute-start(bf16[1024,1024]{1,0:T(8,128)(2,1)} %k_hbm.3), channel_id=1, source_target_pairs={{0,1},{1,2},{2,3},{3,4},{4,5},{5,6},{6,7},{7,8},{8,9},{9,10},{10,1... | collective-permute-start | bytes 6291464 | tf_op jit(solution)/shard_map/ppermute | solution.py:603
  66.1 80.6 %collective-permute-start.7 = (bf16[1024,1024]{1,0:T(8,128)(2,1)}, bf16[1024,1024]{1,0:T(8,128)(2,1)S(1)}, u32[]{:S(2)}, u32[]{:S(2)}) collective-permute-start(bf16[1024,1024]{1,0:T(8,128)(2,1)} %get-tuple-element.10), channel_id=1, source_target_pairs={{0,66},{1,67},{2,64},{3,65},{4,70},{5,71},{6,68},{7,69},{8,74},{9,... | collective-permute-start | bytes 6291464 | tf_op jit(solution)/shard_map/ppermute | solution.py:610
  90.9 29.8 %collective-permute-start.5 = (bf16[1536,512]{1,0:T(8,128)(2,1)}, bf16[1536,512]{1,0:T(8,128)(2,1)}, u32[]{:S(2)}, u32[]{:S(2)}) collective-permute-start(bf16[1536,512]{1,0:T(8,128)(2,1)} %renewed_weights.1.w_ref), channel_id=1, source_target_pairs={{0,1},{1,0},{2,3},{3,2},{4,5},{5,4},{6,7},{7,6},{8,9},{9,8},{10,11... | collective-permute-start | bytes 4718600 | tf_op jit(solution)/shard_map/ppermute | solution.py:555
  91.0 21.3 %collective-permute-start.4 = (bf16[512,1024]{1,0:T(8,128)(2,1)}, bf16[512,1024]{1,0:T(8,128)(2,1)S(1)}, u32[]{:S(2)}, u32[]{:S(2)}) collective-permute-start(bf16[512,1024]{1,0:T(8,128)(2,1)} %get-tuple-element.9), channel_id=1, source_target_pairs={{0,1},{1,2},{2,3},{3,4},{4,5},{5,6},{6,7},{7,8},{8,9},{9,10},{10,1... | collective-permute-start | bytes 3145736 | tf_op jit(solution)/shard_map/ppermute | solution.py:605
  93.4 35.5 %collective-permute-start.3 = (bf16[512,1024]{1,0:T(8,128)(2,1)}, bf16[512,1024]{1,0:T(8,128)(2,1)}, u32[]{:S(2)}, u32[]{:S(2)}) collective-permute-start(bf16[512,1024]{1,0:T(8,128)(2,1)} %get-tuple-element.8), channel_id=1, source_target_pairs={{0,1},{1,2},{2,3},{3,4},{4,5},{5,6},{6,7},{7,8},{8,9},{9,10},{10,1... | collective-permute-start | bytes 3145736 | tf_op jit(solution)/shard_map/ppermute | solution.py:606
  99.8 12.5 %copy-start.2 = (f32[2,512]{1,0:T(2,128)S(1)}, f32[2,512]{1,0:T(2,128)}, u32[]{:S(2)}) copy-start(f32[2,512]{1,0:T(2,128)} %gain_ref.11) | copy-start | bytes 12292
  110.0 2.3 %copy-start = (bf16[1024,2560]{1,0:T(8,128)(2,1)}, bf16[1024,2560]{1,0:T(8,128)(2,1)S(1)}, u32[]{:S(2)}) copy-start(bf16[1024,2560]{1,0:T(8,128)(2,1)S(1)} %probabilities.1.p_hbm) | copy-start | bytes 15728644
  125.8 42.5 %collective-permute-start.9 = (bf16[512,512]{1,0:T(8,128)(2,1)S(1)}, bf16[512,512]{1,0:T(8,128)(2,1)S(1)}, u32[]{:S(2)}, u32[]{:S(2)}) collective-permute-start(bf16[512,512]{1,0:T(8,128)(2,1)S(1)} %shard_map.93.refs_2_.b_ref), channel_id=1, source_target_pairs={{0,64},{64,0},{1,65},{65,1},{2,66},{66,2},{3,67},{67,3},{4,68},{68... | collective-permute-start | bytes 1572872 | tf_op jit(solution)/shard_map/ppermute | solution.py:652
  134.0 37.7 %collective-permute-start.6 = (bf16[512,512]{1,0:T(8,128)(2,1)S(1)}, bf16[512,512]{1,0:T(8,128)(2,1)S(1)}, u32[]{:S(2)}, u32[]{:S(2)}) collective-permute-start(bf16[512,512]{1,0:T(8,128)(2,1)S(1)} %shard_map.94.refs_2_.a_ref), channel_id=1, source_target_pairs={{0,64},{64,0},{1,65},{65,1},{2,66},{66,2},{3,67},{67,3},{4,68},{68... | collective-permute-start | bytes 1572872 | tf_op jit(solution)/shard_map/ppermute | solution.py:652
  134.8 24.5 %collective-permute-start.8 = (bf16[256,512]{1,0:T(8,128)(2,1)S(1)}, bf16[256,512]{1,0:T(8,128)(2,1)S(1)}, u32[]{:S(2)}, u32[]{:S(2)}) collective-permute-start(bf16[256,512]{1,0:T(8,128)(2,1)S(1)} %shard_map.92.refs_1_.a_ref), channel_id=1, source_target_pairs={{0,64},{64,0},{1,65},{65,1},{2,66},{66,2},{3,67},{67,3},{4,68},{68... | collective-permute-start | bytes 786440 | tf_op jit(solution)/shard_map/ppermute | solution.py:652
  137.7 27.5 %collective-permute-start.10 = (bf16[256,512]{1,0:T(8,128)(2,1)S(1)}, bf16[256,512]{1,0:T(8,128)(2,1)S(1)}, u32[]{:S(2)}, u32[]{:S(2)}) collective-permute-start(bf16[256,512]{1,0:T(8,128)(2,1)S(1)} %shard_map.91.refs_1_.a_ref), channel_id=1, source_target_pairs={{0,64},{64,0},{1,65},{65,1},{2,66},{66,2},{3,67},{67,3},{4,68},{68... | collective-permute-start | bytes 786440 | tf_op jit(solution)/shard_map/ppermute | solution.py:652
  146.7 32.7 %collective-permute-start.12 = (bf16[256,512]{1,0:T(8,128)(2,1)S(1)}, bf16[256,512]{1,0:T(8,128)(2,1)S(1)}, u32[]{:S(2)}, u32[]{:S(2)}) collective-permute-start(bf16[256,512]{1,0:T(8,128)(2,1)S(1)} %shard_map.95.refs_2_.b_ref), channel_id=1, source_target_pairs={{0,64},{64,0},{1,65},{65,1},{2,66},{66,2},{3,67},{67,3},{4,68},{68... | collective-permute-start | bytes 786440 | tf_op jit(solution)/shard_map/ppermute | solution.py:652
  159.2 21.9 %collective-permute-start.11 = (bf16[256,512]{1,0:T(8,128)(2,1)S(1)}, bf16[256,512]{1,0:T(8,128)(2,1)S(1)}, u32[]{:S(2)}, u32[]{:S(2)}) collective-permute-start(bf16[256,512]{1,0:T(8,128)(2,1)S(1)} %shard_map.96.b_ref), channel_id=1, source_target_pairs={{0,64},{64,0},{1,65},{65,1},{2,66},{66,2},{3,67},{67,3},{4,68},{68... | collective-permute-start | bytes 786440 | tf_op jit(solution)/shard_map/ppermute | solution.py:652
  171.7 1.6 copy-start.1

commit v7 on v6

--- a/solution.py
+++ b/solution.py
@@ -220,9 +220,10 @@
 
     def body(w, weight_ref, value_ref, weight_out, late_out, early_out, weight, value, sems):
         other = pl.ds(pl.multiple_of((1 - w[1]) * columns, columns), columns)
+        mine = pl.ds(pl.multiple_of(w[0] * HEAD, HEAD), HEAD)
         low, high = pl.ds(0, rows), pl.ds(rows, rows)
         moves = (
-            (weight_ref.at[:, other], weight, weight_out),
+            (weight_ref.at[mine, other], weight, weight_out),
             (value_ref.at[high], value.at[high], late_out),
             (value_ref.at[low], value.at[low], early_out),
         )
@@ -240,7 +241,7 @@
     return pl.pallas_call(
         body,
         out_shape=(
-            pltpu.HBM((out_weight.shape[0], columns), BF),
+            pltpu.HBM((HEAD, columns), BF),
             pltpu.HBM((rows, width), BF),
             pltpu.HBM((rows, width), BF),
         ),
@@ -250,7 +251,7 @@
             in_specs=[any_spec(), any_spec()],
             out_specs=[any_spec(), any_spec(), any_spec()],
             scratch_shapes=[
-                pltpu.VMEM((out_weight.shape[0], columns), BF),
+                pltpu.VMEM((HEAD, columns), BF),
                 pltpu.VMEM(values.shape, BF),
                 pltpu.SemaphoreType.DMA((2, 3)),
             ],
@@ -501,7 +502,7 @@
             + [
                 pl.BlockSpec((HEAD, step), lambda i, w: (w[0], 2 * w[1] + i)),
                 pl.BlockSpec((HEAD, step), lambda i, w: (1 - w[0], 2 * w[1] + i)),
-                pl.BlockSpec((HEAD, step), lambda i, w: (w[0], i)),
+                pl.BlockSpec((HEAD, step), lambda i, w: (0, i)),
             ]
             + [any_spec()] * len(after),
             out_specs=pl.BlockSpec((CHUNK, step), lambda i, w: (0, i)),
@@ -519,12 +520,11 @@
 
     def body(w, acc_ref, a_ref, wa_ref, *refs):
         out_hbm, done, sems = refs[-3:]
-        rows = pl.ds(pl.multiple_of((1 - w[0]) * HEAD, HEAD), HEAD)
         came = a_ref[block * CHUNK : (block + 1) * CHUNK, :]
         copies = []
         for n in range(parts):
             here = slice(n * step, (n + 1) * step)
-            done[:, here] = (acc_ref[:, here] + dot(came, wa_ref[rows, here])).astype(BF)
+            done[:, here] = (acc_ref[:, here] + dot(came, wa_ref[:, here])).astype(BF)
             some = pl.ds(n * step, step)
             copies.append(
                 pltpu.make_async_copy(
@@ -607,7 +607,8 @@
     pairs = [
         (group * count + i, (1 - group) * count + (i ^ 2)) for group in range(2) for i in range(count)
     ]
-    other_weight = lax.ppermute(other_columns, ("head", "seq"), pairs)
+    other_first = lax.ppermute(other_columns, ("head", "seq"), pairs)
+    other_last = partner(other_first, 1)
 
     chip_sum = add_blocks(grads_mine, grads_got)
     slices = over_planes(chip_sum.reshape(PLANES, -1, HEAD))
@@ -658,10 +659,10 @@
         partials = {}
         for at in pair:
             operands = (made[False, at], made[True, at], arrived[False, at])
-            partials[at] = project_chunk(where, operands, out_weight, other_weight, after)
+            partials[at] = project_chunk(where, operands, out_weight, other_first, after)
         for at in pair:
             out = finish_chunk(
-                at, tokens_here, where, partials[at], *arrived[True, at], other_weight, out
+                at, tokens_here, where, partials[at], *arrived[True, at], other_last, out
             )
         after = (out,)
     return out

time: 185 us -> 193 us (1.043)
  waiting for transfers between devices: 25 us -> 32.7 us
  local copies, waits for them, and re-layouts: 3.89 us -> 6.45 us
    ppermute x6, waiting for transfers between devices: 9.56 us -> 16.6 us  [shards(): came = lax.ppermute(piece, 'head', head_pair)]
    pallas_call x4, Pallas kernels: 6.84 us -> 11.8 us  [finish_chunk(): pl.pallas_call(body, out_shape=jax.ShapeDtypeStruct((tokens, columns), BF...]
    pallas_call x6, Pallas kernels: 26.9 us -> 22.8 us  [combined_piece(): pl.pallas_call(body, out_shape=jax.ShapeDtypeStruct((rows, HEAD), BF), gr...]
    unnamed x6 -> x10, local copies, waits for them, and re-layouts: 3.89 us -> 6.45 us
    pallas_call x1, Pallas kernels: 9.82 us -> 7.79 us  [renewed_weights(): pl.pallas_call(renew_body, out_shape=jax.ShapeDtypeStruct((3 * HEAD, HEAD...]
  transfers between devices with their start and end apart: 14 -> 15, of which waited for: 3 -> 4; matrix products, arithmetic and copies ran while one was open for 0% -> 0% of each run, Pallas kernels for 41% -> 38%
where the time goes in v7:
time: 193 us; the launch traced here: 191 us
  Pallas kernels  87.2 us (45%)
  starting transfers between devices  32.8 us (17%)
  waiting for transfers between devices  32.7 us (17%)
  blocking collectives  31.5 us (16%)
  local copies, waits for them, and re-layouts  6.45 us (3%)
    all_to_all x1, blocking collectives, over_planes(): lax.all_to_all(value, 'seq', 0, 0, tiled=True, axis_index_groups=groups)  31.5 us
    pallas_call x6, Pallas kernels, combined_piece(): pl.pallas_call(body, out_shape=jax.ShapeDtypeStruct((rows, HEAD), BF), gr...  22.8 us
    ppermute x6, waiting for transfers between devices, shards(): came = lax.ppermute(piece, 'head', head_pair)  16.6 us
    pallas_call x2, Pallas kernels, head_grads(): pl.pallas_call(grads_body, out_shape=jax.ShapeDtypeStruct((3 * HEAD, HEAD...  14.7 us
    ppermute x6, starting transfers between devices, shards(): came = lax.ppermute(piece, 'head', head_pair)  13.2 us
    all_to_all x1, waiting for transfers between devices, over_planes(): lax.all_to_all(value, 'seq', 0, 0, tiled=True, axis_index_groups=groups)  13 us
    pallas_call x4, Pallas kernels, project_chunk(): pl.pallas_call(body, out_shape=jax.ShapeDtypeStruct((CHUNK, columns), F32...  12.8 us
    pallas_call x4, Pallas kernels, finish_chunk(): pl.pallas_call(body, out_shape=jax.ShapeDtypeStruct((tokens, columns), BF...  11.8 us
  transfers between devices with their start and end apart: 15, of which 4 were waited for; matrix products, arithmetic and copies ran while one was open for 0% of the time, Pallas kernels for 38%

profile of v7, /device:TPU:0, one launch (start us, length us, event | category | flops | bytes accessed | tf_op | source)
XLA Modules:
  0.0 191.2 jit_solution(1585610961572776427)
XLA Ops:
  0.0 0.1 pad_add_fusion.1.where
  0.1 7.3 %head_grads.3 = bf16[1536,512]{1,0:T(8,128)(2,1)S(1)} custom-call(s32[2]{0:T(128)S(1)} %pad_add_fusion.1.where, bf16[1024,1024]{1,0:T(8,128)(2,1)} %k_hbm.3, bf16[1024,1024]{1,0:T(8,128)(2,1)} %value_hbm.11, f32[2,1024]{1,0:T(2,128)} %rate_ref.3, f32[2,512,512]{2,1,0:T(8,128)} %gate_ref.1, f32[2,512,512]{2,1,0:T(8,128)} %lift_ref.1, f32[2,512,512]{2,1,0:T(8,128)} %down_ref.1), custom_call_target="tpu_custom_call" | custom-call | tf_op jit(solution)/shard_map/head_grads/pallas_call | solution.py:118
  7.4 0.1 collective-permute-start.1
  7.5 0.1 pad_add_fusion.where.w
  7.6 7.3 %head_grads.2.mine_ref = f32[1536,512]{1,0:T(8,128)S(1)} custom-call(s32[2]{0:T(128)S(1)} %pad_add_fusion.where.w, bf16[1024,1024]{1,0:T(8,128)(2,1)} %k_hbm.3, bf16[1024,1024]{1,0:T(8,128)(2,1)} %value_hbm.11, f32[2,1024]{1,0:T(2,128)} %rate_ref.3, f32[2,512,512]{2,1,0:T(8,128)} %gate_ref.1, f32[2,512,512]{2,1,0:T(8,128)} %lift_ref.1, f32[2,512,512]{2,1,0:T(8,128)} %down_ref.1), custom_call_target="tpu_custom_call" | custom-call | tf_op jit(solution)/shard_map/head_grads/pallas_call | solution.py:118
  14.9 0.0 collective-permute-done.1.got_ref
  15.0 1.2 add_blocks.1
  16.2 31.5 %all_to_all.10.slices_hbm = bf16[16,96,512]{2,1,0:T(8,128)(2,1)S(1)} all-to-all(bf16[16,96,512]{2,1,0:T(8,128)(2,1)} %bitcast.7), channel_id=1, replica_groups={{0,4,8,12,16,20,24,28,32,36,40,44,48,52,56,60},{1,5,9,13,17,21,25,29,33..., dimensions={0} | all-to-all | bytes 3145728 | tf_op jit(solution)/shard_map/all_to_all | solution.py:560
  47.7 1.0 sum_planes.1.part_ref
  48.8 1.7 collective-permute-start.2
  50.4 3.0 %collective-permute-done.2.other_ref = bf16[96,512]{1,0:T(8,128)(2,1)S(1)} collective-permute-done((bf16[96,512]{1,0:T(8,128)(2,1)S(1)}, bf16[96,512]{1,0:T(8,128)(2,1)S(1)}, u32[]{:S(2)}, u32[]{:S(2)}) %collective-permute-start.2) | collective-permute-done | bytes 98336 | tf_op jit(solution)/shard_map/ppermute | solution.py:555
  53.5 1.3 add_and_repeat.1
  54.8 3.7 %all-to-all-start.1 = ((bf16[16,96,512]{2,1,0:T(8,128)(2,1)}), bf16[16,96,512]{2,1,0:T(8,128)(2,1)S(1)}, u32[]{:S(2)}, u32[]{:S(2)}) async-start(bf16[16,96,512]{2,1,0:T(8,128)(2,1)} %add_and_repeat.1), calls=%async_computation.1 | async-start | bytes 3145728 | tf_op jit(solution)/shard_map/all_to_all | solution.py:560
  58.5 2.6 %collective-permute-start = (bf16[1024,1024]{1,0:T(8,128)(2,1)}, bf16[1024,1024]{1,0:T(8,128)(2,1)}, u32[]{:S(2)}, u32[]{:S(2)}) collective-permute-start(bf16[1024,1024]{1,0:T(8,128)(2,1)} %k_hbm.3), channel_id=1, source_target_pairs={{0,1},{1,2},{2,3},{3,4},{4,5},{5,6},{6,7},{7,8},{8,9},{9,10},{10,1... | collective-permute-start | bytes 6291464 | tf_op jit(solution)/shard_map/ppermute | solution.py:603
  61.1 3.6 %cut_blocks.1 = (bf16[512,1024]{1,0:T(8,128)(2,1)}, bf16[512,1024]{1,0:T(8,128)(2,1)}, bf16[512,1024]{1,0:T(8,128)(2,1)}) custom-call(s32[2]{0:T(128)S(1)} %pad_add_fusion.where.w, bf16[1024,2048]{1,0:T(8,128)(2,1)} %wb_ref.7, bf16[1024,1024]{1,0:T(8,128)(2,1)} %value_hbm.11), custom_call_target="tpu_custom_call" | custom-call | tf_op jit(solution)/shard_map/cut_blocks/pallas_call | solution.py:241
  64.7 2.6 %collective-permute-start.7 = (bf16[512,1024]{1,0:T(8,128)(2,1)}, bf16[512,1024]{1,0:T(8,128)(2,1)}, u32[]{:S(2)}, u32[]{:S(2)}) collective-permute-start(bf16[512,1024]{1,0:T(8,128)(2,1)} %get-tuple-element.10), channel_id=1, source_target_pairs={{0,66},{1,67},{2,64},{3,65},{4,70},{5,71},{6,68},{7,69},{8,74},{9,... | collective-permute-start | bytes 3145736 | tf_op jit(solution)/shard_map/ppermute | solution.py:610
  67.3 13.0 %all-to-all-done.1 = bf16[16,96,512]{2,1,0:T(8,128)(2,1)S(1)} async-done(((bf16[16,96,512]{2,1,0:T(8,128)(2,1)}), bf16[16,96,512]{2,1,0:T(8,128)(2,1)S(1)}, u32[]{:S(2)}, u32[]{:S(2)}) %all-to-all-start.1) | async-done | bytes 1572896 | tf_op jit(solution)/shard_map/all_to_all | solution.py:560
  80.3 0.0 copy-start.2
  80.3 1.1 copy-done.2
  81.4 1.4 copy-done.3
  82.8 7.8 %renewed_weights.1.w_ref = bf16[1536,512]{1,0:T(8,128)(2,1)S(1)} custom-call(s32[2]{0:T(128)S(1)} %pad_add_fusion.where.w, bf16[1536,512]{1,0:T(8,128)(2,1)S(1)} %bitcast.6, f32[2,512,512]{2,1,0:T(8,128)} %gate_ref.1, f32[2,512,512]{2,1,0:T(8,128)} %lift_ref.1, f32[2,512,512]{2,1,0:T(8,128)} %down_ref.1), custom_call_target="tpu_custom_call" | custom-call | tf_op jit(solution)/shard_map/renewed_weights/pallas_call | solution.py:198
  90.6 0.1 collective-permute-start.5
  90.7 2.5 %collective-permute-start.4 = (bf16[512,1024]{1,0:T(8,128)(2,1)}, bf16[512,1024]{1,0:T(8,128)(2,1)S(1)}, u32[]{:S(2)}, u32[]{:S(2)}) collective-permute-start(bf16[512,1024]{1,0:T(8,128)(2,1)} %get-tuple-element.9), channel_id=1, source_target_pairs={{0,1},{1,2},{2,3},{3,4},{4,5},{5,6},{6,7},{7,8},{8,9},{9,10},{10,1... | collective-permute-start | bytes 3145736 | tf_op jit(solution)/shard_map/ppermute | solution.py:605
  93.2 6.3 %collective-permute-start.3 = (bf16[512,1024]{1,0:T(8,128)(2,1)}, bf16[512,1024]{1,0:T(8,128)(2,1)}, u32[]{:S(2)}, u32[]{:S(2)}) collective-permute-start(bf16[512,1024]{1,0:T(8,128)(2,1)} %get-tuple-element.8), channel_id=1, source_target_pairs={{0,1},{1,2},{2,3},{3,4},{4,5},{5,6},{6,7},{7,8},{8,9},{9,10},{10,1... | collective-permute-start | bytes 3145736 | tf_op jit(solution)/shard_map/ppermute | solution.py:606
  99.5 0.0 collective-permute-done.7.wc_ref
  99.5 0.0 collective-permute-start.10
  99.5 0.0 collective-permute-done.edge_ref
  99.5 0.0 copy-start.4
  99.6 10.2 %probabilities.1.p_hbm = bf16[1024,2560]{1,0:T(8,128)(2,1)S(1)} custom-call(s32[1]{0:T(128)} %bitcast.2.flag, bf16[1024,1024]{1,0:T(8,128)(2,1)} %q_hbm.11, bf16[1024,1024]{1,0:T(8,128)(2,1)} %collective-permute-done.edge_ref, bf16[1024,1024]{1,0:T(8,128)(2,1)} %k_hbm.3), custom_call_target="tpu_custom_call" | custom-call | tf_op jit(solution)/shard_map/probabilities/pallas_call | solution.py:391
  109.8 0.0 copy-start
  109.8 2.3 %copy-done = bf16[1024,2560]{1,0:T(8,128)(2,1)} copy-done((bf16[1024,2560]{1,0:T(8,128)(2,1)}, bf16[1024,2560]{1,0:T(8,128)(2,1)S(1)}, u32[]{:S(2)}) %copy-start) | copy-done | bytes 5242904
  112.1 0.0 collective-permute-done.4.refs_0_.refs_1_
  112.1 0.0 copy-done.4
  112.1 2.8 %shard_map.91.refs_1_.a_ref = bf16[256,512]{1,0:T(8,128)(2,1)S(1)} custom-call(s32[2]{0:T(128)S(1)} %pad_add_fusion.where.w, bf16[1024,1024]{1,0:T(8,128)(2,1)} %q_hbm.11, bf16[1024,2560]{1,0:T(8,128)(2,1)} %copy-done, bf16[1536,512]{1,0:T(8,128)(2,1)S(1)} %renewed_weights.1.w_ref, f32[2,512]{1,0:T(2,128)S(1)} %copy-done.4, bf16[1024,1024]{1,0:T(8,128)(2,1)} %value_hbm.11, ...), custom_call_target="tpu_custom_call" | custom-call | tf_op jit(solution)/shard_map/pallas_call | solution.py:463
  114.9 2.8 %shard_map.92.refs_1_.a_ref = bf16[256,512]{1,0:T(8,128)(2,1)S(1)} custom-call(s32[2]{0:T(128)S(1)} %pad_add_fusion.where.w, bf16[1024,1024]{1,0:T(8,128)(2,1)} %q_hbm.11, bf16[1024,2560]{1,0:T(8,128)(2,1)} %copy-done, bf16[1536,512]{1,0:T(8,128)(2,1)S(1)} %renewed_weights.1.w_ref, f32[2,512]{1,0:T(2,128)S(1)} %copy-done.4, bf16[1024,1024]{1,0:T(8,128)(2,1)} %value_hbm.11, ...), custom_call_target="tpu_custom_call" | custom-call | tf_op jit(solution)/shard_map/pallas_call | solution.py:463
  117.7 0.0 collective-permute-done.5.w_ref
  117.7 5.1 %shard_map.93.refs_2_.b_ref = bf16[512,512]{1,0:T(8,128)(2,1)S(1)} custom-call(s32[2]{0:T(128)S(1)} %pad_add_fusion.where.w, bf16[1024,1024]{1,0:T(8,128)(2,1)} %q_hbm.11, bf16[1024,2560]{1,0:T(8,128)(2,1)} %copy-done, bf16[1536,512]{1,0:T(8,128)(2,1)} %collective-permute-done.5.w_ref, f32[2,512]{1,0:T(2,128)S(1)} %copy-done.4, ...), custom_call_target="tpu_custom_call" | custom-call | tf_op jit(solution)/shard_map/pallas_call | solution.py:463
  122.8 3.2 %collective-permute-start.9 = (bf16[512,512]{1,0:T(8,128)(2,1)S(1)}, bf16[512,512]{1,0:T(8,128)(2,1)S(1)}, u32[]{:S(2)}, u32[]{:S(2)}) collective-permute-start(bf16[512,512]{1,0:T(8,128)(2,1)S(1)} %shard_map.93.refs_2_.b_ref), channel_id=1, source_target_pairs={{0,64},{64,0},{1,65},{65,1},{2,66},{66,2},{3,67},{67,3},{4,68},{68... | collective-permute-start | bytes 1572872 | tf_op jit(solution)/shard_map/ppermute | solution.py:653
  126.0 0.0 collective-permute-done.3.refs_0_
  126.0 3.7 %shard_map.94.refs_2_.a_ref = bf16[512,512]{1,0:T(8,128)(2,1)S(1)} custom-call(s32[2]{0:T(128)S(1)} %pad_add_fusion.where.w, bf16[1024,1024]{1,0:T(8,128)(2,1)} %q_hbm.11, bf16[1024,2560]{1,0:T(8,128)(2,1)} %copy-done, bf16[1536,512]{1,0:T(8,128)(2,1)S(1)} %renewed_weights.1.w_ref, f32[2,512]{1,0:T(2,128)S(1)} %copy-done.4, bf16[1024,1024]{1,0:T(8,128)(2,1)} %value_hbm.11, ...), custom_call_target="tpu_custom_call" | custom-call | tf_op jit(solution)/shard_map/pallas_call | solution.py:463
  129.7 0.7 collective-permute-start.6
  130.4 2.9 %collective-permute-start.8 = (bf16[256,512]{1,0:T(8,128)(2,1)S(1)}, bf16[256,512]{1,0:T(8,128)(2,1)S(1)}, u32[]{:S(2)}, u32[]{:S(2)}) collective-permute-start(bf16[256,512]{1,0:T(8,128)(2,1)S(1)} %shard_map.92.refs_1_.a_ref), channel_id=1, source_target_pairs={{0,64},{64,0},{1,65},{65,1},{2,66},{66,2},{3,67},{67,3},{4,68},{68... | collective-permute-start | bytes 786440 | tf_op jit(solution)/shard_map/ppermute | solution.py:653
  133.3 0.6 collective-permute-start.11
  133.9 4.2 %shard_map.95.refs_2_.b_ref = bf16[256,512]{1,0:T(8,128)(2,1)S(1)} custom-call(s32[2]{0:T(128)S(1)} %pad_add_fusion.where.w, bf16[1024,1024]{1,0:T(8,128)(2,1)} %q_hbm.11, bf16[1024,2560]{1,0:T(8,128)(2,1)} %copy-done, bf16[1536,512]{1,0:T(8,128)(2,1)} %collective-permute-done.5.w_ref, f32[2,512]{1,0:T(2,128)S(1)} %copy-done.4, ...), custom_call_target="tpu_custom_call" | custom-call | tf_op jit(solution)/shard_map/pallas_call | solution.py:463
  138.2 4.2 %shard_map.96.b_ref = bf16[256,512]{1,0:T(8,128)(2,1)S(1)} custom-call(s32[2]{0:T(128)S(1)} %pad_add_fusion.where.w, bf16[1024,1024]{1,0:T(8,128)(2,1)} %q_hbm.11, bf16[1024,2560]{1,0:T(8,128)(2,1)} %copy-done, bf16[1536,512]{1,0:T(8,128)(2,1)} %collective-permute-done.5.w_ref, f32[2,512]{1,0:T(2,128)S(1)} %copy-done.4, bf16[1024,1024]{1,0:T(8,128)(2,1)} %value_hbm.11, ...), custom_call_target="tpu_custom_call" | custom-call | tf_op jit(solution)/shard_map/pallas_call | solution.py:463
  142.4 13.9 %collective-permute-done.8.c_ref = bf16[256,512]{1,0:T(8,128)(2,1)S(1)} collective-permute-done((bf16[256,512]{1,0:T(8,128)(2,1)S(1)}, bf16[256,512]{1,0:T(8,128)(2,1)S(1)}, u32[]{:S(2)}, u32[]{:S(2)}) %collective-permute-start.8) | collective-permute-done | bytes 262176 | tf_op jit(solution)/shard_map/ppermute | solution.py:653
  156.2 2.9 %collective-permute-start.13 = (bf16[256,512]{1,0:T(8,128)(2,1)S(1)}, bf16[256,512]{1,0:T(8,128)(2,1)S(1)}, u32[]{:S(2)}, u32[]{:S(2)}) collective-permute-start(bf16[256,512]{1,0:T(8,128)(2,1)S(1)} %shard_map.95.refs_2_.b_ref), channel_id=1, source_target_pairs={{0,64},{64,0},{1,65},{65,1},{2,66},{66,2},{3,67},{67,3},{4,68},{68... | collective-permute-start | bytes 786440 | tf_op jit(solution)/shard_map/ppermute | solution.py:653
  159.1 2.7 %collective-permute-done.11.c_ref = bf16[256,512]{1,0:T(8,128)(2,1)S(1)} collective-permute-done((bf16[256,512]{1,0:T(8,128)(2,1)S(1)}, bf16[256,512]{1,0:T(8,128)(2,1)S(1)}, u32[]{:S(2)}, u32[]{:S(2)}) %collective-permute-start.11) | collective-permute-done | bytes 262176 | tf_op jit(solution)/shard_map/ppermute | solution.py:653
  161.9 2.9 %collective-permute-start.12 = (bf16[256,512]{1,0:T(8,128)(2,1)S(1)}, bf16[256,512]{1,0:T(8,128)(2,1)S(1)}, u32[]{:S(2)}, u32[]{:S(2)}) collective-permute-start(bf16[256,512]{1,0:T(8,128)(2,1)S(1)} %shard_map.96.b_ref), channel_id=1, source_target_pairs={{0,64},{64,0},{1,65},{65,1},{2,66},{66,2},{3,67},{67,3},{4,68},{68... | collective-permute-start | bytes 786440 | tf_op jit(solution)/shard_map/ppermute | solution.py:653
  164.8 3.2 %project.4.acc_ref = f32[256,1024]{1,0:T(8,128)S(1)} custom-call(s32[2]{0:T(128)S(1)} %pad_add_fusion.where.w, bf16[256,512]{1,0:T(8,128)(2,1)S(1)} %shard_map.92.refs_1_.a_ref, bf16[512,512]{1,0:T(8,128)(2,1)S(1)} %shard_map.93.refs_2_.b_ref, bf16[256,512]{1,0:T(8,128)(2,1)S(1)} %collective-permute-done.8.c_ref, bf16[1024,2048]{1,0:T(8,128)(2,1)} %wb_ref.7, ...), custom_call_target="tpu_custom_call" | custom-call | tf_op jit(solution)/shard_map/project/pallas_call | solution.py:495
  168.0 3.2 %project.5.acc_ref = f32[256,1024]{1,0:T(8,128)S(1)} custom-call(s32[2]{0:T(128)S(1)} %pad_add_fusion.where.w, bf16[256,512]{1,0:T(8,128)(2,1)S(1)} %shard_map.91.refs_1_.a_ref, bf16[512,512]{1,0:T(8,128)(2,1)S(1)} %shard_map.93.refs_2_.b_ref, bf16[256,512]{1,0:T(8,128)(2,1)S(1)} %collective-permute-done.11.c_ref, bf16[1024,2048]{1,0:T(8,128)(2,1)} %wb_ref.7, ...), custom_call_target="tpu_custom_call" | custom-call | tf_op jit(solution)/shard_map/project/pallas_call | solution.py:495
  171.2 0.0 collective-permute-done.10.wa_ref
  171.2 0.0 collective-permute-done.9.a_ref
  171.2 2.9 %shard_map.97.refs_0_ = bf16[1024,1024]{1,0:T(8,128)(2,1)} custom-call(s32[2]{0:T(128)S(1)} %pad_add_fusion.where.w, f32[256,1024]{1,0:T(8,128)S(1)} %project.5.acc_ref, bf16[512,512]{1,0:T(8,128)(2,1)S(1)} %collective-permute-done.9.a_ref, bf16[512,1024]{1,0:T(8,128)(2,1)} %collective-permute-done.10.wa_ref), custom_call_target="tpu_custom_call" | custom-call | tf_op jit(solution)/shard_map/pallas_call | solution.py:538
  174.1 2.9 %shard_map.98.refs_0_ = bf16[1024,1024]{1,0:T(8,128)(2,1)} custom-call(s32[2]{0:T(128)S(1)} %pad_add_fusion.where.w, f32[256,1024]{1,0:T(8,128)S(1)} %project.4.acc_ref, bf16[512,512]{1,0:T(8,128)(2,1)S(1)} %collective-permute-done.9.a_ref, bf16[512,1024]{1,0:T(8,128)(2,1)} %collective-permute-done.10.wa_ref, ...), custom_call_target="tpu_custom_call", output_to_operand_aliasing={{}: (4, {})} | custom-call | tf_op jit(solution)/shard_map/pallas_call | solution.py:538
  177.1 0.0 collective-permute-done.6.c_ref
  177.1 0.0 copy-start.1
  177.1 1.6 copy-done.1
  178.7 3.2 %project.6.acc_ref = f32[256,1024]{1,0:T(8,128)S(1)} custom-call(s32[2]{0:T(128)S(1)} %pad_add_fusion.where.w, bf16[512,512]{1,0:T(8,128)(2,1)S(1)} %shard_map.94.refs_2_.a_ref, bf16[256,512]{1,0:T(8,128)(2,1)S(1)} %shard_map.96.b_ref, bf16[512,512]{1,0:T(8,128)(2,1)S(1)} %collective-permute-done.6.c_ref, bf16[1024,2048]{1,0:T(8,128)(2,1)} %wb_ref.7, ...), custom_call_target="tpu_custom_call" | custom-call | tf_op jit(solution)/shard_map/project/pallas_call | solution.py:495
  181.9 3.2 %project.7.acc_ref = f32[256,1024]{1,0:T(8,128)S(1)} custom-call(s32[2]{0:T(128)S(1)} %pad_add_fusion.where.w, bf16[512,512]{1,0:T(8,128)(2,1)S(1)} %shard_map.94.refs_2_.a_ref, bf16[256,512]{1,0:T(8,128)(2,1)S(1)} %shard_map.95.refs_2_.b_ref, bf16[512,512]{1,0:T(8,128)(2,1)S(1)} %collective-permute-done.6.c_ref, bf16[1024,2048]{1,0:T(8,128)(2,1)} %wb_ref.7, ...), custom_call_target="tpu_custom_call" | custom-call | tf_op jit(solution)/shard_map/project/pallas_call | solution.py:495
  185.1 0.0 collective-permute-done.13.a_ref
  185.1 2.9 %shard_map.99.refs_0_ = bf16[1024,1024]{1,0:T(8,128)(2,1)} custom-call(s32[2]{0:T(128)S(1)} %pad_add_fusion.where.w, f32[256,1024]{1,0:T(8,128)S(1)} %project.7.acc_ref, bf16[256,512]{1,0:T(8,128)(2,1)S(1)} %collective-permute-done.13.a_ref, bf16[512,1024]{1,0:T(8,128)(2,1)} %collective-permute-done.10.wa_ref, ...), custom_call_target="tpu_custom_call", output_to_operand_aliasing={{}: (4, {})} | custom-call | tf_op jit(solution)/shard_map/pallas_call | solution.py:538
  188.1 0.0 collective-permute-done.12.a_ref
  188.1 2.9 %shard_map.100 = bf16[1024,1024]{1,0:T(8,128)(2,1)} custom-call(s32[2]{0:T(128)S(1)} %pad_add_fusion.where.w, f32[256,1024]{1,0:T(8,128)S(1)} %project.6.acc_ref, bf16[256,512]{1,0:T(8,128)(2,1)S(1)} %collective-permute-done.12.a_ref, bf16[512,1024]{1,0:T(8,128)(2,1)} %collective-permute-done.10.wa_ref, ...), custom_call_target="tpu_custom_call", output_to_operand_aliasing={{}: (4, {})} | custom-call | tf_op jit(solution)/shard_map/pallas_call | solution.py:538
  (1 shorter events, 0.0 us)
Async XLA Ops:
  7.4 7.5 %collective-permute-start.1 = (bf16[1536,512]{1,0:T(8,128)(2,1)S(1)}, bf16[1536,512]{1,0:T(8,128)(2,1)S(1)}, u32[]{:S(2)}, u32[]{:S(2)}) collective-permute-start(bf16[1536,512]{1,0:T(8,128)(2,1)S(1)} %head_grads.3), channel_id=1, source_target_pairs={{0,1},{1,0},{2,3},{3,2},{4,5},{5,4},{6,7},{7,6},{8,9},{9,8},{10,11... | collective-permute-start | bytes 4718600 | tf_op jit(solution)/shard_map/ppermute | solution.py:555
  48.8 4.7 %collective-permute-start.2 = (bf16[96,512]{1,0:T(8,128)(2,1)S(1)}, bf16[96,512]{1,0:T(8,128)(2,1)S(1)}, u32[]{:S(2)}, u32[]{:S(2)}) collective-permute-start(bf16[96,512]{1,0:T(8,128)(2,1)S(1)} %sum_planes.1.part_ref), channel_id=1, source_target_pairs={{0,2},{1,3},{2,0},{3,1},{4,6},{5,7},{6,4},{7,5},{8,10},{9,11},{10,... | collective-permute-start | bytes 294920 | tf_op jit(solution)/shard_map/ppermute | solution.py:555
  54.8 25.5 %all-to-all-start.1 = ((bf16[16,96,512]{2,1,0:T(8,128)(2,1)}), bf16[16,96,512]{2,1,0:T(8,128)(2,1)S(1)}, u32[]{:S(2)}, u32[]{:S(2)}) async-start(bf16[16,96,512]{2,1,0:T(8,128)(2,1)} %add_and_repeat.1), calls=%async_computation.1 | async-start | bytes 3145728 | tf_op jit(solution)/shard_map/all_to_all | solution.py:560
  58.5 41.0 %collective-permute-start = (bf16[1024,1024]{1,0:T(8,128)(2,1)}, bf16[1024,1024]{1,0:T(8,128)(2,1)}, u32[]{:S(2)}, u32[]{:S(2)}) collective-permute-start(bf16[1024,1024]{1,0:T(8,128)(2,1)} %k_hbm.3), channel_id=1, source_target_pairs={{0,1},{1,2},{2,3},{3,4},{4,5},{5,6},{6,7},{7,8},{8,9},{9,10},{10,1... | collective-permute-start | bytes 6291464 | tf_op jit(solution)/shard_map/ppermute | solution.py:603
  64.7 34.8 %collective-permute-start.7 = (bf16[512,1024]{1,0:T(8,128)(2,1)}, bf16[512,1024]{1,0:T(8,128)(2,1)}, u32[]{:S(2)}, u32[]{:S(2)}) collective-permute-start(bf16[512,1024]{1,0:T(8,128)(2,1)} %get-tuple-element.10), channel_id=1, source_target_pairs={{0,66},{1,67},{2,64},{3,65},{4,70},{5,71},{6,68},{7,69},{8,74},{9,... | collective-permute-start | bytes 3145736 | tf_op jit(solution)/shard_map/ppermute | solution.py:610
  80.3 1.1 copy-start.2
  81.4 1.4 copy-start.3
  90.6 27.1 %collective-permute-start.5 = (bf16[1536,512]{1,0:T(8,128)(2,1)S(1)}, bf16[1536,512]{1,0:T(8,128)(2,1)}, u32[]{:S(2)}, u32[]{:S(2)}) collective-permute-start(bf16[1536,512]{1,0:T(8,128)(2,1)S(1)} %renewed_weights.1.w_ref), channel_id=1, source_target_pairs={{0,1},{1,0},{2,3},{3,2},{4,5},{5,4},{6,7},{7,6},{8,9},{9,8},{10,11... | collective-permute-start | bytes 4718600 | tf_op jit(solution)/shard_map/ppermute | solution.py:555
  90.7 21.4 %collective-permute-start.4 = (bf16[512,1024]{1,0:T(8,128)(2,1)}, bf16[512,1024]{1,0:T(8,128)(2,1)S(1)}, u32[]{:S(2)}, u32[]{:S(2)}) collective-permute-start(bf16[512,1024]{1,0:T(8,128)(2,1)} %get-tuple-element.9), channel_id=1, source_target_pairs={{0,1},{1,2},{2,3},{3,4},{4,5},{5,6},{6,7},{7,8},{8,9},{9,10},{10,1... | collective-permute-start | bytes 3145736 | tf_op jit(solution)/shard_map/ppermute | solution.py:605
  93.2 32.8 %collective-permute-start.3 = (bf16[512,1024]{1,0:T(8,128)(2,1)}, bf16[512,1024]{1,0:T(8,128)(2,1)}, u32[]{:S(2)}, u32[]{:S(2)}) collective-permute-start(bf16[512,1024]{1,0:T(8,128)(2,1)} %get-tuple-element.8), channel_id=1, source_target_pairs={{0,1},{1,2},{2,3},{3,4},{4,5},{5,6},{6,7},{7,8},{8,9},{9,10},{10,1... | collective-permute-start | bytes 3145736 | tf_op jit(solution)/shard_map/ppermute | solution.py:606
  99.5 71.6 %collective-permute-start.10 = (bf16[512,1024]{1,0:T(8,128)(2,1)}, bf16[512,1024]{1,0:T(8,128)(2,1)}, u32[]{:S(2)}, u32[]{:S(2)}) collective-permute-start(bf16[512,1024]{1,0:T(8,128)(2,1)} %collective-permute-done.7.wc_ref), channel_id=1, source_target_pairs={{0,1},{1,0},{2,3},{3,2},{4,5},{5,4},{6,7},{7,6},{8,9},{9,8},{10,11... | collective-permute-start | bytes 3145736 | tf_op jit(solution)/shard_map/ppermute | solution.py:555
  99.5 12.6 %copy-start.4 = (f32[2,512]{1,0:T(2,128)S(1)}, f32[2,512]{1,0:T(2,128)}, u32[]{:S(2)}) copy-start(f32[2,512]{1,0:T(2,128)} %gain_ref.11) | copy-start | bytes 12292
  109.8 2.3 %copy-start = (bf16[1024,2560]{1,0:T(8,128)(2,1)}, bf16[1024,2560]{1,0:T(8,128)(2,1)S(1)}, u32[]{:S(2)}) copy-start(bf16[1024,2560]{1,0:T(8,128)(2,1)S(1)} %probabilities.1.p_hbm) | copy-start | bytes 15728644
  122.8 48.4 %collective-permute-start.9 = (bf16[512,512]{1,0:T(8,128)(2,1)S(1)}, bf16[512,512]{1,0:T(8,128)(2,1)S(1)}, u32[]{:S(2)}, u32[]{:S(2)}) collective-permute-start(bf16[512,512]{1,0:T(8,128)(2,1)S(1)} %shard_map.93.refs_2_.b_ref), channel_id=1, source_target_pairs={{0,64},{64,0},{1,65},{65,1},{2,66},{66,2},{3,67},{67,3},{4,68},{68... | collective-permute-start | bytes 1572872 | tf_op jit(solution)/shard_map/ppermute | solution.py:653
  129.7 47.4 %collective-permute-start.6 = (bf16[512,512]{1,0:T(8,128)(2,1)S(1)}, bf16[512,512]{1,0:T(8,128)(2,1)S(1)}, u32[]{:S(2)}, u32[]{:S(2)}) collective-permute-start(bf16[512,512]{1,0:T(8,128)(2,1)S(1)} %shard_map.94.refs_2_.a_ref), channel_id=1, source_target_pairs={{0,64},{64,0},{1,65},{65,1},{2,66},{66,2},{3,67},{67,3},{4,68},{68... | collective-permute-start | bytes 1572872 | tf_op jit(solution)/shard_map/ppermute | solution.py:653
  130.4 25.8 %collective-permute-start.8 = (bf16[256,512]{1,0:T(8,128)(2,1)S(1)}, bf16[256,512]{1,0:T(8,128)(2,1)S(1)}, u32[]{:S(2)}, u32[]{:S(2)}) collective-permute-start(bf16[256,512]{1,0:T(8,128)(2,1)S(1)} %shard_map.92.refs_1_.a_ref), channel_id=1, source_target_pairs={{0,64},{64,0},{1,65},{65,1},{2,66},{66,2},{3,67},{67,3},{4,68},{68... | collective-permute-start | bytes 786440 | tf_op jit(solution)/shard_map/ppermute | solution.py:653
  133.3 28.5 %collective-permute-start.11 = (bf16[256,512]{1,0:T(8,128)(2,1)S(1)}, bf16[256,512]{1,0:T(8,128)(2,1)S(1)}, u32[]{:S(2)}, u32[]{:S(2)}) collective-permute-start(bf16[256,512]{1,0:T(8,128)(2,1)S(1)} %shard_map.91.refs_1_.a_ref), channel_id=1, source_target_pairs={{0,64},{64,0},{1,65},{65,1},{2,66},{66,2},{3,67},{67,3},{4,68},{68... | collective-permute-start | bytes 786440 | tf_op jit(solution)/shard_map/ppermute | solution.py:653
  156.2 28.9 %collective-permute-start.13 = (bf16[256,512]{1,0:T(8,128)(2,1)S(1)}, bf16[256,512]{1,0:T(8,128)(2,1)S(1)}, u32[]{:S(2)}, u32[]{:S(2)}) collective-permute-start(bf16[256,512]{1,0:T(8,128)(2,1)S(1)} %shard_map.95.refs_2_.b_ref), channel_id=1, source_target_pairs={{0,64},{64,0},{1,65},{65,1},{2,66},{66,2},{3,67},{67,3},{4,68},{68... | collective-permute-start | bytes 786440 | tf_op jit(solution)/shard_map/ppermute | solution.py:653
  161.9 26.2 %collective-permute-start.12 = (bf16[256,512]{1,0:T(8,128)(2,1)S(1)}, bf16[256,512]{1,0:T(8,128)(2,1)S(1)}, u32[]{:S(2)}, u32[]{:S(2)}) collective-permute-start(bf16[256,512]{1,0:T(8,128)(2,1)S(1)} %shard_map.96.b_ref), channel_id=1, source_target_pairs={{0,64},{64,0},{1,65},{65,1},{2,66},{66,2},{3,67},{67,3},{4,68},{68... | collective-permute-start | bytes 786440 | tf_op jit(solution)/shard_map/ppermute | solution.py:653
  177.1 1.6 copy-start.1
